TPU v7x, 128 devices: a whole 4x4x4 slice. The times are simulated.
128 devices in a mesh: ex: 4 (over y), ey: 8 (over z, core), lb: 4 (over x).
Axes of the slice: x: 4, y: 4, z: 4, core: 2. Of those that a mesh axis runs over, the one named last changes fastest.
Arguments:
- atmosphere_state: float32 [15, 128, 32, 1024], P(None, 'lb', 'ex', 'ey'), may hold values from -6 to 6
- diffusivity: float32 [15], replicated, may hold values from 0.004 to 0.012
- mixing: float32 [127], replicated, may hold values from 0.5 to 50
- relaxation: float32 [128], replicated, may hold values from 0.05 to 0.5
- forcing: float32 [15, 128], replicated, may hold values from -3 to 3
- span_map: int32 [4, 8, 1024], P('ex', 'ey'), may hold values from 0 to 1023, each once within a row
- cost_class: int32 [32, 1024], P('ex', 'ey'), may hold values from 0 to 3, as said below
Outputs:
- new_state: float32 [15, 128, 32, 1024], P(None, 'lb', 'ex', 'ey')
Inputs may be any that keep to these rules, and one draw needn't show every extreme that they name: `span_map`: each tile's row lists every one of its 1024 columns exactly once. `cost_class`: sunlit columns, a periodic band of 512 consecutive indices along the second direction, the same for every index along the first, have classes 2 or more; all other columns have classes below 2.
All inputs are finite; a program needn't handle non-finite values.
Results may differ from a plain program's by a relative error of at most 0.00011.
Values sent between devices are 32-bit elements; how exact they have to be, the bound alone decides.
No kernel may reach another device: no remote copies, remote signals or barrier semaphores. Data moves between devices by JAX's collectives and lax.ppermute only.
A program may use at most 128 MiB of HBM per device.

v0:
```python
import math

import jax
import jax.numpy as jnp
import numpy as np
from jax import lax
from jax.sharding import PartitionSpec as P

STEPS = 2
SUBSTEPS = 4


def padded(cells, sides, width):
    for axis, dim in sides:
        count = lax.axis_size(axis)
        head = lax.slice_in_dim(cells, 0, width, axis=dim)
        tail = lax.slice_in_dim(cells, cells.shape[dim] - width, cells.shape[dim], axis=dim)
        cells = jnp.concatenate(
            [
                lax.ppermute(tail, axis, [(i, (i + 1) % count) for i in range(count)]),
                cells,
                lax.ppermute(head, axis, [((i + 1) % count, i) for i in range(count)]),
            ],
            axis=dim,
        )
    return cells


def second_table():
    inner_root = 1.0 / math.sqrt(5.0)
    gll_nodes = np.array([-1.0, -inner_root, inner_root, 1.0])
    weights = np.array(
        [
            np.prod(
                [gll_nodes[target] - gll_nodes[source] for source in range(4) if source != target]
            )
            for target in range(4)
        ]
    )
    first_table = np.zeros((4, 4))
    for target in range(4):
        for source in range(4):
            if source != target:
                first_table[target, source] = weights[target] / (
                    weights[source] * (gll_nodes[target] - gll_nodes[source])
                )
    for target in range(4):
        first_table[target, target] = -first_table[target].sum()
    return (first_table @ first_table).astype(np.float32)


def derive(field, second, blocked):
    fields, levels, width_x, width_y = field.shape
    along_x = jnp.einsum(
        "ij,flejy->fleiy",
        second,
        field.reshape(fields, levels, width_x // 4, 4, width_y),
        precision=lax.Precision.HIGHEST,
    )
    along_y = jnp.einsum("flxy,yz->flxz", field, blocked, precision=lax.Precision.HIGHEST)
    return along_x.reshape(field.shape) + along_y


def join_edges(extended):
    width_x = extended.shape[2] - 2
    place_x = (jnp.arange(width_x) % 4)[:, None]
    center = extended[:, :, 1:-1, :]
    before = extended[:, :, :-2, :]
    after = extended[:, :, 2:, :]
    values = jnp.where(
        place_x == 3,
        0.5 * (center + after),
        jnp.where(place_x == 0, 0.5 * (center + before), center),
    )
    width_y = values.shape[3] - 2
    place_y = jnp.arange(width_y) % 4
    center = values[..., 1:-1]
    before = values[..., :-2]
    after = values[..., 2:]
    return jnp.where(
        place_y == 3,
        0.5 * (center + after),
        jnp.where(place_y == 0, 0.5 * (center + before), center),
    )


def build_matrix(mixing, relaxation):
    zero = jnp.zeros((1,), jnp.float32)
    diagonal = 1.0 + relaxation + jnp.concatenate([zero, mixing]) + jnp.concatenate([mixing, zero])
    return jnp.diag(diagonal) - jnp.diag(mixing, 1) - jnp.diag(mixing, -1)


def run_physics(columns, marks, factor, forcing):
    levels, fields, count = columns.shape
    classes = marks.astype(jnp.int32)
    push = forcing.T[:, :, None]
    current = columns
    for substep in range(SUBSTEPS):
        active = classes >= substep

        def advance(values, active=active):
            solved = (
                jax.scipy.linalg.cho_solve(
                    (factor, True), values.reshape(levels, fields * count)
                ).reshape(values.shape)
                + push
            )
            return jnp.where(active[None, None, :], solved, values)

        def unchanged(values):
            return values

        current = lax.cond(jnp.any(active), advance, unchanged, current)
    return current


def local(atmosphere_state, diffusivity, mixing, relaxation, forcing, span_map, cost_class):
    fields, slab, width_x, width_y = atmosphere_state.shape
    second_np = second_table()
    second = jnp.asarray(second_np)
    blocked = jnp.asarray(np.kron(np.eye(width_y // 4), second_np.T).astype(np.float32))
    current = atmosphere_state
    for repeat in range(STEPS):
        tendency = derive(current, second, blocked)
        extended = padded(tendency, (("ex", 2), ("ey", 3)), 1)
        current = current + diffusivity[:, None, None, None] * join_edges(extended)
    column_count = width_x * width_y
    flat = current.reshape(fields, slab, column_count)
    order = span_map.reshape(column_count)
    inverse = (
        jnp.zeros((column_count,), jnp.int32)
        .at[order]
        .set(jnp.arange(column_count, dtype=jnp.int32))
    )
    ordered = jnp.take(flat, order, axis=2)
    classes = jnp.take(cost_class.reshape(column_count), order).astype(jnp.float32)
    factor = jnp.linalg.cholesky(build_matrix(mixing, relaxation))
    slabs = lax.axis_size("lb")
    tiles = lax.axis_size("ex") * lax.axis_size("ey")
    levels = slab * slabs
    group = column_count // (tiles * slabs)
    received, marks_in = (
        lax.all_to_all(ordered, ("ex", "ey", "lb"), split_axis=2, concat_axis=2, tiled=True),
        lax.all_to_all(
            classes.reshape(1, 1, column_count),
            ("ex", "ey", "lb"),
            split_axis=2,
            concat_axis=2,
            tiled=True,
        ),
    )
    columns = (
        received.reshape(fields, slab, tiles, slabs, group)
        .transpose(3, 1, 0, 2, 4)
        .reshape(levels, fields, tiles * group)
    )
    marks = marks_in.reshape(tiles, slabs, group)[:, 0, :].reshape(tiles * group)
    physics = run_physics(columns, marks, factor, forcing)
    change = jnp.mean(physics - columns, axis=0).reshape(fields, tiles, group)
    shared = jnp.mean(change, axis=1)
    fixed = physics.reshape(slabs, slab, fields, tiles, group) - shared[None, None, :, None, :]
    outgoing = fixed.transpose(2, 1, 3, 0, 4)
    returned = lax.all_to_all(
        outgoing.reshape(fields, slab, column_count),
        ("ex", "ey", "lb"),
        split_axis=2,
        concat_axis=2,
        tiled=True,
    )
    placed = jnp.take(returned, inverse, axis=2)
    return placed.reshape(fields, slab, width_x, width_y)


def solution(mesh):
    return jax.shard_map(
        local,
        mesh=mesh,
        in_specs=(
            P(None, "lb", "ex", "ey"),
            P(),
            P(),
            P(),
            P(),
            P("ex", "ey", None),
            P("ex", "ey"),
        ),
        out_specs=P(None, "lb", "ex", "ey"),
        check_vma=False,
    )
```

profile of v0, /device:TPU:1, one launch (start us, length us, event | category | flops | bytes accessed | tf_op | source)
XLA Modules:
  0.0 395.9 jit_solution(16085769693843109632)
XLA Ops:
  58.6 8.3 %all-to-all-start = ((f32[1,1,1024]{1,0,2:T(1,128)}), f32[1,1,1024]{1,0,2:T(1,128)S(1)}, u32[]{:S(2)}, u32[]{:S(2)}) async-start(f32[1,1,1024]{1,0,2:T(1,128)} %copy.76), calls=%async_computation | async-start | bytes 1048576 | tf_op jit(solution)/shard_map/all_to_all | solution.py:144
  99.1 13.1 %gather_fusion.1 = f32[1024,15,32]{2,1,0:T(8,128)} fusion(f32[15,32,1024]{1,0,2:T(8,128)} %bitcast.118, s32[1024]{0:T(1024)S(1)} %fusion.46), kind=kCustom, calls=%fused_computation.clone | custom fusion | bytes 3936256 | tf_op jit(solution)/shard_map/jit(_take)/gather | solution.py:135
  112.2 8.7 %fusion.56 = f32[1024,15,32]{2,1,0:T(8,128)} fusion(f32[1024,15,32]{2,1,0:T(8,128)} %gather_fusion.1, pred[1024]{0:T(1024)(128)(4,1)S(1)} %compare_and_fusion.1), kind=kLoop, calls=%fused_computation.126 | loop fusion | flops 491520 | bytes 3933184
  120.8 7.7 %reshape.209 = f32[128,1,3840]{2,1,0:T(1,128)} reshape(f32[1024,15,32]{2,1,0:T(8,128)} %fusion.56) | data formatting | bytes 3932160
  128.5 11.2 %all-to-all-start.1 = ((f32[128,1,3840]{2,1,0:T(1,128)}), f32[128,1,3840]{2,1,0:T(1,128)S(1)}, u32[]{:S(2)}, u32[]{:S(2)}) async-start(f32[128,1,3840]{2,1,0:T(1,128)} %reshape.209), calls=%async_computation.1 | async-start | bytes 3932160 | tf_op jit(solution)/shard_map/all_to_all | solution.py:143
  140.0 11.7 %cholesky.19 = f32[128,128]{1,0:T(8,128)S(1)} custom-call(f32[128,128]{1,0:T(8,128)S(1)} %add_multiply_fusion), custom_call_target="Cholesky" | custom-call | tf_op jit(solution)/shard_map/jit(cholesky)/cholesky | solution.py:137
  158.7 10.5 %all-to-all-done.1 = f32[128,1,3840]{2,1,0:T(1,128)S(1)} async-done(((f32[128,1,3840]{2,1,0:T(1,128)}), f32[128,1,3840]{2,1,0:T(1,128)S(1)}, u32[]{:S(2)}, u32[]{:S(2)}) %all-to-all-start.1) | async-done | bytes 1966112 | tf_op jit(solution)/shard_map/all_to_all | solution.py:143
  184.2 9.0 %copy.94 = f32[15,32,1024]{1,2,0:T(8,128)} copy(f32[15,32,1024]{1,0,2:T(8,128)} %bitcast.111) | data formatting | bytes 3932160 | tf_op jit(solution)/shard_map/all_to_all | solution.py:143
  193.2 11.5 %copy.95 = f32[4,32,15,32,8]{1,0,4,3,2:T(4,128)} copy(f32[4,32,15,32,8]{1,2,4,0,3:T(8,128)} %bitcast.112) | data formatting | bytes 3932160 | tf_op jit(solution)/shard_map/transpose | solution.py:154
  204.7 7.2 %reshape.155 = f32[128,15,256]{0,2,1:T(8,128)} reshape(f32[4,32,15,32,8]{1,0,4,3,2:T(4,128)} %copy.95) | data formatting | bytes 3932160 | tf_op jit(solution)/shard_map/reshape | solution.py:155
  211.9 30.9 %conditional.4 = (f32[128,15,256]{0,2,1:T(8,128)S(1)}) conditional(s32[]{:T(128)} %convert_element_type.31, f32[128,15,256]{0,2,1:T(8,128)} %reshape.155, (s32[256]{0:T(256)S(1)}, f32[4,32,15,32,8]{1,4,0,3,2:T(8,128)}, f32[128,128]{1,0:T(8,128)S(1)}, f32[128,15,1]{0,1,2:T(8,128)S(1)}, f32[128,15,256]{0,2,1:T(8,128)}, /*index=5*/s32[]{:T(128)}) %tuple.69), branch_computations={%region_6.8_spmd, %region_7.10_spmd} | conditional | flops 1510965504 | bytes 29762600 | solution.py:113
  211.9 8.7 %copy.96 = f32[4,32,15,32,8]{1,0,4,3,2:T(4,128)} copy(f32[4,32,15,32,8]{1,4,0,3,2:T(8,128)} %get-tuple-element.105) | data formatting | bytes 3932160 | tf_op jit(solution)/shard_map
  226.8 9.8 %custom-call.11 = f32[1,128,128]{1,2,0:T(8,128)S(1)} custom-call(f32[1,128,128]{2,1,0:T(8,128)S(1)} %select_bitcast_fusion), custom_call_target="InvertDiagBlocksLowerTriangular" | custom-call | tf_op jit(solution)/shard_map/cond/branch_1_fun/jit(_cho_solve)/triangular_solve | solution.py:103
  242.7 15.6 %conditional.5 = (f32[128,15,256]{0,2,1:T(8,128)S(1)}) conditional(s32[]{:T(128)} %convert_element_type.30, f32[128,15,256]{0,2,1:T(8,128)S(1)} %get-tuple-element.131, (s32[256]{0:T(256)S(1)}, f32[128,15,256]{0,2,1:T(8,128)S(1)}, f32[128,128]{1,0:T(8,128)S(1)}, f32[128,15,1]{0,1,2:T(8,128)S(1)}, s32[]{:T(128)}) %tuple.70), branch_computations={%region_8.11_spmd, %region_9.12_spmd} | conditional | flops 1510965504 | bytes 14033932 | solution.py:113
  242.8 9.8 %custom-call.12 = f32[1,128,128]{1,2,0:T(8,128)S(1)} custom-call(f32[1,128,128]{2,1,0:T(8,128)S(1)} %select_bitcast_fusion.1), custom_call_target="InvertDiagBlocksLowerTriangular" | custom-call | tf_op jit(solution)/shard_map/cond/branch_1_fun/jit(_cho_solve)/triangular_solve | solution.py:103
  258.3 15.8 %conditional.6 = (f32[128,15,256]{0,2,1:T(8,128)S(1)}) conditional(s32[]{:T(128)} %convert_element_type.29, f32[128,15,256]{0,2,1:T(8,128)S(1)} %get-tuple-element.132, (s32[256]{0:T(256)S(1)}, f32[128,15,256]{0,2,1:T(8,128)S(1)}, f32[128,128]{1,0:T(8,128)S(1)}, f32[128,15,1]{0,1,2:T(8,128)S(1)}, s32[]{:T(128)}) %tuple.71), branch_computations={%region_10.13_spmd, %region_11.14_spmd} | conditional | flops 1510965504 | bytes 14033932 | solution.py:113
  258.5 9.8 %custom-call.13 = f32[1,128,128]{1,2,0:T(8,128)S(1)} custom-call(f32[1,128,128]{2,1,0:T(8,128)S(1)} %select_bitcast_fusion.2), custom_call_target="InvertDiagBlocksLowerTriangular" | custom-call | tf_op jit(solution)/shard_map/cond/branch_1_fun/jit(_cho_solve)/triangular_solve | solution.py:103
  274.1 16.2 %conditional.7 = (f32[128,15,256]{0,2,1:T(8,128)S(1)}) conditional(s32[]{:T(128)} %convert_element_type.28, f32[128,15,256]{0,2,1:T(8,128)S(1)} %get-tuple-element.133, (s32[256]{0:T(256)S(1)}, f32[128,15,256]{0,2,1:T(8,128)S(1)}, f32[128,128]{1,0:T(8,128)S(1)}, f32[128,15,1]{0,1,2:T(8,128)S(1)}) %tuple.72), branch_computations={%region_12.15_spmd, %region_13.16_spmd} | conditional | flops 1510965504 | bytes 14033928 | solution.py:113
  274.4 9.8 %custom-call.14 = f32[1,128,128]{1,2,0:T(8,128)S(1)} custom-call(f32[1,128,128]{2,1,0:T(8,128)S(1)} %select_bitcast_fusion.3), custom_call_target="InvertDiagBlocksLowerTriangular" | custom-call | tf_op jit(solution)/shard_map/cond/branch_1_fun/jit(_cho_solve)/triangular_solve | solution.py:103
  303.2 10.3 %copy.112 = f32[15,32,32,4,8]{1,0,4,3,2:T(8,128)} copy(f32[15,32,32,4,8]{1,3,4,2,0:T(4,128)S(1)} %subtract_bitcast_fusion) | data formatting | bytes 3932160 | tf_op jit(solution)/shard_map/reshape | solution.py:164
  313.5 7.7 %reshape.211 = f32[128,1,3840]{2,1,0:T(1,128)} reshape(f32[1024,15,32]{2,1,0:T(8,128)} %bitcast.114) | data formatting | bytes 3932160
  330.5 25.1 %all-to-all-done.2 = f32[128,1,3840]{2,1,0:T(1,128)} async-done(((f32[128,1,3840]{2,1,0:T(1,128)}), f32[128,1,3840]{2,1,0:T(1,128)}, u32[]{:S(2)}, u32[]{:S(2)}) %all-to-all-start.2) | async-done | bytes 1966112 | tf_op jit(solution)/shard_map/all_to_all | solution.py:163
  368.5 13.1 %gather_fusion.2 = f32[1024,15,32]{2,1,0:T(8,128)} fusion(f32[15,32,1024]{1,0,2:T(8,128)} %bitcast.119, s32[1024]{0:T(1024)S(1)} %fusion.47), kind=kCustom, calls=%fused_computation.1.clone | custom fusion | bytes 3936256 | tf_op jit(solution)/shard_map/jit(_take)/gather | solution.py:170
  381.5 8.7 %broadcast_select_fusion = f32[1024,15,32]{2,1,0:T(8,128)} fusion(f32[1024,15,32]{2,1,0:T(8,128)} %gather_fusion.2, pred[1024]{0:T(1024)(128)(4,1)S(1)} %compare_and_fusion), kind=kLoop, calls=%fused_computation.40 | loop fusion | flops 491520 | bytes 3933184 | tf_op jit(solution)/shard_map/jit(_take)/select_n | solution.py:170
  (131 shorter events, 179.7 us)
Async XLA Ops:
  0.0 30.7 %copy-start = (s32[8,128]{1,0:T(8,128)S(1)}, s32[8,128]{1,0:T(8,128)}, u32[]{:S(2)}) copy-start(s32[8,128]{1,0:T(8,128)} %param.27) | copy-start | bytes 12292
  0.0 5.3 %copy-start.4 = (f32[15,32,8,128]{3,2,1,0:T(8,128)S(1)}, f32[15,32,8,128]{3,2,1,0:T(8,128)}, u32[]{:S(2)}) copy-start(f32[15,32,8,128]{3,2,1,0:T(8,128)} %param.21) | copy-start | bytes 5898244
  0.0 5.3 %copy-start.7 = (f32[128,128,1,1]{1,0,3,2:T(8,128)S(1)}, f32[128,128,1,1]{1,0,3,2:T(8,128)}, u32[]{:S(2)}) copy-start(f32[128,128,1,1]{1,0,3,2:T(8,128)} %constant.152) | copy-start | bytes 196612
  5.3 5.7 %copy-start.9 = (s32[1,1,1024]{2,1,0:T(1,128)S(1)}, s32[1,1,1024]{2,1,0:T(1,128)}, u32[]{:S(2)}) copy-start(s32[1,1,1024]{2,1,0:T(1,128)} %param.26) | copy-start | bytes 12292
  7.3 8.3 %collective-permute-start.1 = (f32[15,32,1,128]{3,1,2,0:T(8,128)S(1)}, f32[15,32,1,128]{3,1,2,0:T(8,128)S(1)}, u32[]{:S(2)}, u32[]{:S(2)}) collective-permute-start(f32[15,32,1,128]{3,1,2,0:T(8,128)S(1)} %get-tuple-element.121), channel_id=1, source_target_pairs={{32,0},{64,32},{96,64},{0,96},{33,1},{65,33},{97,65},{1,97},{34,2}... | collective-permute-start | bytes 737288 | tf_op jit(solution)/shard_map/ppermute | solution.py:22
  11.0 7.7 %collective-permute-start = (f32[15,32,1,128]{3,1,2,0:T(8,128)S(1)}, f32[15,32,1,128]{3,1,2,0:T(8,128)S(1)}, u32[]{:S(2)}, u32[]{:S(2)}) collective-permute-start(f32[15,32,1,128]{3,1,2,0:T(8,128)S(1)} %get-tuple-element.120), channel_id=1, source_target_pairs={{0,32},{32,64},{64,96},{96,0},{1,33},{33,65},{65,97},{97,1},{2,34}... | collective-permute-start | bytes 737288 | tf_op jit(solution)/shard_map/ppermute | solution.py:20
  24.6 11.0 %collective-permute-start.3 = (f32[15,32,10,1]{1,3,2,0:T(1,128)S(1)}, f32[15,32,10,1]{1,3,2,0:T(1,128)S(1)}, u32[]{:S(2)}, u32[]{:S(2)}) collective-permute-start(f32[15,32,10,1]{1,3,2,0:T(1,128)S(1)} %copy.80), channel_id=1, source_target_pairs={{4,0},{8,4},{12,8},{16,12},{20,16},{24,20},{28,24},{0,28},{5,1},{9... | collective-permute-start | bytes 57608 | tf_op jit(solution)/shard_map/ppermute | solution.py:22
  29.1 9.0 %collective-permute-start.2 = (f32[15,32,10,1]{1,3,2,0:T(1,128)S(1)}, f32[15,32,10,1]{1,3,2,0:T(1,128)S(1)}, u32[]{:S(2)}, u32[]{:S(2)}) collective-permute-start(f32[15,32,10,1]{1,3,2,0:T(1,128)S(1)} %copy.79), channel_id=1, source_target_pairs={{0,4},{4,8},{8,12},{12,16},{16,20},{20,24},{24,28},{28,0},{1,5},{5... | collective-permute-start | bytes 57608 | tf_op jit(solution)/shard_map/ppermute | solution.py:20
  45.3 1.5 copy-start.5
  45.3 1.5 copy-start.11
  54.6 1.3 copy-start.3
  55.9 11.1 %collective-permute-start.5 = (f32[15,32,1,128]{3,1,2,0:T(8,128)S(1)}, f32[15,32,1,128]{3,1,2,0:T(8,128)S(1)}, u32[]{:S(2)}, u32[]{:S(2)}) collective-permute-start(f32[15,32,1,128]{3,1,2,0:T(8,128)S(1)} %get-tuple-element.119), channel_id=1, source_target_pairs={{32,0},{64,32},{96,64},{0,96},{33,1},{65,33},{97,65},{1,97},{34,2}... | collective-permute-start | bytes 737288 | tf_op jit(solution)/shard_map/ppermute | solution.py:22
  56.0 11.0 %collective-permute-start.4 = (f32[15,32,1,128]{3,1,2,0:T(8,128)S(1)}, f32[15,32,1,128]{3,1,2,0:T(8,128)S(1)}, u32[]{:S(2)}, u32[]{:S(2)}) collective-permute-start(f32[15,32,1,128]{3,1,2,0:T(8,128)S(1)} %get-tuple-element.118), channel_id=1, source_target_pairs={{0,32},{32,64},{64,96},{96,0},{1,33},{33,65},{65,97},{97,1},{2,34}... | collective-permute-start | bytes 737288 | tf_op jit(solution)/shard_map/ppermute | solution.py:20
  58.6 69.9 %all-to-all-start = ((f32[1,1,1024]{1,0,2:T(1,128)}), f32[1,1,1024]{1,0,2:T(1,128)S(1)}, u32[]{:S(2)}, u32[]{:S(2)}) async-start(f32[1,1,1024]{1,0,2:T(1,128)} %copy.76), calls=%async_computation | async-start | bytes 1048576 | tf_op jit(solution)/shard_map/all_to_all | solution.py:144
  74.5 4.4 %collective-permute-start.7 = (f32[15,32,10,1]{1,3,2,0:T(1,128)S(1)}, f32[15,32,10,1]{1,3,2,0:T(1,128)S(1)}, u32[]{:S(2)}, u32[]{:S(2)}) collective-permute-start(f32[15,32,10,1]{1,3,2,0:T(1,128)S(1)} %copy.89), channel_id=1, source_target_pairs={{4,0},{8,4},{12,8},{16,12},{20,16},{24,20},{28,24},{0,28},{5,1},{9... | collective-permute-start | bytes 57608 | tf_op jit(solution)/shard_map/ppermute | solution.py:22
  78.2 3.4 collective-permute-start.6
  128.5 11.2 %copy-start.12 = (f32[127]{0:T(128)S(1)}, f32[127]{0:T(128)}, u32[]{:S(2)}) copy-start(f32[127]{0:T(128)} %param.23) | copy-start | bytes 1528
  128.5 11.2 %copy-start.13 = (f32[128]{0:T(128)S(1)}, f32[128]{0:T(128)}, u32[]{:S(2)}) copy-start(f32[128]{0:T(128)} %param.24) | copy-start | bytes 1540
  128.5 40.6 %all-to-all-start.1 = ((f32[128,1,3840]{2,1,0:T(1,128)}), f32[128,1,3840]{2,1,0:T(1,128)S(1)}, u32[]{:S(2)}, u32[]{:S(2)}) async-start(f32[128,1,3840]{2,1,0:T(1,128)} %reshape.209), calls=%async_computation.1 | async-start | bytes 3932160 | tf_op jit(solution)/shard_map/all_to_all | solution.py:143
  169.2 1.3 copy-start.6
  204.7 7.2 %copy-start.8 = (f32[15,128]{1,0:T(8,128)S(1)}, f32[15,128]{1,0:T(8,128)}, u32[]{:S(2)}) copy-start(f32[15,128]{1,0:T(8,128)} %param.25) | copy-start | bytes 23044
  238.4 3.3 copy-start.2
  321.2 34.3 %all-to-all-start.2 = ((f32[128,1,3840]{2,1,0:T(1,128)}), f32[128,1,3840]{2,1,0:T(1,128)}, u32[]{:S(2)}, u32[]{:S(2)}) async-start(f32[128,1,3840]{2,1,0:T(1,128)} %reshape.211), calls=%async_computation.2 | async-start | bytes 3932160 | tf_op jit(solution)/shard_map/all_to_all | solution.py:163
  390.2 5.5 %copy-start.1 = (s32[8,128]{1,0:T(8,128)S(1)}, s32[8,128]{1,0:T(8,128)}, u32[]{:S(2)}) copy-start(s32[8,128]{1,0:T(8,128)} %param.27) | copy-start | bytes 12292
  (1 other events, 1.1 us)
where the time goes:
time: 403 us; the launch traced here: 396 us
  local copies, waits for them, and re-layouts  165 us (41%)
  other arithmetic  114 us (28%)
  waiting for transfers between devices  43.5 us (11%)
  starting transfers between devices  34.9 us (9%)
  matrix products  34.2 us (8%)
    another operation x8, other arithmetic, advance(): jax.scipy.linalg.cho_solve((factor, True), values.reshape(levels, fields...  39.3 us
    unnamed x30, local copies, waits for them, and re-layouts  30.6 us
    all_to_all x1, waiting for transfers between devices, local(): lax.all_to_all(outgoing.reshape(fields, slab, column_count), ('ex', 'ey',...  25.1 us
    another operation x8, matrix products, advance(): jax.scipy.linalg.cho_solve((factor, True), values.reshape(levels, fields...  20.6 us
    gather x1, local copies, waits for them, and re-layouts, local(): placed = jnp.take(returned, inverse, axis=2)  13.1 us
    gather x1, local copies, waits for them, and re-layouts, local(): ordered = jnp.take(flat, order, axis=2)  13.1 us
    another operation x3, other arithmetic, local(): factor = jnp.linalg.cholesky(build_matrix(mixing, relaxation))  12.4 us
    concatenate x4, other arithmetic, padded(): jnp.concatenate([lax.ppermute(tail, axis, [(i, (i + 1) % count) for i in...  11.8 us
  transfers between devices with their start and end apart: 11, of which 5 were waited for; matrix products, arithmetic and copies ran while one was open for 23% of the time, Pallas kernels for 0%

commit v1 on v0

v1 whole, which is shorter than its diff:
```python
import math

import jax
import jax.numpy as jnp
import ml_dtypes
import numpy as np
from jax import lax
from jax.experimental import pallas as pl
from jax.experimental.pallas import tpu as pltpu
from jax.sharding import PartitionSpec as P

F32 = jnp.float32
BF16 = jnp.bfloat16
FIELDS = 15
SLAB = 32
ROWS = 8
LANES = 128
LEVELS = 128
TILES = 32
PER = SLAB * ROWS


def second_table():
    inner_root = 1.0 / math.sqrt(5.0)
    nodes = np.array([-1.0, -inner_root, inner_root, 1.0])
    weights = np.array(
        [np.prod([nodes[t] - nodes[s] for s in range(4) if s != t]) for t in range(4)]
    )
    first = np.zeros((4, 4))
    for t in range(4):
        for s in range(4):
            if s != t:
                first[t, s] = weights[t] / (weights[s] * (nodes[t] - nodes[s]))
    for t in range(4):
        first[t, t] = -first[t].sum()
    return first @ first


G = second_table()
NODE = 1.0 / math.sqrt(5.0)
EVEN0 = float(0.5 * (G[0, 0] + G[3, 0]))
ODD3 = float(0.5 * (G[3, 3] - G[0, 3]))
ODD2 = float(0.5 * (G[3, 2] - G[0, 2]))


def y_weights():
    span = 160
    gy = np.kron(np.eye(span // 4), G)
    ey = np.eye(span)
    for left in range(3, span - 1, 4):
        ey[left, left] = ey[left + 1, left + 1] = 0.5
        ey[left, left + 1] = ey[left + 1, left] = 0.5
    b = ey @ gy
    whole = np.zeros((256, 512))
    for index, op in enumerate((ey, b, b @ ey, b @ b)):
        take = op[16:144, :].T
        cols = slice(128 * index, 128 * index + 128)
        whole[:128, cols] = take[16:144]
        whole[128:136, cols] = take[144:152]
        whole[248:256, cols] = take[8:16]
    high = whole.astype(ml_dtypes.bfloat16)
    low = (whole - high.astype(np.float64)).astype(ml_dtypes.bfloat16)
    return high, low


def dot(a, b, dims=(((1,), (0,)), ((), ()))):
    return lax.dot_general(a, b, dims, preferred_element_type=F32)


def split2(x):
    high = x.astype(BF16)
    return high, (x - high.astype(F32)).astype(BF16)


def split3(x):
    high = x.astype(BF16)
    rest = x - high.astype(F32)
    mid = rest.astype(BF16)
    return high, mid, (rest - mid.astype(F32)).astype(BF16)


def prep_kernel(mix_ref, rel_ref, g_ref, span_ref, c_ref, ot_ref, pad, sols, buf):
    j = lax.axis_index("lb")
    row = lax.broadcasted_iota(jnp.int32, (8, LANES), 0)
    lane = lax.broadcasted_iota(jnp.int32, (8, LANES), 1)
    pad[...] = jnp.zeros((8, LANES), F32)
    pad[0:1, 0 : LEVELS - 1] = mix_ref[...]
    m = jnp.broadcast_to(pad[0:1, :], (8, LANES))
    rel = jnp.broadcast_to(rel_ref[...], (8, LANES))
    cut = jnp.where(row < 3, 32 * row + 31, jnp.where(row < 6, 32 * row - 65, -1))
    cutm = jnp.where(lane == cut, m, 0.0)
    kap = jnp.where(lane == cut, 0.0, m)
    after = pltpu.roll(cutm, 1, 1)
    e = 1.0 + rel + cutm + after
    kp = pltpu.roll(kap, 1, 1)
    a, b, c, d = e + kp, e * kp, jnp.ones_like(e), kp
    for t in (1, 2, 4, 8, 16, 32, 64):
        inside = lane >= t
        a2 = jnp.where(inside, pltpu.roll(a, t, 1), 1.0)
        b2 = jnp.where(inside, pltpu.roll(b, t, 1), 0.0)
        c2 = jnp.where(inside, pltpu.roll(c, t, 1), 0.0)
        d2 = jnp.where(inside, pltpu.roll(d, t, 1), 1.0)
        na, nb, nc, nd = a * a2 + b * c2, a * b2 + b * d2, c * a2 + d * c2, c * b2 + d * d2
        scale = 1.0 / (na + nb + nc + nd)
        a, b, c, d = na * scale, nb * scale, nc * scale, nd * scale
    p = (a + b) / (c + d) + kap
    inv = 1.0 / p
    eps = kap * inv
    gam = pltpu.roll(eps, 1, 1)
    fwd, bwd = [gam], [eps]
    for t in (1, 2, 4, 8, 16, 32):
        fwd.append(fwd[-1] * pltpu.roll(fwd[-1], t, 1))
        bwd.append(bwd[-1] * pltpu.roll(bwd[-1], LANES - t, 1))
    rhs = jnp.where(row < 3, cutm, jnp.where(row < 6, after, 1.0))
    x = rhs
    stack = []
    for k in range(4):
        for s in range(7):
            x = x + fwd[s] * pltpu.roll(x, 1 << s, 1)
        x = x * inv
        for s in range(7):
            x = x + bwd[s] * pltpu.roll(x, LANES - (1 << s), 1)
        sols[k] = x
        stack.append(x)
    buf[...] = jnp.zeros(buf.shape, F32)
    for r in (1, 2, 3):
        s = lax.rem(j + r, 4)
        at = jnp.where(s > j, s - 1, s + 3)
        for k in range(4):
            buf[4 * (r - 1) + k : 4 * (r - 1) + k + 1, :] = sols[k, pl.ds(at, 1), :]
    for k in range(4):
        buf[12 + k : 13 + k, :] = (stack[k][6:7] - 1.0) * (1.0 / LEVELS)

    def pick(value, which):
        kept = jnp.where((row == which) & (row < 6), value * rhs, 0.0)
        return jnp.sum(jnp.sum(kept, axis=1, keepdims=True), axis=0, keepdims=True)

    below0 = pick(stack[0], j + 3)
    last = lane[6:7] == 32 * j + 31
    fixed = 1.0 / (p[6:7] - jnp.where(last, below0, 0.0))
    buf[16:17, :] = gam[6:7]
    buf[17:18, :] = fixed
    buf[18:19, :] = eps[6:7]
    buf[40 : 40 + FIELDS, :] = g_ref[...]
    c_ref[...] = pltpu.roll(buf[...], lax.rem(LANES - 32 * j, LANES), 1)
    hrow = jnp.zeros((1, LANES), F32)
    for n in (1, 2, 3):
        hrow = jnp.where(lane[0:1] == n, pick(stack[n], j - 1), hrow)
        hrow = jnp.where(lane[0:1] == 8 + n, pick(stack[n], j + 3), hrow)
    c_ref[19:20, :] = hrow
    zero = jnp.zeros((1, LANES), F32)
    sums = []
    for r in range(3):
        total = zero
        for k in range(4):
            sums.append(total)
            total = total + c_ref[4 * r + k : 4 * r + k + 1, :]
    total = zero + 1.0 / LEVELS
    for k in range(4):
        sums.append(total)
        total = total + c_ref[12 + k : 13 + k, :] + 1.0 / LEVELS
    own = lax.broadcasted_iota(jnp.int32, (16, LANES), 1) < SLAB
    sums = jnp.where(own, jnp.concatenate(sums, axis=0), 0.0)
    push = c_ref[40:56, :]
    c_ref[20:36, 0:16] = lax.dot_general(
        sums,
        push,
        (((1,), (1,)), ((), ())),
        precision=lax.Precision.HIGHEST,
        preferred_element_type=F32,
    )
    spots = span_ref[...]
    for block in range(8):
        place = lax.broadcasted_iota(jnp.int32, (LANES, 1024), 0) + LANES * block
        ot_ref[LANES * block : LANES * (block + 1), :] = jnp.where(
            place == spots, 1.0, 0.0
        ).astype(BF16)


def pack_kernel(x_ref, l_ref, r_ref):
    lane = lax.broadcasted_iota(jnp.int32, (2, ROWS, LANES), 2) // 8
    left = jnp.zeros((2, ROWS, LANES), F32)
    right = jnp.zeros((2, ROWS, LANES), F32)
    for q in range(16):
        turned = x_ref[:, q]
        if q:
            turned = pltpu.roll(turned, 8 * q, 2)
        left = jnp.where(lane == q, turned, left)
        right = jnp.where(lane == (q - 1) % 16, turned, right)
    l_ref[...] = left
    r_ref[...] = right


def along_x(rows):
    out = []
    for e in (0, 4):
        u0, u1, u2, u3 = rows[e : e + 4]
        even = EVEN0 * ((u0 + u3) - (u1 + u2))
        odd = ODD2 * (u2 - u1) + ODD3 * (u3 - u0)
        inner = NODE * odd
        out += [even - odd, even - inner, even + inner, even + odd]
    return out


def half_joined(rows):
    middle = 0.5 * (rows[3] + rows[4])
    return [0.5 * rows[0], rows[1], rows[2], middle, middle, rows[5], rows[6], 0.5 * rows[7]]


def move_kernel(d_ref, x_ref, hl_ref, hr_ref, wh_ref, wl_ref, u_ref, down_ref, up_ref, xh):
    d = d_ref[pl.program_id(0)]
    lane = lax.broadcasted_iota(jnp.int32, (2, ROWS, LANES), 2)
    for q in range(16):
        hl, hr = hl_ref[...], hr_ref[...]
        if q:
            hl = pltpu.roll(hl, LANES - 8 * q, 2)
            hr = pltpu.roll(hr, LANES - 8 * q, 2)
        both = jnp.where(lane >= LANES - 8, hl, jnp.where(lane < 8, hr, 0.0))
        xh[8 * q : 8 * q + 8, :] = both[0]
        xh[128 + 8 * q : 136 + 8 * q, :] = both[1]
    rows = [x_ref[pl.ds(r, SLAB, stride=ROWS), :] for r in range(ROWS)]
    halo = [xh[pl.ds(r, SLAB, stride=ROWS), :] for r in range(ROWS)]
    main = jnp.concatenate(
        [jnp.concatenate(rows, axis=0), jnp.concatenate(halo, axis=0)], axis=1
    )
    high, low = split2(main)
    wh = wh_ref[...]
    t = dot(high, wh) + dot(low, wh) + dot(high, wl_ref[...])
    t1, t2, t3, t4 = [
        [t[SLAB * r : SLAB * r + SLAB, LANES * i : LANES * i + LANES] for r in range(ROWS)]
        for i in range(4)
    ]
    w1 = [g + s for g, s in zip(along_x(t1), t2)]
    w2 = [g + s for g, s in zip(along_x(t3), t4)]
    e1 = [d * v for v in half_joined(w1)]
    r1 = [s + v for s, v in zip(t1, e1)]
    r2 = [s + d * v for s, v in zip(t2, half_joined(w2))]
    w3 = [g + s for g, s in zip(along_x(r1), r2)]
    out = [u + v + d * w for u, v, w in zip(rows, e1, half_joined(w3))]
    half = 0.5 * d
    quarter = half * half
    out[0] = out[0] + quarter * (float(G[3, 3]) * w1[0] + w2[0])
    out[7] = out[7] + quarter * (float(G[0, 0]) * w1[7] + w2[7])
    for r in range(ROWS):
        u_ref[SLAB * r : SLAB * r + SLAB, :] = out[r]
    down_ref[0, 0] = w1[7]
    down_ref[0, 1] = w3[7] + half * w2[7]
    up_ref[0, 0] = w1[0]
    up_ref[0, 1] = w3[0] + half * w2[0]


def meet_kernel(
    d_ref, c_ref, u_ref, top_ref, bot_ref, class_ref, ot_ref,
    x_ref, m1_ref, m2_ref, m3_ref, slot_ref, swt, ch,
):
    f = pl.program_id(0)
    kind = class_ref[...]

    def by_class(values):
        return jnp.where(
            kind >= 2,
            jnp.where(kind == 2, values[2], values[3]),
            jnp.where(kind == 0, values[0], values[1]),
        )

    @pl.when(f == 0)
    def _():
        for l in range(SLAB):
            swt[8 * l : 8 * l + 8, :] = by_class([c_ref[12 + k, l] for k in range(4)])
        ch[...] = jnp.zeros(ch.shape, F32)

    d = d_ref[f]
    half = 0.5 * d
    quarter = half * half
    wt, zt, wb, zb = top_ref[0, 0], top_ref[0, 1], bot_ref[0, 0], bot_ref[0, 1]
    cross_t = quarter * float(G[3, 0]) * wt
    cross_b = quarter * float(G[0, 3]) * wb
    cross = cross_t + cross_b
    add = [
        (half + quarter * float(G[0, 0])) * wt + half * zt,
        (2.0 * quarter * float(G[1, 0])) * wt,
        (2.0 * quarter * float(G[2, 0])) * wt,
        cross,
        cross,
        (2.0 * quarter * float(G[1, 3])) * wb,
        (2.0 * quarter * float(G[2, 3])) * wb,
        (half + quarter * float(G[3, 3])) * wb + half * zb,
    ]
    for r in range(ROWS):
        x_ref[pl.ds(r, SLAB, stride=ROWS), :] = u_ref[SLAB * r : SLAB * r + SLAB, :] + add[r]
    total = [jnp.zeros((ROWS, LANES), F32)] * 13
    for l in range(SLAB):
        x = x_ref[8 * l : 8 * l + 8, :]
        for v in range(12):
            total[v] = total[v] + c_ref[v, l] * x
        total[12] = total[12] + swt[8 * l : 8 * l + 8, :] * x
    for r, ref in enumerate((m1_ref, m2_ref, m3_ref)):
        for k in range(4):
            ref[0, k] = total[4 * r + k] + c_ref[20 + 4 * r + k, f]
    ch[pl.ds(pl.multiple_of(8 * f, 8), 8), :] = total[12] + by_class(
        [c_ref[32 + k, f] for k in range(4)]
    )

    @pl.when(f == FIELDS - 1)
    def _():
        ordered = jnp.zeros((48, 1024), F32)
        for a in range(ROWS):
            part = jnp.concatenate(split3(ch[pl.ds(a, 16, stride=ROWS), :]), axis=0)
            ordered = ordered + dot(part, ot_ref[LANES * a : LANES * a + LANES, :])
        ordered = ordered[0:16] + ordered[16:32] + ordered[32:48]
        for block in range(8):
            slot_ref[16 * block : 16 * block + 16, :] = ordered[:, LANES * block : LANES * block + LANES]


def solve_kernel(c_ref, x_ref, r1_ref, r2_ref, r3_ref, class_ref, o_ref, z):
    group = x_ref.shape[0]
    base = pl.program_id(0) * group
    j = lax.axis_index("lb")
    kind = class_ref[...]
    ups, downs = [], []
    for k in range(4):
        above = jnp.zeros((group, ROWS, LANES), F32)
        below = jnp.zeros((group, ROWS, LANES), F32)
        for r, ref in enumerate((r1_ref, r2_ref, r3_ref)):
            got = ref[:, k]
            from_above = j - (r + 1) >= 0
            above = above + jnp.where(from_above, got, 0.0)
            below = below + jnp.where(from_above, 0.0, got)
        ups.append(above)
        downs.append(below)
    firsts, lasts = [], []
    for k in range(4):
        source = x_ref if k == 0 else o_ref
        above, below = ups[k], downs[k]
        for i in range(k):
            above = above + c_ref[19, k - i] * firsts[i]
            below = below + c_ref[19, 8 + k - i] * lasts[i]
        run = source[:, 0] + above
        z[:, 0] = run
        for l in range(1, SLAB):
            run = source[:, l] + c_ref[16, l] * run
            if l < SLAB - 1:
                z[:, l] = run
        run = (run + below) * c_ref[17, SLAB - 1]
        lasts.append(run)
        active = kind >= k
        for l in range(SLAB - 1, -1, -1):
            if l < SLAB - 1:
                run = c_ref[17, l] * z[:, l] + c_ref[18, l] * run
            old = source[:, l]
            for i in range(group):
                new = run[i] + c_ref[40 + base + i, l]
                o_ref[i, l] = new if k == 0 else jnp.where(active, new, old[i])
        firsts.append(run)


def share_kernel(p_ref, tot_ref, ot_ref, o_ref, sh):
    group = p_ref.shape[0]
    step = pl.program_id(0)

    @pl.when(step == 0)
    def _():
        whole = jnp.concatenate([tot_ref[16 * b : 16 * b + 16, :] for b in range(8)], axis=1)
        whole = jnp.concatenate(split3(whole), axis=0)
        for a in range(ROWS):
            back = dot(whole, ot_ref[LANES * a : LANES * a + LANES, :], (((1,), (1,)), ((), ())))
            back = (back[0:16] + back[16:32] + back[32:48]) * (1.0 / TILES)
            sh[pl.ds(a, 16, stride=ROWS), :] = back

    for i in range(group):
        at = pl.multiple_of((step * group + i) * 8, 8)
        own = sh[pl.ds(at, 8), :]
        for l in range(SLAB):
            o_ref[i, l] = p_ref[i, l] - own


SMEM = pl.BlockSpec(memory_space=pltpu.SMEM)


def whole_spec(shape):
    zeros = (0,) * len(shape)
    return pl.BlockSpec(shape, lambda *_: zeros)


def shaped(*shape, dtype=F32):
    return jax.ShapeDtypeStruct(shape, dtype)


LIMIT = pltpu.CompilerParams(vmem_limit_bytes=40 * 1024 * 1024)


def shift(axis, step):
    count = lax.axis_size(axis)
    return [(i, (i + step) % count) for i in range(count)]


def local(atmosphere_state, diffusivity, mixing, relaxation, forcing, span_map, cost_class):
    state = atmosphere_state
    group = 5
    coef, onehot = pl.pallas_call(
        prep_kernel,
        out_shape=(shaped(56, LANES), shaped(1024, 1024, dtype=BF16)),
        scratch_shapes=[
            pltpu.VMEM((8, LANES), F32),
            pltpu.VMEM((4, 8, LANES), F32),
            pltpu.VMEM((56, LANES), F32),
        ],
        compiler_params=LIMIT,
        name="prep",
    )(mixing.reshape(1, -1), relaxation.reshape(1, -1), forcing, span_map.reshape(1, -1))

    left, right = pl.pallas_call(
        pack_kernel,
        grid=(FIELDS,),
        in_specs=[pl.BlockSpec((2, 16, ROWS, LANES), lambda f: (f, 0, 0, 0))],
        out_specs=[pl.BlockSpec((2, ROWS, LANES), lambda f: (f, 0, 0))] * 2,
        out_shape=(shaped(30, ROWS, LANES), shaped(30, ROWS, LANES)),
        compiler_params=LIMIT,
        name="pack",
    )(state.reshape(30, 16, ROWS, LANES))
    from_left = lax.ppermute(right, "ey", shift("ey", 1))
    from_right = lax.ppermute(left, "ey", shift("ey", -1))

    high, low = y_weights()
    edge = pl.BlockSpec((1, 2, SLAB, LANES), lambda f: (f, 0, 0, 0))
    block = pl.BlockSpec((PER, LANES), lambda f: (f, 0))
    part, down, up = pl.pallas_call(
        move_kernel,
        grid=(FIELDS,),
        in_specs=[
            SMEM,
            block,
            pl.BlockSpec((2, ROWS, LANES), lambda f: (f, 0, 0)),
            pl.BlockSpec((2, ROWS, LANES), lambda f: (f, 0, 0)),
            whole_spec((256, 512)),
            whole_spec((256, 512)),
        ],
        out_specs=[block, edge, edge],
        out_shape=(
            shaped(FIELDS * PER, LANES),
            shaped(FIELDS, 2, SLAB, LANES),
            shaped(FIELDS, 2, SLAB, LANES),
        ),
        scratch_shapes=[pltpu.VMEM((PER, LANES), F32)],
        compiler_params=LIMIT,
        name="move",
    )(
        diffusivity,
        state.reshape(FIELDS * PER, LANES),
        from_left,
        from_right,
        jnp.asarray(high),
        jnp.asarray(low),
    )
    top = lax.ppermute(down, "ex", shift("ex", 1))
    bottom = lax.ppermute(up, "ex", shift("ex", -1))

    four = pl.BlockSpec((1, 4, ROWS, LANES), lambda f: (f, 0, 0, 0))
    moved, m1, m2, m3, slots = pl.pallas_call(
        meet_kernel,
        grid=(FIELDS,),
        in_specs=[
            SMEM, SMEM, block, edge, edge,
            whole_spec((ROWS, LANES)),
            whole_spec((1024, 1024)),
        ],
        out_specs=[block, four, four, four, whole_spec((LANES, LANES))],
        out_shape=(
            shaped(FIELDS * PER, LANES),
            shaped(FIELDS, 4, ROWS, LANES),
            shaped(FIELDS, 4, ROWS, LANES),
            shaped(FIELDS, 4, ROWS, LANES),
            shaped(LANES, LANES),
        ),
        scratch_shapes=[pltpu.VMEM((PER, LANES), F32), pltpu.VMEM((LANES, LANES), F32)],
        compiler_params=LIMIT,
        name="meet",
    )(diffusivity, coef, part, top, bottom, cost_class, onehot)

    s1, s2, s3 = [lax.ppermute(slots, "lb", shift("lb", r)) for r in (1, 2, 3)]
    g1, g2, g3 = [
        lax.ppermute(m, "lb", shift("lb", r)) for m, r in ((m1, 1), (m2, 2), (m3, 3))
    ]
    tiles = ("ex", "ey")
    summed = (slots + s1 + s2 + s3).reshape(TILES, 4, LANES)
    mine = lax.all_to_all(summed, tiles, split_axis=0, concat_axis=0, tiled=True)
    mine = jnp.broadcast_to(jnp.sum(mine, axis=0, keepdims=True), (TILES, 4, LANES))
    total = lax.all_to_all(mine, tiles, split_axis=0, concat_axis=0, tiled=True)

    five = pl.BlockSpec((group, SLAB, ROWS, LANES), lambda f: (f, 0, 0, 0))
    few = pl.BlockSpec((group, 4, ROWS, LANES), lambda f: (f, 0, 0, 0))
    physics = pl.pallas_call(
        solve_kernel,
        grid=(FIELDS // group,),
        in_specs=[SMEM, five, few, few, few, whole_spec((ROWS, LANES))],
        out_specs=five,
        out_shape=shaped(FIELDS, SLAB, ROWS, LANES),
        scratch_shapes=[pltpu.VMEM((group, SLAB, ROWS, LANES), F32)],
        compiler_params=LIMIT,
        name="solve",
    )(coef, moved.reshape(FIELDS, SLAB, ROWS, LANES), g1, g2, g3, cost_class)

    return pl.pallas_call(
        share_kernel,
        grid=(FIELDS // group,),
        in_specs=[five, whole_spec((LANES, LANES)), whole_spec((1024, 1024))],
        out_specs=five,
        out_shape=shaped(FIELDS, SLAB, ROWS, LANES),
        scratch_shapes=[pltpu.VMEM((LANES, LANES), F32)],
        compiler_params=LIMIT,
        name="share",
    )(physics, total.reshape(LANES, LANES), onehot)


def solution(mesh):
    return jax.shard_map(
        local,
        mesh=mesh,
        in_specs=(
            P(None, "lb", "ex", "ey"),
            P(),
            P(),
            P(),
            P(),
            P("ex", "ey", None),
            P("ex", "ey"),
        ),
        out_specs=P(None, "lb", "ex", "ey"),
        check_vma=False,
    )
```

time: 403 us -> 84.7 us (0.21)
  the two profiles are of different devices: /device:TPU:1 before, /device:TPU:0 now
where the time goes in v1:
time: 84.7 us; the launch traced here: 83.4 us
  Pallas kernels  30.4 us (36%)
  starting transfers between devices  19.7 us (23%)
  blocking collectives  14.5 us (17%)
  waiting for transfers between devices  10.7 us (13%)
  local copies, waits for them, and re-layouts  7.85 us (9%)
    all_to_all x1, blocking collectives, local(): lax.all_to_all(summed, tiles, split_axis=0, concat_axis=0, tiled=True)  14.5 us
    pallas_call x1, Pallas kernels, local(): pl.pallas_call(move_kernel, grid=(FIELDS,), in_specs=[SMEM, block, pl.Blo...  9.04 us
    pallas_call x1, Pallas kernels, local(): pl.pallas_call(meet_kernel, grid=(FIELDS,), in_specs=[SMEM, SMEM, block,...  8.05 us
    unnamed x26, local copies, waits for them, and re-layouts  7.21 us
    ppermute x1, waiting for transfers between devices, local(): top = lax.ppermute(down, 'ex', shift('ex', 1))  6.16 us
    pallas_call x1, Pallas kernels, local(): pl.pallas_call(prep_kernel, out_shape=(shaped(56, LANES), shaped(1024, 10...  5.27 us
    ppermute x3, starting transfers between devices, local(): lax.ppermute(m, 'lb', shift('lb', r))  4.51 us
    ppermute x3, starting transfers between devices, local(): s1, s2, s3 = [lax.ppermute(slots, 'lb', shift('lb', r)) for r in (1, 2, 3)]  4.44 us
  transfers between devices with their start and end apart: 11, of which 5 were waited for; matrix products, arithmetic and copies ran while one was open for 1% of the time, Pallas kernels for 11%

profile of v1, /device:TPU:0, one launch (start us, length us, event | category | flops | bytes accessed | tf_op | source)
XLA Modules:
  0.0 83.4 jit_solution(16689998093591404953)
XLA Ops:
  0.0 1.6 %copy-done.2 = f32[15,32,8,128]{3,2,1,0:T(8,128)S(1)} copy-done((f32[15,32,8,128]{3,2,1,0:T(8,128)S(1)}, f32[15,32,8,128]{3,2,1,0:T(8,128)}, u32[]{:S(2)}) %copy-start.2) | copy-done | bytes 1966104
  1.6 1.6 %pack.1 = (f32[30,8,128]{2,1,0:T(8,128)S(1)}, f32[30,8,128]{2,1,0:T(8,128)S(1)}) custom-call(f32[30,16,8,128]{3,2,1,0:T(8,128)S(1)} %bitcast.8), custom_call_target="tpu_custom_call" | custom-call | tf_op jit(solution)/shard_map/pack/pallas_call | solution.py:412
  3.2 3.6 %collective-permute-start.1 = (f32[30,8,128]{2,1,0:T(8,128)S(1)}, f32[30,8,128]{2,1,0:T(8,128)S(1)}, u32[]{:S(2)}, u32[]{:S(2)}) collective-permute-start(f32[30,8,128]{2,1,0:T(8,128)S(1)} %get-tuple-element.19), channel_id=1, source_target_pairs={{0,28},{4,0},{8,4},{12,8},{16,12},{20,16},{24,20},{28,24},{1,29},{... | collective-permute-start | bytes 368648 | tf_op jit(solution)/shard_map/ppermute | solution.py:422
  6.8 2.5 %collective-permute-done.hl_ref = f32[30,8,128]{2,1,0:T(8,128)S(1)} collective-permute-done((f32[30,8,128]{2,1,0:T(8,128)S(1)}, f32[30,8,128]{2,1,0:T(8,128)S(1)}, u32[]{:S(2)}, u32[]{:S(2)}) %collective-permute-start) | collective-permute-done | bytes 122912 | tf_op jit(solution)/shard_map/ppermute | solution.py:421
  9.4 9.0 %move.1 = (f32[3840,128]{1,0:T(8,128)S(1)}, f32[15,2,32,128]{3,2,1,0:T(8,128)S(1)}, f32[15,2,32,128]{3,2,1,0:T(8,128)S(1)}) custom-call(f32[15]{0:T(128)S(1)} %copy-done.10, f32[3840,128]{1,0:T(8,128)S(1)} %bitcast.9, f32[30,8,128]{2,1,0:T(8,128)S(1)} %collective-permute-done.hl_ref, f32[30,8,128]{2,1,0:T(8,128)S(1)} %collective-permute-done.1.hr_ref, ...), custom_call_target="tpu_custom_call" | custom-call | tf_op jit(solution)/shard_map/move/pallas_call | solution.py:427
  18.4 1.6 %collective-permute-start.2 = (f32[15,2,32,128]{3,2,1,0:T(8,128)S(1)}, f32[15,2,32,128]{3,2,1,0:T(8,128)S(1)}, u32[]{:S(2)}, u32[]{:S(2)}) collective-permute-start(f32[15,2,32,128]{3,2,1,0:T(8,128)S(1)} %get-tuple-element.21), channel_id=1, source_target_pairs={{0,32},{32,64},{64,96},{96,0},{1,33},{33,65},{65,97},{97,1},{2,34}... | collective-permute-start | bytes 1474568 | tf_op jit(solution)/shard_map/ppermute | solution.py:455
  20.1 1.7 %collective-permute-start.3 = (f32[15,2,32,128]{3,2,1,0:T(8,128)S(1)}, f32[15,2,32,128]{3,2,1,0:T(8,128)S(1)}, u32[]{:S(2)}, u32[]{:S(2)}) collective-permute-start(f32[15,2,32,128]{3,2,1,0:T(8,128)S(1)} %get-tuple-element.22), channel_id=1, source_target_pairs={{0,96},{32,0},{64,32},{96,64},{1,97},{33,1},{65,33},{97,65},{2,98}... | collective-permute-start | bytes 1474568 | tf_op jit(solution)/shard_map/ppermute | solution.py:456
  21.7 5.3 %prep.1 = (f32[56,128]{1,0:T(8,128)S(1)}, bf16[1024,1024]{1,0:T(8,128)(2,1)S(1)}) custom-call(f32[1,127]{1,0:T(1,128)S(1)} %bitcast.13, f32[1,128]{1,0:T(1,128)S(1)} %bitcast.14, f32[15,128]{1,0:T(8,128)S(1)} %copy-done.8, s32[1,1024]{1,0:T(1,128)S(1)} %bitcast.12), custom_call_target="tpu_custom_call" | custom-call | tf_op jit(solution)/shard_map/prep/pallas_call | solution.py:400
  27.0 6.2 %collective-permute-done.2.top_ref = f32[15,2,32,128]{3,2,1,0:T(8,128)S(1)} collective-permute-done((f32[15,2,32,128]{3,2,1,0:T(8,128)S(1)}, f32[15,2,32,128]{3,2,1,0:T(8,128)S(1)}, u32[]{:S(2)}, u32[]{:S(2)}) %collective-permute-start.2) | collective-permute-done | bytes 491552 | tf_op jit(solution)/shard_map/ppermute | solution.py:455
  33.2 8.1 %meet.1 = (f32[3840,128]{1,0:T(8,128)S(1)}, f32[15,4,8,128]{3,2,1,0:T(8,128)}, f32[15,4,8,128]{3,2,1,0:T(8,128)S(1)}, f32[15,4,8,128]{3,2,1,0:T(8,128)S(1)}, f32[128,128]{1,0:T(8,128)S(1)}) custom-call(f32[15]{0:T(128)S(1)} %copy-done.10, f32[56,128]{1,0:T(8,128)S(1)} %get-tuple-element.17.c_ref, f32[3840,128]{1,0:T(8,128)S(1)} %get-tuple-element.20.u_ref, ...), custom_call_target="tpu_custom_call" | custom-call | tf_op jit(solution)/shard_map/meet/pallas_call | solution.py:459
  41.2 1.3 %copy-done.3 = f32[3840,128]{1,0:T(8,128)} copy-done((f32[3840,128]{1,0:T(8,128)}, f32[3840,128]{1,0:T(8,128)S(1)}, u32[]{:S(2)}) %copy-start.3) | copy-done | bytes 1966104
  42.5 2.8 %collective-permute-start.9 = (f32[128,128]{1,0:T(8,128)S(1)}, f32[128,128]{1,0:T(8,128)S(1)}, u32[]{:S(2)}, u32[]{:S(2)}) collective-permute-start(f32[128,128]{1,0:T(8,128)S(1)} %get-tuple-element.28), channel_id=1, source_target_pairs={{0,3},{1,0},{2,1},{3,2},{4,7},{5,4},{6,5},{7,6},{8,11},{9,8},{10,9... | collective-permute-start | bytes 196616 | tf_op jit(solution)/shard_map/ppermute | solution.py:480
  45.3 0.8 collective-permute-start.8
  46.1 0.9 %collective-permute-start.7 = (f32[128,128]{1,0:T(8,128)S(1)}, f32[128,128]{1,0:T(8,128)S(1)}, u32[]{:S(2)}, u32[]{:S(2)}) collective-permute-start(f32[128,128]{1,0:T(8,128)S(1)} %get-tuple-element.28), channel_id=1, source_target_pairs={{0,1},{1,2},{2,3},{3,0},{4,5},{5,6},{6,7},{7,4},{8,9},{9,10},{10,1... | collective-permute-start | bytes 196616 | tf_op jit(solution)/shard_map/ppermute | solution.py:480
  47.0 1.8 %collective-permute-start.4 = (f32[15,4,8,128]{3,2,1,0:T(8,128)}, f32[15,4,8,128]{3,2,1,0:T(8,128)S(1)}, u32[]{:S(2)}, u32[]{:S(2)}) collective-permute-start(f32[15,4,8,128]{3,2,1,0:T(8,128)} %get-tuple-element.25), channel_id=1, source_target_pairs={{0,1},{1,2},{2,3},{3,0},{4,5},{5,6},{6,7},{7,4},{8,9},{9,10},{10,1... | collective-permute-start | bytes 737288 | tf_op jit(solution)/shard_map/ppermute | solution.py:482
  48.8 2.0 %collective-permute-start.5 = (f32[15,4,8,128]{3,2,1,0:T(8,128)S(1)}, f32[15,4,8,128]{3,2,1,0:T(8,128)S(1)}, u32[]{:S(2)}, u32[]{:S(2)}) collective-permute-start(f32[15,4,8,128]{3,2,1,0:T(8,128)S(1)} %get-tuple-element.26), channel_id=1, source_target_pairs={{0,2},{1,3},{2,0},{3,1},{4,6},{5,7},{6,4},{7,5},{8,10},{9,11},{10,... | collective-permute-start | bytes 737288 | tf_op jit(solution)/shard_map/ppermute | solution.py:482
  51.7 1.0 %collective-permute-done.7 = f32[128,128]{1,0:T(8,128)S(1)} collective-permute-done((f32[128,128]{1,0:T(8,128)S(1)}, f32[128,128]{1,0:T(8,128)S(1)}, u32[]{:S(2)}, u32[]{:S(2)}) %collective-permute-start.7) | collective-permute-done | bytes 65568 | tf_op jit(solution)/shard_map/ppermute | solution.py:480
  52.8 14.5 %all_to_all.10 = f32[32,4,128]{2,1,0:T(4,128)S(1)} all-to-all(f32[32,4,128]{2,1,0:T(4,128)S(1)} %bitcast.15), channel_id=1, replica_groups=mesh['ex'=4,'ey'=8,'lb'=4] {'ex','ey'}, dimensions={0} | all-to-all | bytes 131072 | tf_op jit(solution)/shard_map/all_to_all | solution.py:486
  68.0 3.8 %all-to-all-start.1 = ((f32[32,4,128]{2,1,0:T(4,128)}), f32[32,4,128]{2,1,0:T(4,128)S(1)}, u32[]{:S(2)}, u32[]{:S(2)}) async-start(f32[32,4,128]{2,1,0:T(4,128)} %broadcast_in_dim.2), calls=%async_computation.1 | async-start | bytes 131072 | tf_op jit(solution)/shard_map/all_to_all | solution.py:488
  71.9 1.5 %copy-done.4 = f32[3840,128]{1,0:T(8,128)S(1)} copy-done((f32[3840,128]{1,0:T(8,128)S(1)}, f32[3840,128]{1,0:T(8,128)}, u32[]{:S(2)}) %copy-start.4) | copy-done | bytes 1966104
  73.4 3.9 %solve.1.p_ref = f32[15,32,8,128]{3,2,1,0:T(8,128)S(1)} custom-call(f32[56,128]{1,0:T(8,128)S(1)} %get-tuple-element.17.c_ref, f32[15,32,8,128]{3,2,1,0:T(8,128)S(1)} %bitcast.10, f32[15,4,8,128]{3,2,1,0:T(8,128)S(1)} %collective-permute-done.4.r1_ref, f32[15,4,8,128]{3,2,1,0:T(8,128)S(1)} %collective-permute-done.5.r2_ref, ...), custom_call_target="tpu_custom_call" | custom-call | tf_op jit(solution)/shard_map/solve/pallas_call | solution.py:492
  77.3 1.3 %copy-done = f32[15,32,8,128]{3,2,1,0:T(8,128)} copy-done((f32[15,32,8,128]{3,2,1,0:T(8,128)}, f32[15,32,8,128]{3,2,1,0:T(8,128)S(1)}, u32[]{:S(2)}) %copy-start) | copy-done | bytes 1966104
  79.3 1.5 %copy-done.1 = f32[15,32,8,128]{3,2,1,0:T(8,128)S(1)} copy-done((f32[15,32,8,128]{3,2,1,0:T(8,128)S(1)}, f32[15,32,8,128]{3,2,1,0:T(8,128)}, u32[]{:S(2)}) %copy-start.1) | copy-done | bytes 1966104
  80.9 2.5 %share.1 = f32[15,32,8,128]{3,2,1,0:T(8,128)} custom-call(f32[15,32,8,128]{3,2,1,0:T(8,128)S(1)} %copy-done.1, f32[128,128]{1,0:T(8,128)S(1)} %bitcast.11, bf16[1024,1024]{1,0:T(8,128)(2,1)S(1)} %get-tuple-element.23.ot_ref), custom_call_target="tpu_custom_call" | custom-call | tf_op jit(solution)/shard_map/share/pallas_call | solution.py:503
  (34 shorter events, 2.5 us)
Async XLA Ops:
  0.0 9.3 %copy-start.10 = (f32[15]{0:T(128)S(1)}, f32[15]{0:T(128)}, u32[]{:S(2)}) copy-start(f32[15]{0:T(128)} %d_ref.3) | copy-start | bytes 184
  0.0 1.6 %copy-start.2 = (f32[15,32,8,128]{3,2,1,0:T(8,128)S(1)}, f32[15,32,8,128]{3,2,1,0:T(8,128)}, u32[]{:S(2)}) copy-start(f32[15,32,8,128]{3,2,1,0:T(8,128)} %param.9) | copy-start | bytes 5898244
  1.6 7.8 %copy-start.5 = (bf16[256,512]{1,0:T(8,128)(2,1)S(1)}, bf16[256,512]{1,0:T(8,128)(2,1)}, u32[]{:S(2)}) copy-start(bf16[256,512]{1,0:T(8,128)(2,1)} %constant.7.clone.wl_ref) | copy-start | bytes 786436
  1.6 7.8 %copy-start.6 = (bf16[256,512]{1,0:T(8,128)(2,1)S(1)}, bf16[256,512]{1,0:T(8,128)(2,1)}, u32[]{:S(2)}) copy-start(bf16[256,512]{1,0:T(8,128)(2,1)} %constant.6.clone.wh_ref) | copy-start | bytes 786436
  1.6 20.2 %copy-start.8 = (f32[15,128]{1,0:T(8,128)S(1)}, f32[15,128]{1,0:T(8,128)}, u32[]{:S(2)}) copy-start(f32[15,128]{1,0:T(8,128)} %g_ref.1) | copy-start | bytes 23044
  1.6 20.2 %copy-start.9 = (s32[1,1,1024]{2,1,0:T(1,128)S(1)}, s32[1,1,1024]{2,1,0:T(1,128)}, u32[]{:S(2)}) copy-start(s32[1,1,1024]{2,1,0:T(1,128)} %param.14) | copy-start | bytes 12292
  1.6 20.2 %copy-start.11 = (f32[127]{0:T(128)S(1)}, f32[127]{0:T(128)}, u32[]{:S(2)}) copy-start(f32[127]{0:T(128)} %param.11) | copy-start | bytes 1528
  1.6 20.1 %copy-start.12 = (f32[128]{0:T(128)S(1)}, f32[128]{0:T(128)}, u32[]{:S(2)}) copy-start(f32[128]{0:T(128)} %param.12) | copy-start | bytes 1540
  1.6 31.6 %copy-start.7 = (s32[8,128]{1,0:T(8,128)S(1)}, s32[8,128]{1,0:T(8,128)}, u32[]{:S(2)}) copy-start(s32[8,128]{1,0:T(8,128)} %class_ref.3) | copy-start | bytes 12292
  3.2 6.1 %collective-permute-start = (f32[30,8,128]{2,1,0:T(8,128)S(1)}, f32[30,8,128]{2,1,0:T(8,128)S(1)}, u32[]{:S(2)}, u32[]{:S(2)}) collective-permute-start(f32[30,8,128]{2,1,0:T(8,128)S(1)} %get-tuple-element.18), channel_id=1, source_target_pairs={{0,4},{4,8},{8,12},{12,16},{16,20},{20,24},{24,28},{28,0},{1,5},{5... | collective-permute-start | bytes 368648 | tf_op jit(solution)/shard_map/ppermute | solution.py:421
  3.2 6.1 %collective-permute-start.1 = (f32[30,8,128]{2,1,0:T(8,128)S(1)}, f32[30,8,128]{2,1,0:T(8,128)S(1)}, u32[]{:S(2)}, u32[]{:S(2)}) collective-permute-start(f32[30,8,128]{2,1,0:T(8,128)S(1)} %get-tuple-element.19), channel_id=1, source_target_pairs={{0,28},{4,0},{8,4},{12,8},{16,12},{20,16},{24,20},{28,24},{1,29},{... | collective-permute-start | bytes 368648 | tf_op jit(solution)/shard_map/ppermute | solution.py:422
  18.4 14.8 %collective-permute-start.2 = (f32[15,2,32,128]{3,2,1,0:T(8,128)S(1)}, f32[15,2,32,128]{3,2,1,0:T(8,128)S(1)}, u32[]{:S(2)}, u32[]{:S(2)}) collective-permute-start(f32[15,2,32,128]{3,2,1,0:T(8,128)S(1)} %get-tuple-element.21), channel_id=1, source_target_pairs={{0,32},{32,64},{64,96},{96,0},{1,33},{33,65},{65,97},{97,1},{2,34}... | collective-permute-start | bytes 1474568 | tf_op jit(solution)/shard_map/ppermute | solution.py:455
  20.1 13.1 %collective-permute-start.3 = (f32[15,2,32,128]{3,2,1,0:T(8,128)S(1)}, f32[15,2,32,128]{3,2,1,0:T(8,128)S(1)}, u32[]{:S(2)}, u32[]{:S(2)}) collective-permute-start(f32[15,2,32,128]{3,2,1,0:T(8,128)S(1)} %get-tuple-element.22), channel_id=1, source_target_pairs={{0,96},{32,0},{64,32},{96,64},{1,97},{33,1},{65,33},{97,65},{2,98}... | collective-permute-start | bytes 1474568 | tf_op jit(solution)/shard_map/ppermute | solution.py:456
  41.2 1.3 %copy-start.3 = (f32[3840,128]{1,0:T(8,128)}, f32[3840,128]{1,0:T(8,128)S(1)}, u32[]{:S(2)}) copy-start(f32[3840,128]{1,0:T(8,128)S(1)} %get-tuple-element.24) | copy-start | bytes 5898244
  42.5 8.3 %collective-permute-start.9 = (f32[128,128]{1,0:T(8,128)S(1)}, f32[128,128]{1,0:T(8,128)S(1)}, u32[]{:S(2)}, u32[]{:S(2)}) collective-permute-start(f32[128,128]{1,0:T(8,128)S(1)} %get-tuple-element.28), channel_id=1, source_target_pairs={{0,3},{1,0},{2,1},{3,2},{4,7},{5,4},{6,5},{7,6},{8,11},{9,8},{10,9... | collective-permute-start | bytes 196616 | tf_op jit(solution)/shard_map/ppermute | solution.py:480
  45.3 6.5 %collective-permute-start.8 = (f32[128,128]{1,0:T(8,128)S(1)}, f32[128,128]{1,0:T(8,128)S(1)}, u32[]{:S(2)}, u32[]{:S(2)}) collective-permute-start(f32[128,128]{1,0:T(8,128)S(1)} %get-tuple-element.28), channel_id=1, source_target_pairs={{0,2},{1,3},{2,0},{3,1},{4,6},{5,7},{6,4},{7,5},{8,10},{9,11},{10,... | collective-permute-start | bytes 196616 | tf_op jit(solution)/shard_map/ppermute | solution.py:480
  46.1 6.7 %collective-permute-start.7 = (f32[128,128]{1,0:T(8,128)S(1)}, f32[128,128]{1,0:T(8,128)S(1)}, u32[]{:S(2)}, u32[]{:S(2)}) collective-permute-start(f32[128,128]{1,0:T(8,128)S(1)} %get-tuple-element.28), channel_id=1, source_target_pairs={{0,1},{1,2},{2,3},{3,0},{4,5},{5,6},{6,7},{7,4},{8,9},{9,10},{10,1... | collective-permute-start | bytes 196616 | tf_op jit(solution)/shard_map/ppermute | solution.py:480
  47.0 24.8 %collective-permute-start.4 = (f32[15,4,8,128]{3,2,1,0:T(8,128)}, f32[15,4,8,128]{3,2,1,0:T(8,128)S(1)}, u32[]{:S(2)}, u32[]{:S(2)}) collective-permute-start(f32[15,4,8,128]{3,2,1,0:T(8,128)} %get-tuple-element.25), channel_id=1, source_target_pairs={{0,1},{1,2},{2,3},{3,0},{4,5},{5,6},{6,7},{7,4},{8,9},{9,10},{10,1... | collective-permute-start | bytes 737288 | tf_op jit(solution)/shard_map/ppermute | solution.py:482
  48.8 23.1 %collective-permute-start.5 = (f32[15,4,8,128]{3,2,1,0:T(8,128)S(1)}, f32[15,4,8,128]{3,2,1,0:T(8,128)S(1)}, u32[]{:S(2)}, u32[]{:S(2)}) collective-permute-start(f32[15,4,8,128]{3,2,1,0:T(8,128)S(1)} %get-tuple-element.26), channel_id=1, source_target_pairs={{0,2},{1,3},{2,0},{3,1},{4,6},{5,7},{6,4},{7,5},{8,10},{9,11},{10,... | collective-permute-start | bytes 737288 | tf_op jit(solution)/shard_map/ppermute | solution.py:482
  50.8 21.1 %collective-permute-start.6 = (f32[15,4,8,128]{3,2,1,0:T(8,128)S(1)}, f32[15,4,8,128]{3,2,1,0:T(8,128)S(1)}, u32[]{:S(2)}, u32[]{:S(2)}) collective-permute-start(f32[15,4,8,128]{3,2,1,0:T(8,128)S(1)} %get-tuple-element.27), channel_id=1, source_target_pairs={{0,3},{1,0},{2,1},{3,2},{4,7},{5,4},{6,5},{7,6},{8,11},{9,8},{10,9... | collective-permute-start | bytes 737288 | tf_op jit(solution)/shard_map/ppermute | solution.py:482
  68.0 11.4 %all-to-all-start.1 = ((f32[32,4,128]{2,1,0:T(4,128)}), f32[32,4,128]{2,1,0:T(4,128)S(1)}, u32[]{:S(2)}, u32[]{:S(2)}) async-start(f32[32,4,128]{2,1,0:T(4,128)} %broadcast_in_dim.2), calls=%async_computation.1 | async-start | bytes 131072 | tf_op jit(solution)/shard_map/all_to_all | solution.py:488
  71.8 1.5 %copy-start.4 = (f32[3840,128]{1,0:T(8,128)S(1)}, f32[3840,128]{1,0:T(8,128)}, u32[]{:S(2)}) copy-start(f32[3840,128]{1,0:T(8,128)} %copy-done.3) | copy-start | bytes 5898244
  77.3 1.3 %copy-start = (f32[15,32,8,128]{3,2,1,0:T(8,128)}, f32[15,32,8,128]{3,2,1,0:T(8,128)S(1)}, u32[]{:S(2)}) copy-start(f32[15,32,8,128]{3,2,1,0:T(8,128)S(1)} %solve.1.p_ref) | copy-start | bytes 5898244
  79.3 1.5 %copy-start.1 = (f32[15,32,8,128]{3,2,1,0:T(8,128)S(1)}, f32[15,32,8,128]{3,2,1,0:T(8,128)}, u32[]{:S(2)}) copy-start(f32[15,32,8,128]{3,2,1,0:T(8,128)} %copy-done) | copy-start | bytes 5898244

commit v2 on v1

--- a/solution.py
+++ b/solution.py
@@ -18,6 +18,7 @@
 LEVELS = 128
 TILES = 32
 PER = SLAB * ROWS
+GROUP = 3
 
 
 def second_table():
@@ -107,19 +108,31 @@
     inv = 1.0 / p
     eps = kap * inv
     gam = pltpu.roll(eps, 1, 1)
-    fwd, bwd = [gam], [eps]
-    for t in (1, 2, 4, 8, 16, 32):
-        fwd.append(fwd[-1] * pltpu.roll(fwd[-1], t, 1))
-        bwd.append(bwd[-1] * pltpu.roll(bwd[-1], LANES - t, 1))
+    def levels(first, back):
+        def turn(value, t):
+            return pltpu.roll(value, LANES - t if back else t, 1)
+
+        out, one = [], first
+        for t in (1, 4, 16):
+            two = one * turn(one, t)
+            out.append((t, one, two, two * turn(one, 2 * t)))
+            one = two * turn(two, 2 * t)
+        return out, one, turn
+
+    def sweep(value, plan):
+        out, last, turn = plan
+        for t, one, two, three in out:
+            value = (value + one * turn(value, t)) + (
+                two * turn(value, 2 * t) + three * turn(value, 3 * t)
+            )
+        return value + last * turn(value, 64)
+
+    fwd, bwd = levels(gam, False), levels(eps, True)
     rhs = jnp.where(row < 3, cutm, jnp.where(row < 6, after, 1.0))
     x = rhs
     stack = []
     for k in range(4):
-        for s in range(7):
-            x = x + fwd[s] * pltpu.roll(x, 1 << s, 1)
-        x = x * inv
-        for s in range(7):
-            x = x + bwd[s] * pltpu.roll(x, LANES - (1 << s), 1)
+        x = sweep(sweep(x, fwd) * inv, bwd)
         sols[k] = x
         stack.append(x)
     buf[...] = jnp.zeros(buf.shape, F32)
@@ -177,10 +190,12 @@
         ).astype(BF16)
 
 
-def pack_kernel(x_ref, l_ref, r_ref):
-    lane = lax.broadcasted_iota(jnp.int32, (2, ROWS, LANES), 2) // 8
-    left = jnp.zeros((2, ROWS, LANES), F32)
-    right = jnp.zeros((2, ROWS, LANES), F32)
+def pack_kernel(x_ref, class_ref, span_ref, l_ref, r_ref, info_ref):
+    info_ref[0:8, :] = class_ref[...]
+    info_ref[8:16, :] = span_ref[...]
+    lane = lax.broadcasted_iota(jnp.int32, (2 * GROUP, ROWS, LANES), 2) // 8
+    left = jnp.zeros((2 * GROUP, ROWS, LANES), F32)
+    right = jnp.zeros((2 * GROUP, ROWS, LANES), F32)
     for q in range(16):
         turned = x_ref[:, q]
         if q:
@@ -189,6 +204,17 @@
         right = jnp.where(lane == (q - 1) % 16, turned, right)
     l_ref[...] = left
     r_ref[...] = right
+
+
+def class_rows(info_ref, r):
+    kind = lax.broadcasted_iota(jnp.int32, (8, LANES), 0) - 4
+    return jnp.where(jnp.broadcast_to(info_ref[r : r + 1, :], (8, LANES)) == kind, 1.0, 0.0)
+
+
+def slot_block(info_ref, r):
+    place = lax.broadcasted_iota(jnp.int32, (LANES, 1024), 0) + LANES * r
+    spots = jnp.concatenate([info_ref[8 + i : 9 + i, :] for i in range(8)], axis=1)
+    return jnp.where(place == spots, 1.0, 0.0).astype(BF16)
 
 
 def along_x(rows):
@@ -207,109 +233,147 @@
     return [0.5 * rows[0], rows[1], rows[2], middle, middle, rows[5], rows[6], 0.5 * rows[7]]
 
 
-def move_kernel(d_ref, x_ref, hl_ref, hr_ref, wh_ref, wl_ref, u_ref, down_ref, up_ref, xh):
-    d = d_ref[pl.program_id(0)]
-    lane = lax.broadcasted_iota(jnp.int32, (2, ROWS, LANES), 2)
+def move_kernel(
+    d_ref, c_ref, x_ref, hl_ref, hr_ref, wh_ref, wl_ref, own_ref, top_ref, bot_ref,
+    u_ref, down_ref, up_ref, ch, xh,
+):
+    base = pl.program_id(0) * GROUP
+
+    @pl.when(base == 0)
+    def _():
+        ch[...] = jnp.zeros(ch.shape, F32)
+
+    vh, vl = split2(c_ref[8:16, 0:SLAB])
+    left = jnp.concatenate([vh, vh, vl], axis=1)
+    push = c_ref[28:36, :]
+    field = lax.broadcasted_iota(jnp.int32, (8, LANES), 1)
+    keep = [class_rows(own_ref, r) for r in range(ROWS)]
+    keep_bot = [class_rows(bot_ref, r) for r in range(5)]
+    keep_top = [class_rows(top_ref, r) for r in range(3, 8)]
+    lane = lax.broadcasted_iota(jnp.int32, (2 * GROUP, ROWS, LANES), 2)
     for q in range(16):
         hl, hr = hl_ref[...], hr_ref[...]
         if q:
             hl = pltpu.roll(hl, LANES - 8 * q, 2)
             hr = pltpu.roll(hr, LANES - 8 * q, 2)
         both = jnp.where(lane >= LANES - 8, hl, jnp.where(lane < 8, hr, 0.0))
-        xh[8 * q : 8 * q + 8, :] = both[0]
-        xh[128 + 8 * q : 136 + 8 * q, :] = both[1]
-    rows = [x_ref[pl.ds(r, SLAB, stride=ROWS), :] for r in range(ROWS)]
-    halo = [xh[pl.ds(r, SLAB, stride=ROWS), :] for r in range(ROWS)]
+        for p in range(2 * GROUP):
+            xh[128 * p + 8 * q : 128 * p + 8 * q + 8, :] = both[p]
+    order = [(g, r) for g in range(GROUP) for r in range(ROWS)]
+    rows = [x_ref[pl.ds(PER * g + r, SLAB, stride=ROWS), :] for g, r in order]
+    halo = [xh[pl.ds(PER * g + r, SLAB, stride=ROWS), :] for g, r in order]
     main = jnp.concatenate(
         [jnp.concatenate(rows, axis=0), jnp.concatenate(halo, axis=0)], axis=1
     )
     high, low = split2(main)
-    wh = wh_ref[...]
-    t = dot(high, wh) + dot(low, wh) + dot(high, wl_ref[...])
-    t1, t2, t3, t4 = [
-        [t[SLAB * r : SLAB * r + SLAB, LANES * i : LANES * i + LANES] for r in range(ROWS)]
-        for i in range(4)
-    ]
-    w1 = [g + s for g, s in zip(along_x(t1), t2)]
-    w2 = [g + s for g, s in zip(along_x(t3), t4)]
-    e1 = [d * v for v in half_joined(w1)]
-    r1 = [s + v for s, v in zip(t1, e1)]
-    r2 = [s + d * v for s, v in zip(t2, half_joined(w2))]
-    w3 = [g + s for g, s in zip(along_x(r1), r2)]
-    out = [u + v + d * w for u, v, w in zip(rows, e1, half_joined(w3))]
-    half = 0.5 * d
-    quarter = half * half
-    out[0] = out[0] + quarter * (float(G[3, 3]) * w1[0] + w2[0])
-    out[7] = out[7] + quarter * (float(G[0, 0]) * w1[7] + w2[7])
-    for r in range(ROWS):
-        u_ref[SLAB * r : SLAB * r + SLAB, :] = out[r]
-    down_ref[0, 0] = w1[7]
-    down_ref[0, 1] = w3[7] + half * w2[7]
-    up_ref[0, 0] = w1[0]
-    up_ref[0, 1] = w3[0] + half * w2[0]
+    count = PER * GROUP
+    twice = dot(jnp.concatenate([high, low], axis=0), wh_ref[...])
+    t = twice[:count] + twice[count:] + dot(high, wl_ref[...])
+    for g in range(GROUP):
+        d = d_ref[base + g]
+        own = rows[ROWS * g : ROWS * g + ROWS]
+        t1, t2, t3, t4 = [
+            [
+                t[PER * g + SLAB * r : PER * g + SLAB * r + SLAB, LANES * i : LANES * i + LANES]
+                for r in range(ROWS)
+            ]
+            for i in range(4)
+        ]
+        w1 = [a + b for a, b in zip(along_x(t1), t2)]
+        w2 = [a + b for a, b in zip(along_x(t3), t4)]
+        e1 = [d * v for v in half_joined(w1)]
+        r1 = [a + b for a, b in zip(t1, e1)]
+        r2 = [a + d * b for a, b in zip(t2, half_joined(w2))]
+        w3 = [a + b for a, b in zip(along_x(r1), r2)]
+        out = [u + v + d * w for u, v, w in zip(own, e1, half_joined(w3))]
+        half = 0.5 * d
+        quarter = half * half
+        out[0] = out[0] + quarter * (float(G[3, 3]) * w1[0] + w2[0])
+        out[7] = out[7] + quarter * (float(G[0, 0]) * w1[7] + w2[7])
+        for r in range(ROWS):
+            u_ref[PER * g + SLAB * r : PER * g + SLAB * r + SLAB, :] = out[r]
+        down_ref[g, 0] = w1[7]
+        down_ref[g, 1] = w3[7] + half * w2[7]
+        up_ref[g, 0] = w1[0]
+        up_ref[g, 1] = w3[0] + half * w2[0]
+        edges = [w1[7], w3[7] + half * w2[7], w1[0], w3[0] + half * w2[0]]
+        uh, ul = split2(jnp.concatenate(out + edges, axis=1))
+        res = dot(left, jnp.concatenate([uh, ul, uh], axis=0))
+        extra = jnp.sum(jnp.where(field == base + g, push, 0.0), axis=1, keepdims=True)
+        pieces = [res[:, LANES * i : LANES * i + LANES] for i in range(12)]
+        wd, zd, wu, zu = pieces[8:]
+        shares = [(pieces[r] + extra) * keep[r] for r in range(ROWS)]
+        cross = quarter * float(G[3, 0])
+        shares += [
+            ((half + quarter * float(G[0, 0])) * wd + half * zd) * keep_bot[0],
+            (2.0 * quarter * float(G[1, 0])) * wd * keep_bot[1],
+            (2.0 * quarter * float(G[2, 0])) * wd * keep_bot[2],
+            cross * wd * keep_bot[3],
+            cross * wd * keep_bot[4],
+            cross * wu * keep_top[0],
+            cross * wu * keep_top[1],
+            (2.0 * quarter * float(G[1, 3])) * wu * keep_top[2],
+            (2.0 * quarter * float(G[2, 3])) * wu * keep_top[3],
+            ((half + quarter * float(G[3, 3])) * wu + half * zu) * keep_top[4],
+        ]
+        for i, value in enumerate(shares):
+            ch[pl.ds(16 * i + base + g, 1), :] = jnp.sum(value, axis=0, keepdims=True)
+
+
+def slot_kernel(ch_ref, top_ref, bot_ref, ot_ref, slot_ref):
+    ordered = jnp.zeros((48, 1024), F32)
+    for i in range(18):
+        part = jnp.concatenate(split3(ch_ref[16 * i : 16 * i + 16, :]), axis=0)
+        if i < 8:
+            onehot = ot_ref[LANES * i : LANES * i + LANES, :]
+        elif i < 13:
+            onehot = slot_block(bot_ref, i - 8)
+        else:
+            onehot = slot_block(top_ref, i - 10)
+        ordered = ordered + dot(part, onehot)
+    ordered = ordered[0:16] + ordered[16:32] + ordered[32:48]
+    for block in range(8):
+        slot_ref[16 * block : 16 * block + 16, :] = ordered[:, LANES * block : LANES * block + LANES]
 
 
 def meet_kernel(
-    d_ref, c_ref, u_ref, top_ref, bot_ref, class_ref, ot_ref,
-    x_ref, m1_ref, m2_ref, m3_ref, slot_ref, swt, ch,
+    d_ref, c_ref, u_ref, top_ref, bot_ref, x_ref, m1_ref, m2_ref, m3_ref
 ):
-    f = pl.program_id(0)
-    kind = class_ref[...]
-
-    def by_class(values):
-        return jnp.where(
-            kind >= 2,
-            jnp.where(kind == 2, values[2], values[3]),
-            jnp.where(kind == 0, values[0], values[1]),
-        )
-
-    @pl.when(f == 0)
-    def _():
-        for l in range(SLAB):
-            swt[8 * l : 8 * l + 8, :] = by_class([c_ref[12 + k, l] for k in range(4)])
-        ch[...] = jnp.zeros(ch.shape, F32)
-
-    d = d_ref[f]
-    half = 0.5 * d
-    quarter = half * half
-    wt, zt, wb, zb = top_ref[0, 0], top_ref[0, 1], bot_ref[0, 0], bot_ref[0, 1]
-    cross_t = quarter * float(G[3, 0]) * wt
-    cross_b = quarter * float(G[0, 3]) * wb
-    cross = cross_t + cross_b
-    add = [
-        (half + quarter * float(G[0, 0])) * wt + half * zt,
-        (2.0 * quarter * float(G[1, 0])) * wt,
-        (2.0 * quarter * float(G[2, 0])) * wt,
-        cross,
-        cross,
-        (2.0 * quarter * float(G[1, 3])) * wb,
-        (2.0 * quarter * float(G[2, 3])) * wb,
-        (half + quarter * float(G[3, 3])) * wb + half * zb,
-    ]
-    for r in range(ROWS):
-        x_ref[pl.ds(r, SLAB, stride=ROWS), :] = u_ref[SLAB * r : SLAB * r + SLAB, :] + add[r]
-    total = [jnp.zeros((ROWS, LANES), F32)] * 13
-    for l in range(SLAB):
-        x = x_ref[8 * l : 8 * l + 8, :]
-        for v in range(12):
-            total[v] = total[v] + c_ref[v, l] * x
-        total[12] = total[12] + swt[8 * l : 8 * l + 8, :] * x
-    for r, ref in enumerate((m1_ref, m2_ref, m3_ref)):
-        for k in range(4):
-            ref[0, k] = total[4 * r + k] + c_ref[20 + 4 * r + k, f]
-    ch[pl.ds(pl.multiple_of(8 * f, 8), 8), :] = total[12] + by_class(
-        [c_ref[32 + k, f] for k in range(4)]
-    )
-
-    @pl.when(f == FIELDS - 1)
-    def _():
-        ordered = jnp.zeros((48, 1024), F32)
-        for a in range(ROWS):
-            part = jnp.concatenate(split3(ch[pl.ds(a, 16, stride=ROWS), :]), axis=0)
-            ordered = ordered + dot(part, ot_ref[LANES * a : LANES * a + LANES, :])
-        ordered = ordered[0:16] + ordered[16:32] + ordered[32:48]
-        for block in range(8):
-            slot_ref[16 * block : 16 * block + 16, :] = ordered[:, LANES * block : LANES * block + LANES]
+    base = pl.program_id(0) * GROUP
+
+    vh, vl = split2(c_ref[0:16, 0:SLAB])
+    left = jnp.concatenate([vh, vh, vl], axis=1)
+    push = c_ref[20:36, :]
+    lane = lax.broadcasted_iota(jnp.int32, (16, LANES), 1)
+    for g in range(GROUP):
+        d = d_ref[base + g]
+        half = 0.5 * d
+        quarter = half * half
+        wt, zt, wb, zb = top_ref[g, 0], top_ref[g, 1], bot_ref[g, 0], bot_ref[g, 1]
+        cross = quarter * float(G[3, 0]) * wt + quarter * float(G[0, 3]) * wb
+        add = [
+            (half + quarter * float(G[0, 0])) * wt + half * zt,
+            (2.0 * quarter * float(G[1, 0])) * wt,
+            (2.0 * quarter * float(G[2, 0])) * wt,
+            cross,
+            cross,
+            (2.0 * quarter * float(G[1, 3])) * wb,
+            (2.0 * quarter * float(G[2, 3])) * wb,
+            (half + quarter * float(G[3, 3])) * wb + half * zb,
+        ]
+        rows = []
+        for r in range(ROWS):
+            at = PER * g + SLAB * r
+            rows.append(u_ref[at : at + SLAB, :] + add[r])
+            x_ref[pl.ds(PER * g + r, SLAB, stride=ROWS), :] = rows[r]
+        uh, ul = split2(jnp.concatenate(rows, axis=1))
+        res = dot(left, jnp.concatenate([uh, ul, uh], axis=0))
+        extra = jnp.sum(jnp.where(lane == base + g, push, 0.0), axis=1, keepdims=True)
+        res = res + extra
+        for r in range(ROWS):
+            here = res[:, LANES * r : LANES * r + LANES]
+            for n, ref in enumerate((m1_ref, m2_ref, m3_ref)):
+                ref[pl.ds(32 * g + r, 4, stride=ROWS), :] = here[4 * n : 4 * n + 4]
 
 
 def solve_kernel(c_ref, x_ref, r1_ref, r2_ref, r3_ref, class_ref, o_ref, z):
@@ -354,13 +418,14 @@
         firsts.append(run)
 
 
-def share_kernel(p_ref, tot_ref, ot_ref, o_ref, sh):
+def share_kernel(p_ref, ot_ref, a_ref, b_ref, c_ref, d_ref, o_ref, sh):
     group = p_ref.shape[0]
     step = pl.program_id(0)
 
     @pl.when(step == 0)
     def _():
-        whole = jnp.concatenate([tot_ref[16 * b : 16 * b + 16, :] for b in range(8)], axis=1)
+        whole = (a_ref[...] + b_ref[...]) + (c_ref[...] + d_ref[...])
+        whole = jnp.concatenate([whole[16 * b : 16 * b + 16, :] for b in range(8)], axis=1)
         whole = jnp.concatenate(split3(whole), axis=0)
         for a in range(ROWS):
             back = dot(whole, ot_ref[LANES * a : LANES * a + LANES, :], (((1,), (1,)), ((), ())))
@@ -386,7 +451,16 @@
     return jax.ShapeDtypeStruct(shape, dtype)
 
 
-LIMIT = pltpu.CompilerParams(vmem_limit_bytes=40 * 1024 * 1024)
+LIMIT = pltpu.CompilerParams(vmem_limit_bytes=24 * 1024 * 1024)
+
+
+def stay(x):
+    return pltpu.with_memory_space_constraint(x, pltpu.HBM)
+
+
+def ring(value, axis, step):
+    count = lax.axis_size(axis)
+    return [lax.ppermute(value, axis, shift(axis, r)) for r in range(step, count, step)]
 
 
 def shift(axis, step):
@@ -409,83 +483,113 @@
         name="prep",
     )(mixing.reshape(1, -1), relaxation.reshape(1, -1), forcing, span_map.reshape(1, -1))
 
-    left, right = pl.pallas_call(
+    steps = FIELDS // GROUP
+    left, right, info = pl.pallas_call(
         pack_kernel,
-        grid=(FIELDS,),
-        in_specs=[pl.BlockSpec((2, 16, ROWS, LANES), lambda f: (f, 0, 0, 0))],
-        out_specs=[pl.BlockSpec((2, ROWS, LANES), lambda f: (f, 0, 0))] * 2,
-        out_shape=(shaped(30, ROWS, LANES), shaped(30, ROWS, LANES)),
+        grid=(steps,),
+        in_specs=[
+            pl.BlockSpec((2 * GROUP, 16, ROWS, LANES), lambda f: (f, 0, 0, 0)),
+            whole_spec((ROWS, LANES)),
+            whole_spec((ROWS, LANES)),
+        ],
+        out_specs=[pl.BlockSpec((2 * GROUP, ROWS, LANES), lambda f: (f, 0, 0))] * 2
+        + [whole_spec((16, LANES))],
+        out_shape=(
+            shaped(30, ROWS, LANES),
+            shaped(30, ROWS, LANES),
+            shaped(16, LANES, dtype=jnp.int32),
+        ),
         compiler_params=LIMIT,
         name="pack",
-    )(state.reshape(30, 16, ROWS, LANES))
+    )(
+        state.reshape(30, 16, ROWS, LANES),
+        stay(cost_class),
+        stay(span_map.reshape(ROWS, LANES)),
+    )
     from_left = lax.ppermute(right, "ey", shift("ey", 1))
     from_right = lax.ppermute(left, "ey", shift("ey", -1))
+    info_top = lax.ppermute(info, "ex", shift("ex", 1))
+    info_bot = lax.ppermute(info, "ex", shift("ex", -1))
 
     high, low = y_weights()
-    edge = pl.BlockSpec((1, 2, SLAB, LANES), lambda f: (f, 0, 0, 0))
-    block = pl.BlockSpec((PER, LANES), lambda f: (f, 0))
-    part, down, up = pl.pallas_call(
+    edge = pl.BlockSpec((GROUP, 2, SLAB, LANES), lambda f: (f, 0, 0, 0))
+    block = pl.BlockSpec((GROUP * PER, LANES), lambda f: (f, 0))
+    halo = pl.BlockSpec((2 * GROUP, ROWS, LANES), lambda f: (f, 0, 0))
+    table = whole_spec((16, LANES))
+    part, down, up, pieces = pl.pallas_call(
         move_kernel,
-        grid=(FIELDS,),
+        grid=(steps,),
         in_specs=[
             SMEM,
+            whole_spec((56, LANES)),
             block,
-            pl.BlockSpec((2, ROWS, LANES), lambda f: (f, 0, 0)),
-            pl.BlockSpec((2, ROWS, LANES), lambda f: (f, 0, 0)),
+            halo,
+            halo,
             whole_spec((256, 512)),
             whole_spec((256, 512)),
+            table,
+            table,
+            table,
         ],
-        out_specs=[block, edge, edge],
+        out_specs=[block, edge, edge, whole_spec((18 * 16, LANES))],
         out_shape=(
             shaped(FIELDS * PER, LANES),
             shaped(FIELDS, 2, SLAB, LANES),
             shaped(FIELDS, 2, SLAB, LANES),
+            shaped(18 * 16, LANES),
         ),
-        scratch_shapes=[pltpu.VMEM((PER, LANES), F32)],
+        scratch_shapes=[pltpu.VMEM((GROUP * PER, LANES), F32)],
         compiler_params=LIMIT,
         name="move",
     )(
         diffusivity,
+        coef,
         state.reshape(FIELDS * PER, LANES),
         from_left,
         from_right,
-        jnp.asarray(high),
-        jnp.asarray(low),
+        stay(jnp.asarray(high)),
+        stay(jnp.asarray(low)),
+        info,
+        info_top,
+        info_bot,
     )
     top = lax.ppermute(down, "ex", shift("ex", 1))
     bottom = lax.ppermute(up, "ex", shift("ex", -1))
 
-    four = pl.BlockSpec((1, 4, ROWS, LANES), lambda f: (f, 0, 0, 0))
-    moved, m1, m2, m3, slots = pl.pallas_call(
+    slots = pl.pallas_call(
+        slot_kernel,
+        out_shape=shaped(LANES, LANES),
+        compiler_params=LIMIT,
+        name="slot",
+    )(pieces, info_top, info_bot, onehot)
+    slots = sum(ring(slots, "lb", 1), slots)
+    others = ring(slots, "ey", 2)
+
+    four = pl.BlockSpec((GROUP * 32, LANES), lambda f: (f, 0))
+    moved, m1, m2, m3 = pl.pallas_call(
         meet_kernel,
-        grid=(FIELDS,),
-        in_specs=[
-            SMEM, SMEM, block, edge, edge,
-            whole_spec((ROWS, LANES)),
-            whole_spec((1024, 1024)),
-        ],
-        out_specs=[block, four, four, four, whole_spec((LANES, LANES))],
+        grid=(steps,),
+        in_specs=[SMEM, whole_spec((56, LANES)), block, edge, edge],
+        out_specs=[block, four, four, four],
         out_shape=(
             shaped(FIELDS * PER, LANES),
-            shaped(FIELDS, 4, ROWS, LANES),
-            shaped(FIELDS, 4, ROWS, LANES),
-            shaped(FIELDS, 4, ROWS, LANES),
-            shaped(LANES, LANES),
+            shaped(FIELDS * 32, LANES),
+            shaped(FIELDS * 32, LANES),
+            shaped(FIELDS * 32, LANES),
         ),
-        scratch_shapes=[pltpu.VMEM((PER, LANES), F32), pltpu.VMEM((LANES, LANES), F32)],
         compiler_params=LIMIT,
         name="meet",
-    )(diffusivity, coef, part, top, bottom, cost_class, onehot)
-
-    s1, s2, s3 = [lax.ppermute(slots, "lb", shift("lb", r)) for r in (1, 2, 3)]
+    )(diffusivity, coef, part, top, bottom)
+
     g1, g2, g3 = [
-        lax.ppermute(m, "lb", shift("lb", r)) for m, r in ((m1, 1), (m2, 2), (m3, 3))
+        lax.ppermute(m, "lb", shift("lb", r)).reshape(FIELDS, 4, ROWS, LANES)
+        for m, r in ((m1, 1), (m2, 2), (m3, 3))
     ]
-    tiles = ("ex", "ey")
-    summed = (slots + s1 + s2 + s3).reshape(TILES, 4, LANES)
-    mine = lax.all_to_all(summed, tiles, split_axis=0, concat_axis=0, tiled=True)
-    mine = jnp.broadcast_to(jnp.sum(mine, axis=0, keepdims=True), (TILES, 4, LANES))
-    total = lax.all_to_all(mine, tiles, split_axis=0, concat_axis=0, tiled=True)
+    *others, moved = lax.optimization_barrier((*others, moved))
+    slots = sum(others, slots)
+    size = lax.axis_size("ey")
+    slots = slots + lax.ppermute(slots, "ey", [(i, i ^ 1) for i in range(size)])
+    others = ring(slots, "ex", 1)
 
     five = pl.BlockSpec((group, SLAB, ROWS, LANES), lambda f: (f, 0, 0, 0))
     few = pl.BlockSpec((group, 4, ROWS, LANES), lambda f: (f, 0, 0, 0))
@@ -500,16 +604,17 @@
         name="solve",
     )(coef, moved.reshape(FIELDS, SLAB, ROWS, LANES), g1, g2, g3, cost_class)
 
+    *others, physics = lax.optimization_barrier((*others, physics))
     return pl.pallas_call(
         share_kernel,
         grid=(FIELDS // group,),
-        in_specs=[five, whole_spec((LANES, LANES)), whole_spec((1024, 1024))],
+        in_specs=[five, whole_spec((1024, 1024))] + [whole_spec((LANES, LANES))] * 4,
         out_specs=five,
         out_shape=shaped(FIELDS, SLAB, ROWS, LANES),
         scratch_shapes=[pltpu.VMEM((LANES, LANES), F32)],
         compiler_params=LIMIT,
         name="share",
-    )(physics, total.reshape(LANES, LANES), onehot)
+    )(physics, onehot, slots, *others)
 
 
 def solution(mesh):

time: 84.7 us -> 62.5 us (0.74); the launches traced: 83.4 us -> 62.3 us
  blocking collectives: 14.5 us -> 0 us
  Pallas kernels: 30.4 us -> 22.3 us
  local copies, waits for them, and re-layouts: 7.85 us -> 1.61 us
  waiting for transfers between devices: 10.7 us -> 15 us
  starting transfers between devices: 19.7 us -> 23.2 us
    all_to_all x1 -> x0, blocking collectives: 14.5 us -> none  [local(): lax.all_to_all(summed, tiles, split_axis=0, concat_axis=0, tiled=True)]
    ppermute x6 -> x15, waiting for transfers between devices: 1.3 us -> 15 us  [the longest x9 8.38 us: ring(): lax.ppermute(value, axis, shift(axis, r))]
    ppermute x6 -> x15, starting transfers between devices: 8.95 us -> 16.3 us  [the longest x9 9.24 us: ring(): lax.ppermute(value, axis, shift(axis, r))]
    pallas_call x3 -> x4, Pallas kernels: 18.7 us -> 11.9 us  [the longest x1 7.49 us: local(): pl.pallas_call(move_kernel, grid=(steps,), in_specs=[SMEM, whole_spec((56...]
    ppermute x1, waiting for transfers between devices: 6.16 us -> 0.01 us  [local(): top = lax.ppermute(down, 'ex', shift('ex', 1))]
    unnamed x26 -> x16, local copies, waits for them, and re-layouts: 7.21 us -> 1.61 us
    all_to_all x1 -> x0, starting transfers between devices: 3.83 us -> none  [local(): total = lax.all_to_all(mine, tiles, split_axis=0, concat_axis=0, tiled=True)]
    ppermute x1, waiting for transfers between devices: 2.54 us -> 0.01 us  [local(): from_left = lax.ppermute(right, 'ey', shift('ey', 1))]
  transfers between devices with their start and end apart: 11 -> 19, of which waited for: 5 -> 10; matrix products, arithmetic and copies ran while one was open for 1% -> 0% of each run, Pallas kernels for 11% -> 17%
where the time goes in v2:
time: 62.5 us; the launch traced here: 62.3 us
  starting transfers between devices  23.2 us (37%)
  Pallas kernels  22.3 us (36%)
  waiting for transfers between devices  15 us (24%)
  local copies, waits for them, and re-layouts  1.61 us (3%)
    ppermute x9, starting transfers between devices, ring(): lax.ppermute(value, axis, shift(axis, r))  9.24 us
    ppermute x9, waiting for transfers between devices, ring(): lax.ppermute(value, axis, shift(axis, r))  8.38 us
    pallas_call x1, Pallas kernels, local(): pl.pallas_call(move_kernel, grid=(steps,), in_specs=[SMEM, whole_spec((56...  7.49 us
    ppermute x3, waiting for transfers between devices, local(): lax.ppermute(m, 'lb', shift('lb', r)).reshape(FIELDS, 4, ROWS, LANES)  4.45 us
    ppermute x3, starting transfers between devices, local(): lax.ppermute(m, 'lb', shift('lb', r)).reshape(FIELDS, 4, ROWS, LANES)  3.96 us
    pallas_call x1, Pallas kernels, local(): pl.pallas_call(solve_kernel, grid=(FIELDS // group,), in_specs=[SMEM, fiv...  3.94 us
    pallas_call x1, Pallas kernels, local(): pl.pallas_call(prep_kernel, out_shape=(shaped(56, LANES), shaped(1024, 10...  3.88 us
    ppermute x1, starting transfers between devices, local(): from_right = lax.ppermute(left, 'ey', shift('ey', -1))  3.57 us
  transfers between devices with their start and end apart: 19, of which 10 were waited for; matrix products, arithmetic and copies ran while one was open for 0% of the time, Pallas kernels for 17%

profile of v2, /device:TPU:0, one launch (start us, length us, event | category | flops | bytes accessed | tf_op | source)
XLA Modules:
  0.0 62.3 jit_solution(11381681355606643399)
XLA Ops:
  0.0 1.6 %copy-done = f32[15,32,8,128]{3,2,1,0:T(8,128)S(1)} copy-done((f32[15,32,8,128]{3,2,1,0:T(8,128)S(1)}, f32[15,32,8,128]{3,2,1,0:T(8,128)}, u32[]{:S(2)}) %copy-start) | copy-done | bytes 1966104
  1.6 1.7 %pack.1 = (f32[30,8,128]{2,1,0:T(8,128)S(1)}, f32[30,8,128]{2,1,0:T(8,128)S(1)}, s32[16,128]{1,0:T(8,128)S(1)}) custom-call(f32[30,16,8,128]{3,2,1,0:T(8,128)S(1)} %bitcast.10, s32[8,128]{1,0:T(8,128)} %class_ref.3, s32[8,128]{1,0:T(8,128)} %bitcast.16), custom_call_target="tpu_custom_call" | custom-call | tf_op jit(solution)/shard_map/pack/pallas_call | solution.py:487
  3.4 3.6 %collective-permute-start.1 = (f32[30,8,128]{2,1,0:T(8,128)S(1)}, f32[30,8,128]{2,1,0:T(8,128)S(1)}, u32[]{:S(2)}, u32[]{:S(2)}) collective-permute-start(f32[30,8,128]{2,1,0:T(8,128)S(1)} %get-tuple-element.28), channel_id=1, source_target_pairs={{0,28},{4,0},{8,4},{12,8},{16,12},{20,16},{24,20},{28,24},{1,29},{... | collective-permute-start | bytes 368648 | tf_op jit(solution)/shard_map/ppermute | solution.py:510
  6.9 3.0 %collective-permute-start.3 = (s32[16,128]{1,0:T(8,128)S(1)}, s32[16,128]{1,0:T(8,128)S(1)}, u32[]{:S(2)}, u32[]{:S(2)}) collective-permute-start(s32[16,128]{1,0:T(8,128)S(1)} %get-tuple-element.29.own_ref), channel_id=1, source_target_pairs={{0,96},{32,0},{64,32},{96,64},{1,97},{33,1},{65,33},{97,65},{2,98}... | collective-permute-start | bytes 24584 | tf_op jit(solution)/shard_map/ppermute | solution.py:512
  10.0 3.9 %prep.1 = (f32[56,128]{1,0:T(8,128)S(1)}, bf16[1024,1024]{1,0:T(8,128)(2,1)S(1)}) custom-call(f32[1,127]{1,0:T(1,128)S(1)} %bitcast.18, f32[1,128]{1,0:T(1,128)S(1)} %bitcast.19, f32[15,128]{1,0:T(8,128)S(1)} %copy-done.4, s32[1,1024]{1,0:T(1,128)S(1)} %bitcast.17), custom_call_target="tpu_custom_call" | custom-call | tf_op jit(solution)/shard_map/prep/pallas_call | solution.py:474
  13.9 0.9 %collective-permute-done.2.top_ref = s32[16,128]{1,0:T(8,128)S(1)} collective-permute-done((s32[16,128]{1,0:T(8,128)S(1)}, s32[16,128]{1,0:T(8,128)S(1)}, u32[]{:S(2)}, u32[]{:S(2)}) %collective-permute-start.2) | collective-permute-done | bytes 8224 | tf_op jit(solution)/shard_map/ppermute | solution.py:511
  14.8 7.5 %move.1 = (f32[3840,128]{1,0:T(8,128)S(1)}, f32[15,2,32,128]{3,2,1,0:T(8,128)S(1)}, f32[15,2,32,128]{3,2,1,0:T(8,128)S(1)}, f32[288,128]{1,0:T(8,128)S(1)}) custom-call(f32[15]{0:T(128)S(1)} %copy-done.5, f32[56,128]{1,0:T(8,128)S(1)} %get-tuple-element.26.c_ref, f32[3840,128]{1,0:T(8,128)S(1)} %bitcast.11, f32[30,8,128]{2,1,0:T(8,128)S(1)} %collective-permute-done.hl_ref, ...), custom_call_target="tpu_custom_call" | custom-call | tf_op jit(solution)/shard_map/move/pallas_call | solution.py:519
  22.4 3.2 %collective-permute-start.11 = (f32[15,2,32,128]{3,2,1,0:T(8,128)S(1)}, f32[15,2,32,128]{3,2,1,0:T(8,128)S(1)}, u32[]{:S(2)}, u32[]{:S(2)}) collective-permute-start(f32[15,2,32,128]{3,2,1,0:T(8,128)S(1)} %get-tuple-element.34), channel_id=1, source_target_pairs={{0,96},{32,0},{64,32},{96,64},{1,97},{33,1},{65,33},{97,65},{2,98}... | collective-permute-start | bytes 1474568 | tf_op jit(solution)/shard_map/ppermute | solution.py:557
  26.4 2.8 %collective-permute-start.6 = (f32[128,128]{1,0:T(8,128)S(1)}, f32[128,128]{1,0:T(8,128)S(1)}, u32[]{:S(2)}, u32[]{:S(2)}) collective-permute-start(f32[128,128]{1,0:T(8,128)S(1)} %slot.1), channel_id=1, source_target_pairs={{0,3},{1,0},{2,1},{3,2},{4,7},{5,4},{6,5},{7,6},{8,11},{9,8},{10,9... | collective-permute-start | bytes 196616 | tf_op jit(solution)/shard_map/ppermute | solution.py:463
  29.2 0.8 %collective-permute-start.5 = (f32[128,128]{1,0:T(8,128)S(1)}, f32[128,128]{1,0:T(8,128)S(1)}, u32[]{:S(2)}, u32[]{:S(2)}) collective-permute-start(f32[128,128]{1,0:T(8,128)S(1)} %slot.1), channel_id=1, source_target_pairs={{0,2},{1,3},{2,0},{3,1},{4,6},{5,7},{6,4},{7,5},{8,10},{9,11},{10,... | collective-permute-start | bytes 196616 | tf_op jit(solution)/shard_map/ppermute | solution.py:463
  30.0 0.9 %collective-permute-start.4 = (f32[128,128]{1,0:T(8,128)S(1)}, f32[128,128]{1,0:T(8,128)S(1)}, u32[]{:S(2)}, u32[]{:S(2)}) collective-permute-start(f32[128,128]{1,0:T(8,128)S(1)} %slot.1), channel_id=1, source_target_pairs={{0,1},{1,2},{2,3},{3,0},{4,5},{5,6},{6,7},{7,4},{8,9},{9,10},{10,1... | collective-permute-start | bytes 196616 | tf_op jit(solution)/shard_map/ppermute | solution.py:463
  31.1 3.9 %collective-permute-done.5 = f32[128,128]{1,0:T(8,128)S(1)} collective-permute-done((f32[128,128]{1,0:T(8,128)S(1)}, f32[128,128]{1,0:T(8,128)S(1)}, u32[]{:S(2)}, u32[]{:S(2)}) %collective-permute-start.5) | collective-permute-done | bytes 65568 | tf_op jit(solution)/shard_map/ppermute | solution.py:463
  35.7 2.3 %collective-permute-start.9 = (f32[128,128]{1,0:T(8,128)S(1)}, f32[128,128]{1,0:T(8,128)S(1)}, u32[]{:S(2)}, u32[]{:S(2)}) collective-permute-start(f32[128,128]{1,0:T(8,128)S(1)} %add_add_fusion.1), channel_id=1, source_target_pairs={{0,24},{4,28},{8,0},{12,4},{16,8},{20,12},{24,16},{28,20},{1,25},{... | collective-permute-start | bytes 196616 | tf_op jit(solution)/shard_map/ppermute | solution.py:463
  38.1 1.3 %collective-permute-start.7 = (f32[128,128]{1,0:T(8,128)S(1)}, f32[128,128]{1,0:T(8,128)S(1)}, u32[]{:S(2)}, u32[]{:S(2)}) collective-permute-start(f32[128,128]{1,0:T(8,128)S(1)} %add_add_fusion.1), channel_id=1, source_target_pairs={{0,8},{4,12},{8,16},{12,20},{16,24},{20,28},{24,0},{28,4},{1,9},{5... | collective-permute-start | bytes 196616 | tf_op jit(solution)/shard_map/ppermute | solution.py:463
  39.3 1.9 %meet.1 = (f32[3840,128]{1,0:T(8,128)S(1)}, f32[480,128]{1,0:T(8,128)S(1)}, f32[480,128]{1,0:T(8,128)S(1)}, f32[480,128]{1,0:T(8,128)S(1)}) custom-call(f32[15]{0:T(128)S(1)} %copy-done.5, f32[56,128]{1,0:T(8,128)S(1)} %get-tuple-element.26.c_ref, f32[3840,128]{1,0:T(8,128)S(1)} %get-tuple-element.32.u_ref, ...), custom_call_target="tpu_custom_call" | custom-call | tf_op jit(solution)/shard_map/meet/pallas_call | solution.py:569
  41.2 2.7 %collective-permute-done.8 = f32[128,128]{1,0:T(8,128)S(1)} collective-permute-done((f32[128,128]{1,0:T(8,128)S(1)}, f32[128,128]{1,0:T(8,128)S(1)}, u32[]{:S(2)}, u32[]{:S(2)}) %collective-permute-start.8) | collective-permute-done | bytes 65568 | tf_op jit(solution)/shard_map/ppermute | solution.py:463
  44.2 2.0 %collective-permute-start.17 = (f32[480,128]{1,0:T(8,128)S(1)}, f32[480,128]{1,0:T(8,128)S(1)}, u32[]{:S(2)}, u32[]{:S(2)}) collective-permute-start(f32[480,128]{1,0:T(8,128)S(1)} %get-tuple-element.41), channel_id=1, source_target_pairs={{0,2},{1,3},{2,0},{3,1},{4,6},{5,7},{6,4},{7,5},{8,10},{9,11},{10,... | collective-permute-start | bytes 737288 | tf_op jit(solution)/shard_map/ppermute | solution.py:585
  46.3 1.9 %collective-permute-start.18 = (f32[480,128]{1,0:T(8,128)S(1)}, f32[480,128]{1,0:T(8,128)S(1)}, u32[]{:S(2)}, u32[]{:S(2)}) collective-permute-start(f32[480,128]{1,0:T(8,128)S(1)} %get-tuple-element.42), channel_id=1, source_target_pairs={{0,3},{1,0},{2,1},{3,2},{4,7},{5,4},{6,5},{7,6},{8,11},{9,8},{10,9... | collective-permute-start | bytes 737288 | tf_op jit(solution)/shard_map/ppermute | solution.py:585
  48.3 1.2 %collective-permute-done.12 = f32[128,128]{1,0:T(8,128)S(1)} collective-permute-done((f32[128,128]{1,0:T(8,128)S(1)}, f32[128,128]{1,0:T(8,128)S(1)}, u32[]{:S(2)}, u32[]{:S(2)}) %collective-permute-start.12) | collective-permute-done | bytes 65568 | tf_op jit(solution)/shard_map/ppermute | solution.py:591
  49.6 1.2 %collective-permute-start.15 = (f32[128,128]{1,0:T(8,128)S(1)}, f32[128,128]{1,0:T(8,128)S(1)}, u32[]{:S(2)}, u32[]{:S(2)}) collective-permute-start(f32[128,128]{1,0:T(8,128)S(1)} %add.27.a_ref), channel_id=1, source_target_pairs={{0,96},{32,0},{64,32},{96,64},{1,97},{33,1},{65,33},{97,65},{2,98}... | collective-permute-start | bytes 196616 | tf_op jit(solution)/shard_map/ppermute | solution.py:463
  50.7 3.6 %collective-permute-done.16 = f32[480,128]{1,0:T(8,128)S(1)} collective-permute-done((f32[480,128]{1,0:T(8,128)S(1)}, f32[480,128]{1,0:T(8,128)S(1)}, u32[]{:S(2)}, u32[]{:S(2)}) %collective-permute-start.16) | collective-permute-done | bytes 245792 | tf_op jit(solution)/shard_map/ppermute | solution.py:585
  54.3 0.9 %collective-permute-done.18 = f32[480,128]{1,0:T(8,128)S(1)} collective-permute-done((f32[480,128]{1,0:T(8,128)S(1)}, f32[480,128]{1,0:T(8,128)S(1)}, u32[]{:S(2)}, u32[]{:S(2)}) %collective-permute-start.18) | collective-permute-done | bytes 245792 | tf_op jit(solution)/shard_map/ppermute | solution.py:585
  55.2 3.9 %solve.1.p_ref = f32[15,32,8,128]{3,2,1,0:T(8,128)S(1)} custom-call(f32[56,128]{1,0:T(8,128)S(1)} %get-tuple-element.26.c_ref, f32[15,32,8,128]{3,2,1,0:T(8,128)S(1)} %bitcast.12, f32[15,4,8,128]{3,2,1,0:T(8,128)S(1)} %bitcast.13, f32[15,4,8,128]{3,2,1,0:T(8,128)S(1)} %bitcast.14, f32[15,4,8,128]{3,2,1,0:T(8,128)S(1)} %bitcast.15, s32[8,128]{1,0:T(8,128)S(1)} %copy-done.2), custom_call_target="tpu_custom_call" | custom-call | tf_op jit(solution)/shard_map/solve/pallas_call | solution.py:596
  59.8 2.5 %share.1 = f32[15,32,8,128]{3,2,1,0:T(8,128)} custom-call(f32[15,32,8,128]{3,2,1,0:T(8,128)S(1)} %solve.1.p_ref, bf16[1024,1024]{1,0:T(8,128)(2,1)S(1)} %get-tuple-element.31.ot_ref, f32[128,128]{1,0:T(8,128)S(1)} %add.27.a_ref, f32[128,128]{1,0:T(8,128)S(1)} %collective-permute-done.13.b_ref, f32[128,128]{1,0:T(8,128)S(1)} %collective-permute-done.14.c_ref, ...), custom_call_target="tpu_custom_call" | custom-call | tf_op jit(solution)/shard_map/share/pallas_call | solution.py:608
  (40 shorter events, 2.9 us)
Async XLA Ops:
  0.0 9.9 %copy-start.7 = (f32[128]{0:T(128)S(1)}, f32[128]{0:T(128)}, u32[]{:S(2)}) copy-start(f32[128]{0:T(128)} %param.12) | copy-start | bytes 1540
  0.0 9.9 %copy-start.6 = (f32[127]{0:T(128)S(1)}, f32[127]{0:T(128)}, u32[]{:S(2)}) copy-start(f32[127]{0:T(128)} %param.11) | copy-start | bytes 1528
  0.0 14.8 %copy-start.5 = (f32[15]{0:T(128)S(1)}, f32[15]{0:T(128)}, u32[]{:S(2)}) copy-start(f32[15]{0:T(128)} %d_ref.3) | copy-start | bytes 184
  1.6 13.2 %copy-start.1 = (f32[15,32,8,128]{3,2,1,0:T(8,128)S(1)}, f32[15,32,8,128]{3,2,1,0:T(8,128)}, u32[]{:S(2)}) copy-start(f32[15,32,8,128]{3,2,1,0:T(8,128)} %param.9) | copy-start | bytes 5898244
  3.3 11.5 %collective-permute-start = (f32[30,8,128]{2,1,0:T(8,128)S(1)}, f32[30,8,128]{2,1,0:T(8,128)S(1)}, u32[]{:S(2)}, u32[]{:S(2)}) collective-permute-start(f32[30,8,128]{2,1,0:T(8,128)S(1)} %get-tuple-element.27), channel_id=1, source_target_pairs={{0,4},{4,8},{8,12},{12,16},{16,20},{20,24},{24,28},{28,0},{1,5},{5... | collective-permute-start | bytes 368648 | tf_op jit(solution)/shard_map/ppermute | solution.py:509
  3.4 11.5 %collective-permute-start.1 = (f32[30,8,128]{2,1,0:T(8,128)S(1)}, f32[30,8,128]{2,1,0:T(8,128)S(1)}, u32[]{:S(2)}, u32[]{:S(2)}) collective-permute-start(f32[30,8,128]{2,1,0:T(8,128)S(1)} %get-tuple-element.28), channel_id=1, source_target_pairs={{0,28},{4,0},{8,4},{12,8},{16,12},{20,16},{24,20},{28,24},{1,29},{... | collective-permute-start | bytes 368648 | tf_op jit(solution)/shard_map/ppermute | solution.py:510
  6.9 6.9 %collective-permute-start.3 = (s32[16,128]{1,0:T(8,128)S(1)}, s32[16,128]{1,0:T(8,128)S(1)}, u32[]{:S(2)}, u32[]{:S(2)}) collective-permute-start(s32[16,128]{1,0:T(8,128)S(1)} %get-tuple-element.29.own_ref), channel_id=1, source_target_pairs={{0,96},{32,0},{64,32},{96,64},{1,97},{33,1},{65,33},{97,65},{2,98}... | collective-permute-start | bytes 24584 | tf_op jit(solution)/shard_map/ppermute | solution.py:512
  9.9 4.9 %collective-permute-start.2 = (s32[16,128]{1,0:T(8,128)S(1)}, s32[16,128]{1,0:T(8,128)S(1)}, u32[]{:S(2)}, u32[]{:S(2)}) collective-permute-start(s32[16,128]{1,0:T(8,128)S(1)} %get-tuple-element.29.own_ref), channel_id=1, source_target_pairs={{0,32},{32,64},{64,96},{96,0},{1,33},{33,65},{65,97},{97,1},{2,34}... | collective-permute-start | bytes 24584 | tf_op jit(solution)/shard_map/ppermute | solution.py:511
  22.3 17.0 %collective-permute-start.10 = (f32[15,2,32,128]{3,2,1,0:T(8,128)S(1)}, f32[15,2,32,128]{3,2,1,0:T(8,128)S(1)}, u32[]{:S(2)}, u32[]{:S(2)}) collective-permute-start(f32[15,2,32,128]{3,2,1,0:T(8,128)S(1)} %get-tuple-element.33), channel_id=1, source_target_pairs={{0,32},{32,64},{64,96},{96,0},{1,33},{33,65},{65,97},{97,1},{2,34}... | collective-permute-start | bytes 1474568 | tf_op jit(solution)/shard_map/ppermute | solution.py:556
  22.4 16.9 %collective-permute-start.11 = (f32[15,2,32,128]{3,2,1,0:T(8,128)S(1)}, f32[15,2,32,128]{3,2,1,0:T(8,128)S(1)}, u32[]{:S(2)}, u32[]{:S(2)}) collective-permute-start(f32[15,2,32,128]{3,2,1,0:T(8,128)S(1)} %get-tuple-element.34), channel_id=1, source_target_pairs={{0,96},{32,0},{64,32},{96,64},{1,97},{33,1},{65,33},{97,65},{2,98}... | collective-permute-start | bytes 1474568 | tf_op jit(solution)/shard_map/ppermute | solution.py:557
  26.4 28.8 %copy-start.2 = (s32[8,128]{1,0:T(8,128)S(1)}, s32[8,128]{1,0:T(8,128)}, u32[]{:S(2)}) copy-start(s32[8,128]{1,0:T(8,128)} %class_ref.3) | copy-start | bytes 12292
  26.4 4.7 %collective-permute-start.6 = (f32[128,128]{1,0:T(8,128)S(1)}, f32[128,128]{1,0:T(8,128)S(1)}, u32[]{:S(2)}, u32[]{:S(2)}) collective-permute-start(f32[128,128]{1,0:T(8,128)S(1)} %slot.1), channel_id=1, source_target_pairs={{0,3},{1,0},{2,1},{3,2},{4,7},{5,4},{6,5},{7,6},{8,11},{9,8},{10,9... | collective-permute-start | bytes 196616 | tf_op jit(solution)/shard_map/ppermute | solution.py:463
  29.2 5.8 %collective-permute-start.5 = (f32[128,128]{1,0:T(8,128)S(1)}, f32[128,128]{1,0:T(8,128)S(1)}, u32[]{:S(2)}, u32[]{:S(2)}) collective-permute-start(f32[128,128]{1,0:T(8,128)S(1)} %slot.1), channel_id=1, source_target_pairs={{0,2},{1,3},{2,0},{3,1},{4,6},{5,7},{6,4},{7,5},{8,10},{9,11},{10,... | collective-permute-start | bytes 196616 | tf_op jit(solution)/shard_map/ppermute | solution.py:463
  30.0 5.7 %collective-permute-start.4 = (f32[128,128]{1,0:T(8,128)S(1)}, f32[128,128]{1,0:T(8,128)S(1)}, u32[]{:S(2)}, u32[]{:S(2)}) collective-permute-start(f32[128,128]{1,0:T(8,128)S(1)} %slot.1), channel_id=1, source_target_pairs={{0,1},{1,2},{2,3},{3,0},{4,5},{5,6},{6,7},{7,4},{8,9},{9,10},{10,1... | collective-permute-start | bytes 196616 | tf_op jit(solution)/shard_map/ppermute | solution.py:463
  35.7 5.5 %collective-permute-start.9 = (f32[128,128]{1,0:T(8,128)S(1)}, f32[128,128]{1,0:T(8,128)S(1)}, u32[]{:S(2)}, u32[]{:S(2)}) collective-permute-start(f32[128,128]{1,0:T(8,128)S(1)} %add_add_fusion.1), channel_id=1, source_target_pairs={{0,24},{4,28},{8,0},{12,4},{16,8},{20,12},{24,16},{28,20},{1,25},{... | collective-permute-start | bytes 196616 | tf_op jit(solution)/shard_map/ppermute | solution.py:463
  38.1 5.9 %collective-permute-start.8 = (f32[128,128]{1,0:T(8,128)S(1)}, f32[128,128]{1,0:T(8,128)S(1)}, u32[]{:S(2)}, u32[]{:S(2)}) collective-permute-start(f32[128,128]{1,0:T(8,128)S(1)} %add_add_fusion.1), channel_id=1, source_target_pairs={{0,16},{4,20},{8,24},{12,28},{16,0},{20,4},{24,8},{28,12},{1,17},{... | collective-permute-start | bytes 196616 | tf_op jit(solution)/shard_map/ppermute | solution.py:463
  38.1 6.2 %collective-permute-start.7 = (f32[128,128]{1,0:T(8,128)S(1)}, f32[128,128]{1,0:T(8,128)S(1)}, u32[]{:S(2)}, u32[]{:S(2)}) collective-permute-start(f32[128,128]{1,0:T(8,128)S(1)} %add_add_fusion.1), channel_id=1, source_target_pairs={{0,8},{4,12},{8,16},{12,20},{16,24},{20,28},{24,0},{28,4},{1,9},{5... | collective-permute-start | bytes 196616 | tf_op jit(solution)/shard_map/ppermute | solution.py:463
  44.2 10.0 %collective-permute-start.16 = (f32[480,128]{1,0:T(8,128)S(1)}, f32[480,128]{1,0:T(8,128)S(1)}, u32[]{:S(2)}, u32[]{:S(2)}) collective-permute-start(f32[480,128]{1,0:T(8,128)S(1)} %get-tuple-element.40), channel_id=1, source_target_pairs={{0,1},{1,2},{2,3},{3,0},{4,5},{5,6},{6,7},{7,4},{8,9},{9,10},{10,1... | collective-permute-start | bytes 737288 | tf_op jit(solution)/shard_map/ppermute | solution.py:585
  44.2 10.0 %collective-permute-start.17 = (f32[480,128]{1,0:T(8,128)S(1)}, f32[480,128]{1,0:T(8,128)S(1)}, u32[]{:S(2)}, u32[]{:S(2)}) collective-permute-start(f32[480,128]{1,0:T(8,128)S(1)} %get-tuple-element.41), channel_id=1, source_target_pairs={{0,2},{1,3},{2,0},{3,1},{4,6},{5,7},{6,4},{7,5},{8,10},{9,11},{10,... | collective-permute-start | bytes 737288 | tf_op jit(solution)/shard_map/ppermute | solution.py:585
  46.3 8.9 %collective-permute-start.18 = (f32[480,128]{1,0:T(8,128)S(1)}, f32[480,128]{1,0:T(8,128)S(1)}, u32[]{:S(2)}, u32[]{:S(2)}) collective-permute-start(f32[480,128]{1,0:T(8,128)S(1)} %get-tuple-element.42), channel_id=1, source_target_pairs={{0,3},{1,0},{2,1},{3,2},{4,7},{5,4},{6,5},{7,6},{8,11},{9,8},{10,9... | collective-permute-start | bytes 737288 | tf_op jit(solution)/shard_map/ppermute | solution.py:585
  48.2 1.3 %collective-permute-start.12 = (f32[128,128]{1,0:T(8,128)S(1)}, f32[128,128]{1,0:T(8,128)S(1)}, u32[]{:S(2)}, u32[]{:S(2)}) collective-permute-start(f32[128,128]{1,0:T(8,128)S(1)} %add_add_fusion), channel_id=1, source_target_pairs={{0,4},{4,0},{8,12},{12,8},{16,20},{20,16},{24,28},{28,24},{1,5},{5... | collective-permute-start | bytes 196616 | tf_op jit(solution)/shard_map/ppermute | solution.py:591
  49.6 9.6 %collective-permute-start.15 = (f32[128,128]{1,0:T(8,128)S(1)}, f32[128,128]{1,0:T(8,128)S(1)}, u32[]{:S(2)}, u32[]{:S(2)}) collective-permute-start(f32[128,128]{1,0:T(8,128)S(1)} %add.27.a_ref), channel_id=1, source_target_pairs={{0,96},{32,0},{64,32},{96,64},{1,97},{33,1},{65,33},{97,65},{2,98}... | collective-permute-start | bytes 196616 | tf_op jit(solution)/shard_map/ppermute | solution.py:463
  50.7 8.4 %collective-permute-start.14 = (f32[128,128]{1,0:T(8,128)S(1)}, f32[128,128]{1,0:T(8,128)S(1)}, u32[]{:S(2)}, u32[]{:S(2)}) collective-permute-start(f32[128,128]{1,0:T(8,128)S(1)} %add.27.a_ref), channel_id=1, source_target_pairs={{0,64},{32,96},{64,0},{96,32},{1,65},{33,97},{65,1},{97,33},{2,66}... | collective-permute-start | bytes 196616 | tf_op jit(solution)/shard_map/ppermute | solution.py:463
  54.3 5.5 %collective-permute-start.13 = (f32[128,128]{1,0:T(8,128)S(1)}, f32[128,128]{1,0:T(8,128)S(1)}, u32[]{:S(2)}, u32[]{:S(2)}) collective-permute-start(f32[128,128]{1,0:T(8,128)S(1)} %add.27.a_ref), channel_id=1, source_target_pairs={{0,32},{32,64},{64,96},{96,0},{1,33},{33,65},{65,97},{97,1},{2,34}... | collective-permute-start | bytes 196616 | tf_op jit(solution)/shard_map/ppermute | solution.py:463
  (3 other events, 18.3 us)

commit v3 on v2

--- a/solution.py
+++ b/solution.py
@@ -18,7 +18,7 @@
 LEVELS = 128
 TILES = 32
 PER = SLAB * ROWS
-GROUP = 3
+GROUP = 5
 
 
 def second_table():
@@ -61,7 +61,13 @@
         whole[248:256, cols] = take[8:16]
     high = whole.astype(ml_dtypes.bfloat16)
     low = (whole - high.astype(np.float64)).astype(ml_dtypes.bfloat16)
-    return high, low
+    table = np.zeros((512, 512), ml_dtypes.bfloat16)
+    table[0:128] = table[128:256] = high[:128]
+    table[256:384] = low[:128]
+    table[384:392], table[504:512] = high[128:136], high[248:256]
+    table[392:400], table[400:408] = high[248:256], high[128:136]
+    table[408:416], table[416:424] = low[248:256], low[128:136]
+    return table
 
 
 def dot(a, b, dims=(((1,), (0,)), ((), ()))):
@@ -190,9 +196,7 @@
         ).astype(BF16)
 
 
-def pack_kernel(x_ref, class_ref, span_ref, l_ref, r_ref, info_ref):
-    info_ref[0:8, :] = class_ref[...]
-    info_ref[8:16, :] = span_ref[...]
+def pack_kernel(x_ref, l_ref, r_ref):
     lane = lax.broadcasted_iota(jnp.int32, (2 * GROUP, ROWS, LANES), 2) // 8
     left = jnp.zeros((2 * GROUP, ROWS, LANES), F32)
     right = jnp.zeros((2 * GROUP, ROWS, LANES), F32)
@@ -234,7 +238,7 @@
 
 
 def move_kernel(
-    d_ref, c_ref, x_ref, hl_ref, hr_ref, wh_ref, wl_ref, own_ref, top_ref, bot_ref,
+    d_ref, c_ref, x_ref, hl_ref, hr_ref, w_ref, own_ref, top_ref, bot_ref,
     u_ref, down_ref, up_ref, ch, xh,
 ):
     base = pl.program_id(0) * GROUP
@@ -257,18 +261,16 @@
             hl = pltpu.roll(hl, LANES - 8 * q, 2)
             hr = pltpu.roll(hr, LANES - 8 * q, 2)
         both = jnp.where(lane >= LANES - 8, hl, jnp.where(lane < 8, hr, 0.0))
+        upper = both.astype(BF16).astype(F32)
+        both = upper + pltpu.roll(both - upper, 16, 2) + pltpu.roll(upper, 32, 2)
         for p in range(2 * GROUP):
             xh[128 * p + 8 * q : 128 * p + 8 * q + 8, :] = both[p]
     order = [(g, r) for g in range(GROUP) for r in range(ROWS)]
     rows = [x_ref[pl.ds(PER * g + r, SLAB, stride=ROWS), :] for g, r in order]
     halo = [xh[pl.ds(PER * g + r, SLAB, stride=ROWS), :] for g, r in order]
-    main = jnp.concatenate(
-        [jnp.concatenate(rows, axis=0), jnp.concatenate(halo, axis=0)], axis=1
-    )
-    high, low = split2(main)
-    count = PER * GROUP
-    twice = dot(jnp.concatenate([high, low], axis=0), wh_ref[...])
-    t = twice[:count] + twice[count:] + dot(high, wl_ref[...])
+    high, low = split2(jnp.concatenate(rows, axis=0))
+    edge = jnp.concatenate(halo, axis=0).astype(BF16)
+    t = dot(jnp.concatenate([high, low, high, edge], axis=1), w_ref[...])
     for g in range(GROUP):
         d = d_ref[base + g]
         own = rows[ROWS * g : ROWS * g + ROWS]
@@ -470,7 +472,7 @@
 
 def local(atmosphere_state, diffusivity, mixing, relaxation, forcing, span_map, cost_class):
     state = atmosphere_state
-    group = 5
+    group = 15
     coef, onehot = pl.pallas_call(
         prep_kernel,
         out_shape=(shaped(56, LANES), shaped(1024, 1024, dtype=BF16)),
@@ -484,34 +486,22 @@
     )(mixing.reshape(1, -1), relaxation.reshape(1, -1), forcing, span_map.reshape(1, -1))
 
     steps = FIELDS // GROUP
-    left, right, info = pl.pallas_call(
+    info = jnp.concatenate([cost_class, span_map.reshape(ROWS, LANES)], axis=0)
+    left, right = pl.pallas_call(
         pack_kernel,
         grid=(steps,),
-        in_specs=[
-            pl.BlockSpec((2 * GROUP, 16, ROWS, LANES), lambda f: (f, 0, 0, 0)),
-            whole_spec((ROWS, LANES)),
-            whole_spec((ROWS, LANES)),
-        ],
-        out_specs=[pl.BlockSpec((2 * GROUP, ROWS, LANES), lambda f: (f, 0, 0))] * 2
-        + [whole_spec((16, LANES))],
-        out_shape=(
-            shaped(30, ROWS, LANES),
-            shaped(30, ROWS, LANES),
-            shaped(16, LANES, dtype=jnp.int32),
-        ),
+        in_specs=[pl.BlockSpec((2 * GROUP, 16, ROWS, LANES), lambda f: (f, 0, 0, 0))],
+        out_specs=[pl.BlockSpec((2 * GROUP, ROWS, LANES), lambda f: (f, 0, 0))] * 2,
+        out_shape=(shaped(30, ROWS, LANES), shaped(30, ROWS, LANES)),
         compiler_params=LIMIT,
         name="pack",
-    )(
-        state.reshape(30, 16, ROWS, LANES),
-        stay(cost_class),
-        stay(span_map.reshape(ROWS, LANES)),
-    )
+    )(state.reshape(30, 16, ROWS, LANES))
     from_left = lax.ppermute(right, "ey", shift("ey", 1))
     from_right = lax.ppermute(left, "ey", shift("ey", -1))
     info_top = lax.ppermute(info, "ex", shift("ex", 1))
     info_bot = lax.ppermute(info, "ex", shift("ex", -1))
 
-    high, low = y_weights()
+    table_y = y_weights()
     edge = pl.BlockSpec((GROUP, 2, SLAB, LANES), lambda f: (f, 0, 0, 0))
     block = pl.BlockSpec((GROUP * PER, LANES), lambda f: (f, 0))
     halo = pl.BlockSpec((2 * GROUP, ROWS, LANES), lambda f: (f, 0, 0))
@@ -525,8 +515,7 @@
             block,
             halo,
             halo,
-            whole_spec((256, 512)),
-            whole_spec((256, 512)),
+            whole_spec((512, 512)),
             table,
             table,
             table,
@@ -547,14 +536,12 @@
         state.reshape(FIELDS * PER, LANES),
         from_left,
         from_right,
-        stay(jnp.asarray(high)),
-        stay(jnp.asarray(low)),
+        stay(jnp.asarray(table_y)),
         info,
         info_top,
         info_bot,
     )
     top = lax.ppermute(down, "ex", shift("ex", 1))
-    bottom = lax.ppermute(up, "ex", shift("ex", -1))
 
     slots = pl.pallas_call(
         slot_kernel,
@@ -562,6 +549,8 @@
         compiler_params=LIMIT,
         name="slot",
     )(pieces, info_top, info_bot, onehot)
+    up, slots = lax.optimization_barrier((up, slots))
+    bottom = lax.ppermute(up, "ex", shift("ex", -1))
     slots = sum(ring(slots, "lb", 1), slots)
     others = ring(slots, "ey", 2)
 

time: 62.5 us -> 59.3 us (0.949)
  Pallas kernels: 22.3 us -> 18.5 us
  waiting for transfers between devices: 15 us -> 13.8 us
  starting transfers between devices: 23.2 us -> 24.3 us
  other arithmetic: 0.05 us -> 0.73 us
    ppermute x3, waiting for transfers between devices: 4.45 us -> 2.31 us  [local(): lax.ppermute(m, 'lb', shift('lb', r)).reshape(FIELDS, 4, ROWS, LANES)]
    ppermute x9, starting transfers between devices: 9.24 us -> 11.4 us  [ring(): lax.ppermute(value, axis, shift(axis, r))]
    pallas_call x1, Pallas kernels: 7.49 us -> 5.81 us  [local(): pl.pallas_call(move_kernel, grid=(steps,), in_specs=[SMEM, whole_spec((56...]
    pallas_call x1, Pallas kernels: 1.72 us -> 0.72 us  [local(): pl.pallas_call(pack_kernel, grid=(steps,), in_specs=[pl.BlockSpec((2 * GR...]
    ppermute x9, waiting for transfers between devices: 8.38 us -> 9.3 us  [ring(): lax.ppermute(value, axis, shift(axis, r))]
    ppermute x1, starting transfers between devices: 3.22 us -> 2.32 us  [local(): bottom = lax.ppermute(up, 'ex', shift('ex', -1))]
    concatenate x0 -> x1, other arithmetic: none -> 0.69 us  [local(): info = jnp.concatenate([cost_class, span_map.reshape(ROWS, LANES)], axis=0)]
  transfers between devices with their start and end apart: 19 -> 19, of which waited for: 10 -> 11; matrix products, arithmetic and copies ran while one was open for 0% -> 1% of each run, Pallas kernels for 17% -> 15%
where the time goes in v3:
time: 59.3 us; the launch traced here: 59.1 us
  starting transfers between devices  24.3 us (41%)
  Pallas kernels  18.5 us (31%)
  waiting for transfers between devices  13.8 us (23%)
  local copies, waits for them, and re-layouts  1.61 us (3%)
  other arithmetic  0.73 us (1%)
    ppermute x9, starting transfers between devices, ring(): lax.ppermute(value, axis, shift(axis, r))  11.4 us
    ppermute x9, waiting for transfers between devices, ring(): lax.ppermute(value, axis, shift(axis, r))  9.3 us
    pallas_call x1, Pallas kernels, local(): pl.pallas_call(move_kernel, grid=(steps,), in_specs=[SMEM, whole_spec((56...  5.81 us
    ppermute x3, starting transfers between devices, local(): lax.ppermute(m, 'lb', shift('lb', r)).reshape(FIELDS, 4, ROWS, LANES)  3.96 us
    pallas_call x1, Pallas kernels, local(): pl.pallas_call(prep_kernel, out_shape=(shaped(56, LANES), shaped(1024, 10...  3.88 us
    ppermute x1, starting transfers between devices, local(): from_right = lax.ppermute(left, 'ey', shift('ey', -1))  3.57 us
    pallas_call x1, Pallas kernels, local(): pl.pallas_call(solve_kernel, grid=(FIELDS // group,), in_specs=[SMEM, fiv...  3.53 us
    ppermute x1, starting transfers between devices, local(): info_bot = lax.ppermute(info, 'ex', shift('ex', -1))  3.01 us
  transfers between devices with their start and end apart: 19, of which 11 were waited for; matrix products, arithmetic and copies ran while one was open for 1% of the time, Pallas kernels for 15%

profile of v3, /device:TPU:0, one launch (start us, length us, event | category | flops | bytes accessed | tf_op | source)
XLA Modules:
  0.0 59.1 jit_solution(3268913060993685995)
XLA Ops:
  0.0 1.6 %copy-done = f32[15,32,8,128]{3,2,1,0:T(8,128)S(1)} copy-done((f32[15,32,8,128]{3,2,1,0:T(8,128)S(1)}, f32[15,32,8,128]{3,2,1,0:T(8,128)}, u32[]{:S(2)}) %copy-start) | copy-done | bytes 1966104
  2.4 3.6 %collective-permute-start.1 = (f32[30,8,128]{2,1,0:T(8,128)S(1)}, f32[30,8,128]{2,1,0:T(8,128)S(1)}, u32[]{:S(2)}, u32[]{:S(2)}) collective-permute-start(f32[30,8,128]{2,1,0:T(8,128)S(1)} %get-tuple-element.29), channel_id=1, source_target_pairs={{0,28},{4,0},{8,4},{12,8},{16,12},{20,16},{24,20},{28,24},{1,29},{... | collective-permute-start | bytes 368648 | tf_op jit(solution)/shard_map/ppermute | solution.py:500
  6.6 3.0 %collective-permute-start.3 = (s32[16,128]{1,0:T(8,128)S(1)}, s32[16,128]{1,0:T(8,128)S(1)}, u32[]{:S(2)}, u32[]{:S(2)}) collective-permute-start(s32[16,128]{1,0:T(8,128)S(1)} %pad_add_fusion.own_ref), channel_id=1, source_target_pairs={{0,96},{32,0},{64,32},{96,64},{1,97},{33,1},{65,33},{97,65},{2,98}... | collective-permute-start | bytes 24584 | tf_op jit(solution)/shard_map/ppermute | solution.py:502
  9.7 3.9 %prep.1 = (f32[56,128]{1,0:T(8,128)S(1)}, bf16[1024,1024]{1,0:T(8,128)(2,1)S(1)}) custom-call(f32[1,127]{1,0:T(1,128)S(1)} %bitcast.18, f32[1,128]{1,0:T(1,128)S(1)} %bitcast.19, f32[15,128]{1,0:T(8,128)S(1)} %copy-done.4, s32[1,1024]{1,0:T(1,128)S(1)} %bitcast.17), custom_call_target="tpu_custom_call" | custom-call | tf_op jit(solution)/shard_map/prep/pallas_call | solution.py:476
  13.6 0.9 %collective-permute-done.2.top_ref = s32[16,128]{1,0:T(8,128)S(1)} collective-permute-done((s32[16,128]{1,0:T(8,128)S(1)}, s32[16,128]{1,0:T(8,128)S(1)}, u32[]{:S(2)}, u32[]{:S(2)}) %collective-permute-start.2) | collective-permute-done | bytes 8224 | tf_op jit(solution)/shard_map/ppermute | solution.py:501
  14.5 5.8 %move.1 = (f32[3840,128]{1,0:T(8,128)S(1)}, f32[15,2,32,128]{3,2,1,0:T(8,128)S(1)}, f32[15,2,32,128]{3,2,1,0:T(8,128)S(1)}, f32[288,128]{1,0:T(8,128)S(1)}) custom-call(f32[15]{0:T(128)S(1)} %copy-done.5, f32[56,128]{1,0:T(8,128)S(1)} %get-tuple-element.27.c_ref, f32[3840,128]{1,0:T(8,128)S(1)} %bitcast.11, f32[30,8,128]{2,1,0:T(8,128)S(1)} %collective-permute-done.hl_ref, ...), custom_call_target="tpu_custom_call" | custom-call | tf_op jit(solution)/shard_map/move/pallas_call | solution.py:509
  20.3 0.8 %slot.1 = f32[128,128]{1,0:T(8,128)S(1)} custom-call(f32[288,128]{1,0:T(8,128)S(1)} %get-tuple-element.31.ch_ref, s32[16,128]{1,0:T(8,128)S(1)} %collective-permute-done.2.top_ref, s32[16,128]{1,0:T(8,128)S(1)} %collective-permute-done.3.bot_ref, bf16[1024,1024]{1,0:T(8,128)(2,1)S(1)} %get-tuple-element.32.ot_ref), custom_call_target="tpu_custom_call" | custom-call | tf_op jit(solution)/shard_map/slot/pallas_call | solution.py:546
  21.1 2.3 %collective-permute-start.11 = (f32[15,2,32,128]{3,2,1,0:T(8,128)S(1)}, f32[15,2,32,128]{3,2,1,0:T(8,128)S(1)}, u32[]{:S(2)}, u32[]{:S(2)}) collective-permute-start(f32[15,2,32,128]{3,2,1,0:T(8,128)S(1)} %get-tuple-element.36), channel_id=1, source_target_pairs={{0,96},{32,0},{64,32},{96,64},{1,97},{33,1},{65,33},{97,65},{2,98}... | collective-permute-start | bytes 1474568 | tf_op jit(solution)/shard_map/ppermute | solution.py:553
  23.5 2.8 %collective-permute-start.6 = (f32[128,128]{1,0:T(8,128)S(1)}, f32[128,128]{1,0:T(8,128)S(1)}, u32[]{:S(2)}, u32[]{:S(2)}) collective-permute-start(f32[128,128]{1,0:T(8,128)S(1)} %slot.1), channel_id=1, source_target_pairs={{0,3},{1,0},{2,1},{3,2},{4,7},{5,4},{6,5},{7,6},{8,11},{9,8},{10,9... | collective-permute-start | bytes 196616 | tf_op jit(solution)/shard_map/ppermute | solution.py:465
  26.2 0.8 %collective-permute-start.5 = (f32[128,128]{1,0:T(8,128)S(1)}, f32[128,128]{1,0:T(8,128)S(1)}, u32[]{:S(2)}, u32[]{:S(2)}) collective-permute-start(f32[128,128]{1,0:T(8,128)S(1)} %slot.1), channel_id=1, source_target_pairs={{0,2},{1,3},{2,0},{3,1},{4,6},{5,7},{6,4},{7,5},{8,10},{9,11},{10,... | collective-permute-start | bytes 196616 | tf_op jit(solution)/shard_map/ppermute | solution.py:465
  27.0 0.9 %collective-permute-start.4 = (f32[128,128]{1,0:T(8,128)S(1)}, f32[128,128]{1,0:T(8,128)S(1)}, u32[]{:S(2)}, u32[]{:S(2)}) collective-permute-start(f32[128,128]{1,0:T(8,128)S(1)} %slot.1), channel_id=1, source_target_pairs={{0,1},{1,2},{2,3},{3,0},{4,5},{5,6},{6,7},{7,4},{8,9},{9,10},{10,1... | collective-permute-start | bytes 196616 | tf_op jit(solution)/shard_map/ppermute | solution.py:465
  28.1 3.9 %collective-permute-done.5 = f32[128,128]{1,0:T(8,128)S(1)} collective-permute-done((f32[128,128]{1,0:T(8,128)S(1)}, f32[128,128]{1,0:T(8,128)S(1)}, u32[]{:S(2)}, u32[]{:S(2)}) %collective-permute-start.5) | collective-permute-done | bytes 65568 | tf_op jit(solution)/shard_map/ppermute | solution.py:465
  32.7 2.4 %collective-permute-start.9 = (f32[128,128]{1,0:T(8,128)S(1)}, f32[128,128]{1,0:T(8,128)S(1)}, u32[]{:S(2)}, u32[]{:S(2)}) collective-permute-start(f32[128,128]{1,0:T(8,128)S(1)} %add_add_fusion.1), channel_id=1, source_target_pairs={{0,24},{4,28},{8,0},{12,4},{16,8},{20,12},{24,16},{28,20},{1,25},{... | collective-permute-start | bytes 196616 | tf_op jit(solution)/shard_map/ppermute | solution.py:465
  35.1 1.3 %collective-permute-start.7 = (f32[128,128]{1,0:T(8,128)S(1)}, f32[128,128]{1,0:T(8,128)S(1)}, u32[]{:S(2)}, u32[]{:S(2)}) collective-permute-start(f32[128,128]{1,0:T(8,128)S(1)} %add_add_fusion.1), channel_id=1, source_target_pairs={{0,8},{4,12},{8,16},{12,20},{16,24},{20,28},{24,0},{28,4},{1,9},{5... | collective-permute-start | bytes 196616 | tf_op jit(solution)/shard_map/ppermute | solution.py:465
  36.3 1.6 %meet.1 = (f32[3840,128]{1,0:T(8,128)S(1)}, f32[480,128]{1,0:T(8,128)S(1)}, f32[480,128]{1,0:T(8,128)S(1)}, f32[480,128]{1,0:T(8,128)S(1)}) custom-call(f32[15]{0:T(128)S(1)} %copy-done.5, f32[56,128]{1,0:T(8,128)S(1)} %get-tuple-element.27.c_ref, f32[3840,128]{1,0:T(8,128)S(1)} %get-tuple-element.34.u_ref, ...), custom_call_target="tpu_custom_call" | custom-call | tf_op jit(solution)/shard_map/meet/pallas_call | solution.py:558
  37.9 3.0 %collective-permute-done.8 = f32[128,128]{1,0:T(8,128)S(1)} collective-permute-done((f32[128,128]{1,0:T(8,128)S(1)}, f32[128,128]{1,0:T(8,128)S(1)}, u32[]{:S(2)}, u32[]{:S(2)}) %collective-permute-start.8) | collective-permute-done | bytes 65568 | tf_op jit(solution)/shard_map/ppermute | solution.py:465
  41.3 2.0 %collective-permute-start.17 = (f32[480,128]{1,0:T(8,128)S(1)}, f32[480,128]{1,0:T(8,128)S(1)}, u32[]{:S(2)}, u32[]{:S(2)}) collective-permute-start(f32[480,128]{1,0:T(8,128)S(1)} %get-tuple-element.43), channel_id=1, source_target_pairs={{0,2},{1,3},{2,0},{3,1},{4,6},{5,7},{6,4},{7,5},{8,10},{9,11},{10,... | collective-permute-start | bytes 737288 | tf_op jit(solution)/shard_map/ppermute | solution.py:574
  43.3 1.9 %collective-permute-start.18 = (f32[480,128]{1,0:T(8,128)S(1)}, f32[480,128]{1,0:T(8,128)S(1)}, u32[]{:S(2)}, u32[]{:S(2)}) collective-permute-start(f32[480,128]{1,0:T(8,128)S(1)} %get-tuple-element.44), channel_id=1, source_target_pairs={{0,3},{1,0},{2,1},{3,2},{4,7},{5,4},{6,5},{7,6},{8,11},{9,8},{10,9... | collective-permute-start | bytes 737288 | tf_op jit(solution)/shard_map/ppermute | solution.py:574
  45.3 1.2 %collective-permute-done.12 = f32[128,128]{1,0:T(8,128)S(1)} collective-permute-done((f32[128,128]{1,0:T(8,128)S(1)}, f32[128,128]{1,0:T(8,128)S(1)}, u32[]{:S(2)}, u32[]{:S(2)}) %collective-permute-start.12) | collective-permute-done | bytes 65568 | tf_op jit(solution)/shard_map/ppermute | solution.py:580
  46.6 3.3 %collective-permute-start.15 = (f32[128,128]{1,0:T(8,128)S(1)}, f32[128,128]{1,0:T(8,128)S(1)}, u32[]{:S(2)}, u32[]{:S(2)}) collective-permute-start(f32[128,128]{1,0:T(8,128)S(1)} %add.27.a_ref), channel_id=1, source_target_pairs={{0,96},{32,0},{64,32},{96,64},{1,97},{33,1},{65,33},{97,65},{2,98}... | collective-permute-start | bytes 196616 | tf_op jit(solution)/shard_map/ppermute | solution.py:465
  49.9 1.6 %collective-permute-done.16 = f32[480,128]{1,0:T(8,128)S(1)} collective-permute-done((f32[480,128]{1,0:T(8,128)S(1)}, f32[480,128]{1,0:T(8,128)S(1)}, u32[]{:S(2)}, u32[]{:S(2)}) %collective-permute-start.16) | collective-permute-done | bytes 245792 | tf_op jit(solution)/shard_map/ppermute | solution.py:574
  52.2 3.5 %solve.1.p_ref = f32[15,32,8,128]{3,2,1,0:T(8,128)S(1)} custom-call(f32[56,128]{1,0:T(8,128)S(1)} %get-tuple-element.27.c_ref, f32[15,32,8,128]{3,2,1,0:T(8,128)S(1)} %bitcast.12, f32[15,4,8,128]{3,2,1,0:T(8,128)S(1)} %bitcast.13, f32[15,4,8,128]{3,2,1,0:T(8,128)S(1)} %bitcast.14, f32[15,4,8,128]{3,2,1,0:T(8,128)S(1)} %bitcast.15, s32[8,128]{1,0:T(8,128)S(1)} %copy-done.2), custom_call_target="tpu_custom_call" | custom-call | tf_op jit(solution)/shard_map/solve/pallas_call | solution.py:585
  56.0 1.0 %collective-permute-done.13.b_ref = f32[128,128]{1,0:T(8,128)S(1)} collective-permute-done((f32[128,128]{1,0:T(8,128)S(1)}, f32[128,128]{1,0:T(8,128)S(1)}, u32[]{:S(2)}, u32[]{:S(2)}) %collective-permute-start.13) | collective-permute-done | bytes 65568 | tf_op jit(solution)/shard_map/ppermute | solution.py:465
  56.9 2.2 %share.1 = f32[15,32,8,128]{3,2,1,0:T(8,128)} custom-call(f32[15,32,8,128]{3,2,1,0:T(8,128)S(1)} %solve.1.p_ref, bf16[1024,1024]{1,0:T(8,128)(2,1)S(1)} %get-tuple-element.32.ot_ref, f32[128,128]{1,0:T(8,128)S(1)} %add.27.a_ref, f32[128,128]{1,0:T(8,128)S(1)} %collective-permute-done.13.b_ref, f32[128,128]{1,0:T(8,128)S(1)} %collective-permute-done.14.c_ref, ...), custom_call_target="tpu_custom_call" | custom-call | tf_op jit(solution)/shard_map/share/pallas_call | solution.py:597
  (41 shorter events, 3.8 us)
Async XLA Ops:
  0.0 9.6 %copy-start.7 = (f32[128]{0:T(128)S(1)}, f32[128]{0:T(128)}, u32[]{:S(2)}) copy-start(f32[128]{0:T(128)} %param.11) | copy-start | bytes 1540
  0.0 9.6 %copy-start.6 = (f32[127]{0:T(128)S(1)}, f32[127]{0:T(128)}, u32[]{:S(2)}) copy-start(f32[127]{0:T(128)} %param.10) | copy-start | bytes 1528
  0.0 14.5 %copy-start.5 = (f32[15]{0:T(128)S(1)}, f32[15]{0:T(128)}, u32[]{:S(2)}) copy-start(f32[15]{0:T(128)} %d_ref.3) | copy-start | bytes 184
  1.6 8.1 %copy-start.4 = (f32[15,128]{1,0:T(8,128)S(1)}, f32[15,128]{1,0:T(8,128)}, u32[]{:S(2)}) copy-start(f32[15,128]{1,0:T(8,128)} %g_ref.1) | copy-start | bytes 23044
  1.6 12.9 %copy-start.1 = (f32[15,32,8,128]{3,2,1,0:T(8,128)S(1)}, f32[15,32,8,128]{3,2,1,0:T(8,128)}, u32[]{:S(2)}) copy-start(f32[15,32,8,128]{3,2,1,0:T(8,128)} %param.8) | copy-start | bytes 5898244
  2.3 12.2 %collective-permute-start = (f32[30,8,128]{2,1,0:T(8,128)S(1)}, f32[30,8,128]{2,1,0:T(8,128)S(1)}, u32[]{:S(2)}, u32[]{:S(2)}) collective-permute-start(f32[30,8,128]{2,1,0:T(8,128)S(1)} %get-tuple-element.28), channel_id=1, source_target_pairs={{0,4},{4,8},{8,12},{12,16},{16,20},{20,24},{24,28},{28,0},{1,5},{5... | collective-permute-start | bytes 368648 | tf_op jit(solution)/shard_map/ppermute | solution.py:499
  2.4 12.1 %collective-permute-start.1 = (f32[30,8,128]{2,1,0:T(8,128)S(1)}, f32[30,8,128]{2,1,0:T(8,128)S(1)}, u32[]{:S(2)}, u32[]{:S(2)}) collective-permute-start(f32[30,8,128]{2,1,0:T(8,128)S(1)} %get-tuple-element.29), channel_id=1, source_target_pairs={{0,28},{4,0},{8,4},{12,8},{16,12},{20,16},{24,20},{28,24},{1,29},{... | collective-permute-start | bytes 368648 | tf_op jit(solution)/shard_map/ppermute | solution.py:500
  6.6 6.9 %collective-permute-start.3 = (s32[16,128]{1,0:T(8,128)S(1)}, s32[16,128]{1,0:T(8,128)S(1)}, u32[]{:S(2)}, u32[]{:S(2)}) collective-permute-start(s32[16,128]{1,0:T(8,128)S(1)} %pad_add_fusion.own_ref), channel_id=1, source_target_pairs={{0,96},{32,0},{64,32},{96,64},{1,97},{33,1},{65,33},{97,65},{2,98}... | collective-permute-start | bytes 24584 | tf_op jit(solution)/shard_map/ppermute | solution.py:502
  9.6 4.9 %collective-permute-start.2 = (s32[16,128]{1,0:T(8,128)S(1)}, s32[16,128]{1,0:T(8,128)S(1)}, u32[]{:S(2)}, u32[]{:S(2)}) collective-permute-start(s32[16,128]{1,0:T(8,128)S(1)} %pad_add_fusion.own_ref), channel_id=1, source_target_pairs={{0,32},{32,64},{64,96},{96,0},{1,33},{33,65},{65,97},{97,1},{2,34}... | collective-permute-start | bytes 24584 | tf_op jit(solution)/shard_map/ppermute | solution.py:501
  21.1 15.2 %collective-permute-start.11 = (f32[15,2,32,128]{3,2,1,0:T(8,128)S(1)}, f32[15,2,32,128]{3,2,1,0:T(8,128)S(1)}, u32[]{:S(2)}, u32[]{:S(2)}) collective-permute-start(f32[15,2,32,128]{3,2,1,0:T(8,128)S(1)} %get-tuple-element.36), channel_id=1, source_target_pairs={{0,96},{32,0},{64,32},{96,64},{1,97},{33,1},{65,33},{97,65},{2,98}... | collective-permute-start | bytes 1474568 | tf_op jit(solution)/shard_map/ppermute | solution.py:553
  23.5 12.9 %collective-permute-start.10 = (f32[15,2,32,128]{3,2,1,0:T(8,128)S(1)}, f32[15,2,32,128]{3,2,1,0:T(8,128)S(1)}, u32[]{:S(2)}, u32[]{:S(2)}) collective-permute-start(f32[15,2,32,128]{3,2,1,0:T(8,128)S(1)} %get-tuple-element.35), channel_id=1, source_target_pairs={{0,32},{32,64},{64,96},{96,0},{1,33},{33,65},{65,97},{97,1},{2,34}... | collective-permute-start | bytes 1474568 | tf_op jit(solution)/shard_map/ppermute | solution.py:544
  23.5 4.7 %collective-permute-start.6 = (f32[128,128]{1,0:T(8,128)S(1)}, f32[128,128]{1,0:T(8,128)S(1)}, u32[]{:S(2)}, u32[]{:S(2)}) collective-permute-start(f32[128,128]{1,0:T(8,128)S(1)} %slot.1), channel_id=1, source_target_pairs={{0,3},{1,0},{2,1},{3,2},{4,7},{5,4},{6,5},{7,6},{8,11},{9,8},{10,9... | collective-permute-start | bytes 196616 | tf_op jit(solution)/shard_map/ppermute | solution.py:465
  26.2 5.8 %collective-permute-start.5 = (f32[128,128]{1,0:T(8,128)S(1)}, f32[128,128]{1,0:T(8,128)S(1)}, u32[]{:S(2)}, u32[]{:S(2)}) collective-permute-start(f32[128,128]{1,0:T(8,128)S(1)} %slot.1), channel_id=1, source_target_pairs={{0,2},{1,3},{2,0},{3,1},{4,6},{5,7},{6,4},{7,5},{8,10},{9,11},{10,... | collective-permute-start | bytes 196616 | tf_op jit(solution)/shard_map/ppermute | solution.py:465
  27.0 5.7 %collective-permute-start.4 = (f32[128,128]{1,0:T(8,128)S(1)}, f32[128,128]{1,0:T(8,128)S(1)}, u32[]{:S(2)}, u32[]{:S(2)}) collective-permute-start(f32[128,128]{1,0:T(8,128)S(1)} %slot.1), channel_id=1, source_target_pairs={{0,1},{1,2},{2,3},{3,0},{4,5},{5,6},{6,7},{7,4},{8,9},{9,10},{10,1... | collective-permute-start | bytes 196616 | tf_op jit(solution)/shard_map/ppermute | solution.py:465
  32.7 5.2 %collective-permute-start.9 = (f32[128,128]{1,0:T(8,128)S(1)}, f32[128,128]{1,0:T(8,128)S(1)}, u32[]{:S(2)}, u32[]{:S(2)}) collective-permute-start(f32[128,128]{1,0:T(8,128)S(1)} %add_add_fusion.1), channel_id=1, source_target_pairs={{0,24},{4,28},{8,0},{12,4},{16,8},{20,12},{24,16},{28,20},{1,25},{... | collective-permute-start | bytes 196616 | tf_op jit(solution)/shard_map/ppermute | solution.py:465
  35.1 5.9 %collective-permute-start.8 = (f32[128,128]{1,0:T(8,128)S(1)}, f32[128,128]{1,0:T(8,128)S(1)}, u32[]{:S(2)}, u32[]{:S(2)}) collective-permute-start(f32[128,128]{1,0:T(8,128)S(1)} %add_add_fusion.1), channel_id=1, source_target_pairs={{0,16},{4,20},{8,24},{12,28},{16,0},{20,4},{24,8},{28,12},{1,17},{... | collective-permute-start | bytes 196616 | tf_op jit(solution)/shard_map/ppermute | solution.py:465
  35.1 6.2 %collective-permute-start.7 = (f32[128,128]{1,0:T(8,128)S(1)}, f32[128,128]{1,0:T(8,128)S(1)}, u32[]{:S(2)}, u32[]{:S(2)}) collective-permute-start(f32[128,128]{1,0:T(8,128)S(1)} %add_add_fusion.1), channel_id=1, source_target_pairs={{0,8},{4,12},{8,16},{12,20},{16,24},{20,28},{24,0},{28,4},{1,9},{5... | collective-permute-start | bytes 196616 | tf_op jit(solution)/shard_map/ppermute | solution.py:465
  41.3 10.2 %collective-permute-start.16 = (f32[480,128]{1,0:T(8,128)S(1)}, f32[480,128]{1,0:T(8,128)S(1)}, u32[]{:S(2)}, u32[]{:S(2)}) collective-permute-start(f32[480,128]{1,0:T(8,128)S(1)} %get-tuple-element.42), channel_id=1, source_target_pairs={{0,1},{1,2},{2,3},{3,0},{4,5},{5,6},{6,7},{7,4},{8,9},{9,10},{10,1... | collective-permute-start | bytes 737288 | tf_op jit(solution)/shard_map/ppermute | solution.py:574
  41.3 10.2 %collective-permute-start.17 = (f32[480,128]{1,0:T(8,128)S(1)}, f32[480,128]{1,0:T(8,128)S(1)}, u32[]{:S(2)}, u32[]{:S(2)}) collective-permute-start(f32[480,128]{1,0:T(8,128)S(1)} %get-tuple-element.43), channel_id=1, source_target_pairs={{0,2},{1,3},{2,0},{3,1},{4,6},{5,7},{6,4},{7,5},{8,10},{9,11},{10,... | collective-permute-start | bytes 737288 | tf_op jit(solution)/shard_map/ppermute | solution.py:574
  43.3 8.9 %collective-permute-start.18 = (f32[480,128]{1,0:T(8,128)S(1)}, f32[480,128]{1,0:T(8,128)S(1)}, u32[]{:S(2)}, u32[]{:S(2)}) collective-permute-start(f32[480,128]{1,0:T(8,128)S(1)} %get-tuple-element.44), channel_id=1, source_target_pairs={{0,3},{1,0},{2,1},{3,2},{4,7},{5,4},{6,5},{7,6},{8,11},{9,8},{10,9... | collective-permute-start | bytes 737288 | tf_op jit(solution)/shard_map/ppermute | solution.py:574
  45.2 1.3 %collective-permute-start.12 = (f32[128,128]{1,0:T(8,128)S(1)}, f32[128,128]{1,0:T(8,128)S(1)}, u32[]{:S(2)}, u32[]{:S(2)}) collective-permute-start(f32[128,128]{1,0:T(8,128)S(1)} %add_add_fusion), channel_id=1, source_target_pairs={{0,4},{4,0},{8,12},{12,8},{16,20},{20,16},{24,28},{28,24},{1,5},{5... | collective-permute-start | bytes 196616 | tf_op jit(solution)/shard_map/ppermute | solution.py:580
  46.6 9.2 %collective-permute-start.15 = (f32[128,128]{1,0:T(8,128)S(1)}, f32[128,128]{1,0:T(8,128)S(1)}, u32[]{:S(2)}, u32[]{:S(2)}) collective-permute-start(f32[128,128]{1,0:T(8,128)S(1)} %add.27.a_ref), channel_id=1, source_target_pairs={{0,96},{32,0},{64,32},{96,64},{1,97},{33,1},{65,33},{97,65},{2,98}... | collective-permute-start | bytes 196616 | tf_op jit(solution)/shard_map/ppermute | solution.py:465
  49.9 6.1 %collective-permute-start.14 = (f32[128,128]{1,0:T(8,128)S(1)}, f32[128,128]{1,0:T(8,128)S(1)}, u32[]{:S(2)}, u32[]{:S(2)}) collective-permute-start(f32[128,128]{1,0:T(8,128)S(1)} %add.27.a_ref), channel_id=1, source_target_pairs={{0,64},{32,96},{64,0},{96,32},{1,65},{33,97},{65,1},{97,33},{2,66}... | collective-permute-start | bytes 196616 | tf_op jit(solution)/shard_map/ppermute | solution.py:465
  51.4 5.5 %collective-permute-start.13 = (f32[128,128]{1,0:T(8,128)S(1)}, f32[128,128]{1,0:T(8,128)S(1)}, u32[]{:S(2)}, u32[]{:S(2)}) collective-permute-start(f32[128,128]{1,0:T(8,128)S(1)} %add.27.a_ref), channel_id=1, source_target_pairs={{0,32},{32,64},{64,96},{96,0},{1,33},{33,65},{65,97},{97,1},{2,34}... | collective-permute-start | bytes 196616 | tf_op jit(solution)/shard_map/ppermute | solution.py:465
  (3 other events, 14.0 us)

commit v4 on v3

--- a/solution.py
+++ b/solution.py
@@ -86,7 +86,7 @@
     return high, mid, (rest - mid.astype(F32)).astype(BF16)
 
 
-def prep_kernel(mix_ref, rel_ref, g_ref, span_ref, c_ref, ot_ref, pad, sols, buf):
+def prep_kernel(mix_ref, rel_ref, g_ref, c_ref, pad, sols, buf):
     j = lax.axis_index("lb")
     row = lax.broadcasted_iota(jnp.int32, (8, LANES), 0)
     lane = lax.broadcasted_iota(jnp.int32, (8, LANES), 1)
@@ -188,15 +188,16 @@
         precision=lax.Precision.HIGHEST,
         preferred_element_type=F32,
     )
-    spots = span_ref[...]
+
+
+def table_kernel(class_ref, span_ref, ot_ref, info_ref):
+    info_ref[0:8, :] = class_ref[...]
+    info_ref[8:16, :] = span_ref[...]
     for block in range(8):
-        place = lax.broadcasted_iota(jnp.int32, (LANES, 1024), 0) + LANES * block
-        ot_ref[LANES * block : LANES * (block + 1), :] = jnp.where(
-            place == spots, 1.0, 0.0
-        ).astype(BF16)
-
-
-def pack_kernel(x_ref, l_ref, r_ref):
+        ot_ref[LANES * block : LANES * (block + 1), :] = slot_block(info_ref, block)
+
+
+def pack_kernel(x_ref, info_ref, l_ref, r_ref):
     lane = lax.broadcasted_iota(jnp.int32, (2 * GROUP, ROWS, LANES), 2) // 8
     left = jnp.zeros((2 * GROUP, ROWS, LANES), F32)
     right = jnp.zeros((2 * GROUP, ROWS, LANES), F32)
@@ -420,13 +421,13 @@
         firsts.append(run)
 
 
-def share_kernel(p_ref, ot_ref, a_ref, b_ref, c_ref, d_ref, o_ref, sh):
+def share_kernel(p_ref, ot_ref, a_ref, b_ref, o_ref, sh):
     group = p_ref.shape[0]
     step = pl.program_id(0)
 
     @pl.when(step == 0)
     def _():
-        whole = (a_ref[...] + b_ref[...]) + (c_ref[...] + d_ref[...])
+        whole = a_ref[...] + b_ref[...]
         whole = jnp.concatenate([whole[16 * b : 16 * b + 16, :] for b in range(8)], axis=1)
         whole = jnp.concatenate(split3(whole), axis=0)
         for a in range(ROWS):
@@ -460,6 +461,11 @@
     return pltpu.with_memory_space_constraint(x, pltpu.HBM)
 
 
+def swap(value, axis, mask):
+    count = lax.axis_size(axis)
+    return lax.ppermute(value, axis, [(i, i ^ mask) for i in range(count)])
+
+
 def ring(value, axis, step):
     count = lax.axis_size(axis)
     return [lax.ppermute(value, axis, shift(axis, r)) for r in range(step, count, step)]
@@ -473,9 +479,9 @@
 def local(atmosphere_state, diffusivity, mixing, relaxation, forcing, span_map, cost_class):
     state = atmosphere_state
     group = 15
-    coef, onehot = pl.pallas_call(
+    coef = pl.pallas_call(
         prep_kernel,
-        out_shape=(shaped(56, LANES), shaped(1024, 1024, dtype=BF16)),
+        out_shape=shaped(56, LANES),
         scratch_shapes=[
             pltpu.VMEM((8, LANES), F32),
             pltpu.VMEM((4, 8, LANES), F32),
@@ -483,19 +489,27 @@
         ],
         compiler_params=LIMIT,
         name="prep",
-    )(mixing.reshape(1, -1), relaxation.reshape(1, -1), forcing, span_map.reshape(1, -1))
+    )(mixing.reshape(1, -1), relaxation.reshape(1, -1), forcing)
 
     steps = FIELDS // GROUP
-    info = jnp.concatenate([cost_class, span_map.reshape(ROWS, LANES)], axis=0)
+    onehot, info = pl.pallas_call(
+        table_kernel,
+        out_shape=(shaped(1024, 1024, dtype=BF16), shaped(16, LANES, dtype=jnp.int32)),
+        compiler_params=LIMIT,
+        name="table",
+    )(stay(cost_class), stay(span_map.reshape(ROWS, LANES)))
     left, right = pl.pallas_call(
         pack_kernel,
         grid=(steps,),
-        in_specs=[pl.BlockSpec((2 * GROUP, 16, ROWS, LANES), lambda f: (f, 0, 0, 0))],
+        in_specs=[
+            pl.BlockSpec((2 * GROUP, 16, ROWS, LANES), lambda f: (f, 0, 0, 0)),
+            pl.BlockSpec(memory_space=pl.ANY),
+        ],
         out_specs=[pl.BlockSpec((2 * GROUP, ROWS, LANES), lambda f: (f, 0, 0))] * 2,
         out_shape=(shaped(30, ROWS, LANES), shaped(30, ROWS, LANES)),
         compiler_params=LIMIT,
         name="pack",
-    )(state.reshape(30, 16, ROWS, LANES))
+    )(state.reshape(30, 16, ROWS, LANES), info)
     from_left = lax.ppermute(right, "ey", shift("ey", 1))
     from_right = lax.ppermute(left, "ey", shift("ey", -1))
     info_top = lax.ppermute(info, "ex", shift("ex", 1))
@@ -551,6 +565,7 @@
     )(pieces, info_top, info_bot, onehot)
     up, slots = lax.optimization_barrier((up, slots))
     bottom = lax.ppermute(up, "ex", shift("ex", -1))
+    slots = slots + swap(slots, "ey", 1)
     slots = sum(ring(slots, "lb", 1), slots)
     others = ring(slots, "ey", 2)
 
@@ -576,9 +591,8 @@
     ]
     *others, moved = lax.optimization_barrier((*others, moved))
     slots = sum(others, slots)
-    size = lax.axis_size("ey")
-    slots = slots + lax.ppermute(slots, "ey", [(i, i ^ 1) for i in range(size)])
-    others = ring(slots, "ex", 1)
+    slots = slots + swap(slots, "ex", 1)
+    other = swap(slots, "ex", 3)
 
     five = pl.BlockSpec((group, SLAB, ROWS, LANES), lambda f: (f, 0, 0, 0))
     few = pl.BlockSpec((group, 4, ROWS, LANES), lambda f: (f, 0, 0, 0))
@@ -593,17 +607,17 @@
         name="solve",
     )(coef, moved.reshape(FIELDS, SLAB, ROWS, LANES), g1, g2, g3, cost_class)
 
-    *others, physics = lax.optimization_barrier((*others, physics))
+    other, physics = lax.optimization_barrier((other, physics))
     return pl.pallas_call(
         share_kernel,
         grid=(FIELDS // group,),
-        in_specs=[five, whole_spec((1024, 1024))] + [whole_spec((LANES, LANES))] * 4,
+        in_specs=[five, whole_spec((1024, 1024))] + [whole_spec((LANES, LANES))] * 2,
         out_specs=five,
         out_shape=shaped(FIELDS, SLAB, ROWS, LANES),
         scratch_shapes=[pltpu.VMEM((LANES, LANES), F32)],
         compiler_params=LIMIT,
         name="share",
-    )(physics, onehot, slots, *others)
+    )(physics, onehot, slots, other)
 
 
 def solution(mesh):

time: 59.3 us -> 57.5 us (0.970)
  waiting for transfers between devices: 13.8 us -> 8.94 us
  starting transfers between devices: 24.3 us -> 27.1 us
  Pallas kernels: 18.5 us -> 19.2 us
  other arithmetic: 0.73 us -> 0.05 us
    ppermute x9 -> x6, waiting for transfers between devices: 9.3 us -> 2.84 us  [ring(): lax.ppermute(value, axis, shift(axis, r))]
    ppermute x1 -> x3, waiting for transfers between devices: 1.24 us -> 5.15 us  [swap(): return lax.ppermute(value, axis, [(i, i ^ mask) for i in range(count)])]
    ppermute x1 -> x3, starting transfers between devices: 0.09 us -> 3.73 us  [swap(): return lax.ppermute(value, axis, [(i, i ^ mask) for i in range(count)])]
    ppermute x1, starting transfers between devices: 0.01 us -> 1.58 us  [local(): info_top = lax.ppermute(info, 'ex', shift('ex', 1))]
    ppermute x9 -> x6, starting transfers between devices: 11.4 us -> 9.94 us  [ring(): lax.ppermute(value, axis, shift(axis, r))]
    ppermute x3, waiting for transfers between devices: 2.31 us -> 0.93 us  [local(): lax.ppermute(m, 'lb', shift('lb', r)).reshape(FIELDS, 4, ROWS, LANES)]
    ppermute x1, starting transfers between devices: 3.01 us -> 1.66 us  [local(): info_bot = lax.ppermute(info, 'ex', shift('ex', -1))]
    ppermute x1, waiting for transfers between devices: 0.94 us -> 0.01 us  [local(): info_top = lax.ppermute(info, 'ex', shift('ex', 1))]
  transfers between devices with their start and end apart: 19 -> 18, of which waited for: 11 -> 5; matrix products, arithmetic and copies ran while one was open for 1% -> 0% of each run, Pallas kernels for 15% -> 15%
where the time goes in v4:
time: 57.5 us; the launch traced here: 57 us
  starting transfers between devices  27.1 us (47%)
  Pallas kernels  19.2 us (33%)
  waiting for transfers between devices  8.94 us (16%)
  local copies, waits for them, and re-layouts  1.57 us (3%)
    ppermute x6, starting transfers between devices, ring(): lax.ppermute(value, axis, shift(axis, r))  9.94 us
    pallas_call x1, Pallas kernels, local(): pl.pallas_call(move_kernel, grid=(steps,), in_specs=[SMEM, whole_spec((56...  5.81 us
    ppermute x3, waiting for transfers between devices, swap(): return lax.ppermute(value, axis, [(i, i ^ mask) for i in range(count)])  5.15 us
    ppermute x3, starting transfers between devices, local(): lax.ppermute(m, 'lb', shift('lb', r)).reshape(FIELDS, 4, ROWS, LANES)  4.58 us
    ppermute x3, starting transfers between devices, swap(): return lax.ppermute(value, axis, [(i, i ^ mask) for i in range(count)])  3.73 us
    ppermute x1, starting transfers between devices, local(): from_right = lax.ppermute(left, 'ey', shift('ey', -1))  3.57 us
    pallas_call x1, Pallas kernels, local(): pl.pallas_call(solve_kernel, grid=(FIELDS // group,), in_specs=[SMEM, fiv...  3.53 us
    pallas_call x1, Pallas kernels, local(): pl.pallas_call(prep_kernel, out_shape=shaped(56, LANES), scratch_shapes=[...  3.4 us
  transfers between devices with their start and end apart: 18, of which 5 were waited for; matrix products, arithmetic and copies ran while one was open for 0% of the time, Pallas kernels for 15%

profile of v4, /device:TPU:0, one launch (start us, length us, event | category | flops | bytes accessed | tf_op | source)
XLA Modules:
  0.0 57.0 jit_solution(374232702850240188)
XLA Ops:
  0.0 1.2 %table.1 = (bf16[1024,1024]{1,0:T(8,128)(2,1)S(1)}, s32[16,128]{1,0:T(8,128)S(1)}) custom-call(s32[8,128]{1,0:T(8,128)} %class_ref.3, s32[8,128]{1,0:T(8,128)} %bitcast.17), custom_call_target="tpu_custom_call" | custom-call | tf_op jit(solution)/shard_map/table/pallas_call | solution.py:495
  1.3 1.5 %copy-done = f32[15,32,8,128]{3,2,1,0:T(8,128)S(1)} copy-done((f32[15,32,8,128]{3,2,1,0:T(8,128)S(1)}, f32[15,32,8,128]{3,2,1,0:T(8,128)}, u32[]{:S(2)}) %copy-start) | copy-done | bytes 1966104
  3.6 3.6 %collective-permute-start.1 = (f32[30,8,128]{2,1,0:T(8,128)S(1)}, f32[30,8,128]{2,1,0:T(8,128)S(1)}, u32[]{:S(2)}, u32[]{:S(2)}) collective-permute-start(f32[30,8,128]{2,1,0:T(8,128)S(1)} %get-tuple-element.27), channel_id=1, source_target_pairs={{0,28},{4,0},{8,4},{12,8},{16,12},{20,16},{24,20},{28,24},{1,29},{... | collective-permute-start | bytes 368648 | tf_op jit(solution)/shard_map/ppermute | solution.py:514
  7.1 1.6 %collective-permute-start.2 = (s32[16,128]{1,0:T(8,128)S(1)}, s32[16,128]{1,0:T(8,128)S(1)}, u32[]{:S(2)}, u32[]{:S(2)}) collective-permute-start(s32[16,128]{1,0:T(8,128)S(1)} %get-tuple-element.25.info_ref.own_ref), channel_id=1, source_target_pairs={{0,32},{32,64},{64,96},{96,0},{1,33},{33,65},{65,97},{97,1},{2,34}... | collective-permute-start | bytes 24584 | tf_op jit(solution)/shard_map/ppermute | solution.py:515
  8.7 1.7 %collective-permute-start.3 = (s32[16,128]{1,0:T(8,128)S(1)}, s32[16,128]{1,0:T(8,128)S(1)}, u32[]{:S(2)}, u32[]{:S(2)}) collective-permute-start(s32[16,128]{1,0:T(8,128)S(1)} %get-tuple-element.25.info_ref.own_ref), channel_id=1, source_target_pairs={{0,96},{32,0},{64,32},{96,64},{1,97},{33,1},{65,33},{97,65},{2,98}... | collective-permute-start | bytes 24584 | tf_op jit(solution)/shard_map/ppermute | solution.py:516
  10.4 3.4 %prep.1.c_ref = f32[56,128]{1,0:T(8,128)S(1)} custom-call(f32[1,127]{1,0:T(1,128)S(1)} %bitcast.15, f32[1,128]{1,0:T(1,128)S(1)} %bitcast.16, f32[15,128]{1,0:T(8,128)S(1)} %copy-done.3), custom_call_target="tpu_custom_call" | custom-call | tf_op jit(solution)/shard_map/prep/pallas_call | solution.py:482
  13.8 5.8 %move.1 = (f32[3840,128]{1,0:T(8,128)S(1)}, f32[15,2,32,128]{3,2,1,0:T(8,128)S(1)}, f32[15,2,32,128]{3,2,1,0:T(8,128)S(1)}, f32[288,128]{1,0:T(8,128)S(1)}) custom-call(f32[15]{0:T(128)S(1)} %copy-done.4, f32[56,128]{1,0:T(8,128)S(1)} %prep.1.c_ref, f32[3840,128]{1,0:T(8,128)S(1)} %bitcast.10, f32[30,8,128]{2,1,0:T(8,128)S(1)} %collective-permute-done.hl_ref, ...), custom_call_target="tpu_custom_call" | custom-call | tf_op jit(solution)/shard_map/move/pallas_call | solution.py:523
  19.6 0.8 %slot.1 = f32[128,128]{1,0:T(8,128)S(1)} custom-call(f32[288,128]{1,0:T(8,128)S(1)} %get-tuple-element.29.ch_ref, s32[16,128]{1,0:T(8,128)S(1)} %collective-permute-done.2.top_ref, s32[16,128]{1,0:T(8,128)S(1)} %collective-permute-done.3.bot_ref, bf16[1024,1024]{1,0:T(8,128)(2,1)S(1)} %get-tuple-element.30.ot_ref), custom_call_target="tpu_custom_call" | custom-call | tf_op jit(solution)/shard_map/slot/pallas_call | solution.py:560
  20.4 1.8 %collective-permute-start.12 = (f32[15,2,32,128]{3,2,1,0:T(8,128)S(1)}, f32[15,2,32,128]{3,2,1,0:T(8,128)S(1)}, u32[]{:S(2)}, u32[]{:S(2)}) collective-permute-start(f32[15,2,32,128]{3,2,1,0:T(8,128)S(1)} %get-tuple-element.34), channel_id=1, source_target_pairs={{0,96},{32,0},{64,32},{96,64},{1,97},{33,1},{65,33},{97,65},{2,98}... | collective-permute-start | bytes 1474568 | tf_op jit(solution)/shard_map/ppermute | solution.py:567
  22.5 1.3 %collective-permute-done.4 = f32[128,128]{1,0:T(8,128)S(1)} collective-permute-done((f32[128,128]{1,0:T(8,128)S(1)}, f32[128,128]{1,0:T(8,128)S(1)}, u32[]{:S(2)}, u32[]{:S(2)}) %collective-permute-start.4) | collective-permute-done | bytes 65568 | tf_op jit(solution)/shard_map/ppermute | solution.py:466
  23.8 1.6 %collective-permute-start.5 = (f32[128,128]{1,0:T(8,128)S(1)}, f32[128,128]{1,0:T(8,128)S(1)}, u32[]{:S(2)}, u32[]{:S(2)}) collective-permute-start(f32[128,128]{1,0:T(8,128)S(1)} %add.24), channel_id=1, source_target_pairs={{0,1},{1,2},{2,3},{3,0},{4,5},{5,6},{6,7},{7,4},{8,9},{9,10},{10,1... | collective-permute-start | bytes 196616 | tf_op jit(solution)/shard_map/ppermute | solution.py:471
  25.3 2.7 %collective-permute-start.6 = (f32[128,128]{1,0:T(8,128)S(1)}, f32[128,128]{1,0:T(8,128)S(1)}, u32[]{:S(2)}, u32[]{:S(2)}) collective-permute-start(f32[128,128]{1,0:T(8,128)S(1)} %add.24), channel_id=1, source_target_pairs={{0,2},{1,3},{2,0},{3,1},{4,6},{5,7},{6,4},{7,5},{8,10},{9,11},{10,... | collective-permute-start | bytes 196616 | tf_op jit(solution)/shard_map/ppermute | solution.py:471
  28.1 1.4 %collective-permute-start.7 = (f32[128,128]{1,0:T(8,128)S(1)}, f32[128,128]{1,0:T(8,128)S(1)}, u32[]{:S(2)}, u32[]{:S(2)}) collective-permute-start(f32[128,128]{1,0:T(8,128)S(1)} %add.24), channel_id=1, source_target_pairs={{0,3},{1,0},{2,1},{3,2},{4,7},{5,4},{6,5},{7,6},{8,11},{9,8},{10,9... | collective-permute-start | bytes 196616 | tf_op jit(solution)/shard_map/ppermute | solution.py:471
  29.5 2.1 %collective-permute-done.6 = f32[128,128]{1,0:T(8,128)S(1)} collective-permute-done((f32[128,128]{1,0:T(8,128)S(1)}, f32[128,128]{1,0:T(8,128)S(1)}, u32[]{:S(2)}, u32[]{:S(2)}) %collective-permute-start.6) | collective-permute-done | bytes 65568 | tf_op jit(solution)/shard_map/ppermute | solution.py:471
  31.6 0.7 %collective-permute-done.7 = f32[128,128]{1,0:T(8,128)S(1)} collective-permute-done((f32[128,128]{1,0:T(8,128)S(1)}, f32[128,128]{1,0:T(8,128)S(1)}, u32[]{:S(2)}, u32[]{:S(2)}) %collective-permute-start.7) | collective-permute-done | bytes 65568 | tf_op jit(solution)/shard_map/ppermute | solution.py:471
  32.3 2.3 %collective-permute-start.10 = (f32[128,128]{1,0:T(8,128)S(1)}, f32[128,128]{1,0:T(8,128)S(1)}, u32[]{:S(2)}, u32[]{:S(2)}) collective-permute-start(f32[128,128]{1,0:T(8,128)S(1)} %add_add_fusion.1), channel_id=1, source_target_pairs={{0,24},{4,28},{8,0},{12,4},{16,8},{20,12},{24,16},{28,20},{1,25},{... | collective-permute-start | bytes 196616 | tf_op jit(solution)/shard_map/ppermute | solution.py:471
  34.7 1.9 %collective-permute-start.9 = (f32[128,128]{1,0:T(8,128)S(1)}, f32[128,128]{1,0:T(8,128)S(1)}, u32[]{:S(2)}, u32[]{:S(2)}) collective-permute-start(f32[128,128]{1,0:T(8,128)S(1)} %add_add_fusion.1), channel_id=1, source_target_pairs={{0,16},{4,20},{8,24},{12,28},{16,0},{20,4},{24,8},{28,12},{1,17},{... | collective-permute-start | bytes 196616 | tf_op jit(solution)/shard_map/ppermute | solution.py:471
  36.6 1.6 %meet.1 = (f32[3840,128]{1,0:T(8,128)S(1)}, f32[480,128]{1,0:T(8,128)S(1)}, f32[480,128]{1,0:T(8,128)S(1)}, f32[480,128]{1,0:T(8,128)S(1)}) custom-call(f32[15]{0:T(128)S(1)} %copy-done.4, f32[56,128]{1,0:T(8,128)S(1)} %prep.1.c_ref, f32[3840,128]{1,0:T(8,128)S(1)} %get-tuple-element.32.u_ref, f32[15,2,32,128]{3,2,1,0:T(8,128)S(1)} %collective-permute-done.11.top_ref, ...), custom_call_target="tpu_custom_call" | custom-call | tf_op jit(solution)/shard_map/meet/pallas_call | solution.py:573
  38.8 3.5 %collective-permute-start.16 = (f32[480,128]{1,0:T(8,128)S(1)}, f32[480,128]{1,0:T(8,128)S(1)}, u32[]{:S(2)}, u32[]{:S(2)}) collective-permute-start(f32[480,128]{1,0:T(8,128)S(1)} %get-tuple-element.41), channel_id=1, source_target_pairs={{0,2},{1,3},{2,0},{3,1},{4,6},{5,7},{6,4},{7,5},{8,10},{9,11},{10,... | collective-permute-start | bytes 737288 | tf_op jit(solution)/shard_map/ppermute | solution.py:589
  43.2 3.9 %collective-permute-done.13 = f32[128,128]{1,0:T(8,128)S(1)} collective-permute-done((f32[128,128]{1,0:T(8,128)S(1)}, f32[128,128]{1,0:T(8,128)S(1)}, u32[]{:S(2)}, u32[]{:S(2)}) %collective-permute-start.13) | collective-permute-done | bytes 65568 | tf_op jit(solution)/shard_map/ppermute | solution.py:466
  47.1 3.3 %collective-permute-start.14 = (f32[128,128]{1,0:T(8,128)S(1)}, f32[128,128]{1,0:T(8,128)S(1)}, u32[]{:S(2)}, u32[]{:S(2)}) collective-permute-start(f32[128,128]{1,0:T(8,128)S(1)} %add.31.a_ref), channel_id=1, source_target_pairs={{0,96},{32,64},{64,32},{96,0},{1,97},{33,65},{65,33},{97,1},{2,98}... | collective-permute-start | bytes 196616 | tf_op jit(solution)/shard_map/ppermute | solution.py:466
  50.4 0.9 %collective-permute-done.16 = f32[480,128]{1,0:T(8,128)S(1)} collective-permute-done((f32[480,128]{1,0:T(8,128)S(1)}, f32[480,128]{1,0:T(8,128)S(1)}, u32[]{:S(2)}, u32[]{:S(2)}) %collective-permute-start.16) | collective-permute-done | bytes 245792 | tf_op jit(solution)/shard_map/ppermute | solution.py:589
  51.3 3.5 %solve.1.p_ref = f32[15,32,8,128]{3,2,1,0:T(8,128)S(1)} custom-call(f32[56,128]{1,0:T(8,128)S(1)} %prep.1.c_ref, f32[15,32,8,128]{3,2,1,0:T(8,128)S(1)} %bitcast.11, f32[15,4,8,128]{3,2,1,0:T(8,128)S(1)} %bitcast.12, f32[15,4,8,128]{3,2,1,0:T(8,128)S(1)} %bitcast.13, f32[15,4,8,128]{3,2,1,0:T(8,128)S(1)} %bitcast.14, s32[8,128]{1,0:T(8,128)S(1)} %copy-done.2), custom_call_target="tpu_custom_call" | custom-call | tf_op jit(solution)/shard_map/solve/pallas_call | solution.py:599
  54.9 2.2 %share.1 = f32[15,32,8,128]{3,2,1,0:T(8,128)} custom-call(f32[15,32,8,128]{3,2,1,0:T(8,128)S(1)} %solve.1.p_ref, bf16[1024,1024]{1,0:T(8,128)(2,1)S(1)} %get-tuple-element.30.ot_ref, f32[128,128]{1,0:T(8,128)S(1)} %add.31.a_ref, f32[128,128]{1,0:T(8,128)S(1)} %collective-permute-done.14.b_ref), custom_call_target="tpu_custom_call" | custom-call | tf_op jit(solution)/shard_map/share/pallas_call | solution.py:611
  (38 shorter events, 2.6 us)
Async XLA Ops:
  0.0 10.4 %copy-start.5 = (f32[127]{0:T(128)S(1)}, f32[127]{0:T(128)}, u32[]{:S(2)}) copy-start(f32[127]{0:T(128)} %param.10) | copy-start | bytes 1528
  0.0 10.4 %copy-start.6 = (f32[128]{0:T(128)S(1)}, f32[128]{0:T(128)}, u32[]{:S(2)}) copy-start(f32[128]{0:T(128)} %param.11) | copy-start | bytes 1540
  0.0 10.4 %copy-start.3 = (f32[15,128]{1,0:T(8,128)S(1)}, f32[15,128]{1,0:T(8,128)}, u32[]{:S(2)}) copy-start(f32[15,128]{1,0:T(8,128)} %g_ref.1) | copy-start | bytes 23044
  0.0 13.8 %copy-start.4 = (f32[15]{0:T(128)S(1)}, f32[15]{0:T(128)}, u32[]{:S(2)}) copy-start(f32[15]{0:T(128)} %d_ref.3) | copy-start | bytes 184
  2.8 11.0 %copy-start.1 = (f32[15,32,8,128]{3,2,1,0:T(8,128)S(1)}, f32[15,32,8,128]{3,2,1,0:T(8,128)}, u32[]{:S(2)}) copy-start(f32[15,32,8,128]{3,2,1,0:T(8,128)} %param.8) | copy-start | bytes 5898244
  3.5 10.3 %collective-permute-start = (f32[30,8,128]{2,1,0:T(8,128)S(1)}, f32[30,8,128]{2,1,0:T(8,128)S(1)}, u32[]{:S(2)}, u32[]{:S(2)}) collective-permute-start(f32[30,8,128]{2,1,0:T(8,128)S(1)} %get-tuple-element.26), channel_id=1, source_target_pairs={{0,4},{4,8},{8,12},{12,16},{16,20},{20,24},{24,28},{28,0},{1,5},{5... | collective-permute-start | bytes 368648 | tf_op jit(solution)/shard_map/ppermute | solution.py:513
  3.6 10.2 %collective-permute-start.1 = (f32[30,8,128]{2,1,0:T(8,128)S(1)}, f32[30,8,128]{2,1,0:T(8,128)S(1)}, u32[]{:S(2)}, u32[]{:S(2)}) collective-permute-start(f32[30,8,128]{2,1,0:T(8,128)S(1)} %get-tuple-element.27), channel_id=1, source_target_pairs={{0,28},{4,0},{8,4},{12,8},{16,12},{20,16},{24,20},{28,24},{1,29},{... | collective-permute-start | bytes 368648 | tf_op jit(solution)/shard_map/ppermute | solution.py:514
  7.1 6.6 %collective-permute-start.2 = (s32[16,128]{1,0:T(8,128)S(1)}, s32[16,128]{1,0:T(8,128)S(1)}, u32[]{:S(2)}, u32[]{:S(2)}) collective-permute-start(s32[16,128]{1,0:T(8,128)S(1)} %get-tuple-element.25.info_ref.own_ref), channel_id=1, source_target_pairs={{0,32},{32,64},{64,96},{96,0},{1,33},{33,65},{65,97},{97,1},{2,34}... | collective-permute-start | bytes 24584 | tf_op jit(solution)/shard_map/ppermute | solution.py:515
  8.7 5.1 %collective-permute-start.3 = (s32[16,128]{1,0:T(8,128)S(1)}, s32[16,128]{1,0:T(8,128)S(1)}, u32[]{:S(2)}, u32[]{:S(2)}) collective-permute-start(s32[16,128]{1,0:T(8,128)S(1)} %get-tuple-element.25.info_ref.own_ref), channel_id=1, source_target_pairs={{0,96},{32,0},{64,32},{96,64},{1,97},{33,1},{65,33},{97,65},{2,98}... | collective-permute-start | bytes 24584 | tf_op jit(solution)/shard_map/ppermute | solution.py:516
  20.4 16.1 %collective-permute-start.12 = (f32[15,2,32,128]{3,2,1,0:T(8,128)S(1)}, f32[15,2,32,128]{3,2,1,0:T(8,128)S(1)}, u32[]{:S(2)}, u32[]{:S(2)}) collective-permute-start(f32[15,2,32,128]{3,2,1,0:T(8,128)S(1)} %get-tuple-element.34), channel_id=1, source_target_pairs={{0,96},{32,0},{64,32},{96,64},{1,97},{33,1},{65,33},{97,65},{2,98}... | collective-permute-start | bytes 1474568 | tf_op jit(solution)/shard_map/ppermute | solution.py:567
  22.3 14.3 %collective-permute-start.11 = (f32[15,2,32,128]{3,2,1,0:T(8,128)S(1)}, f32[15,2,32,128]{3,2,1,0:T(8,128)S(1)}, u32[]{:S(2)}, u32[]{:S(2)}) collective-permute-start(f32[15,2,32,128]{3,2,1,0:T(8,128)S(1)} %get-tuple-element.33), channel_id=1, source_target_pairs={{0,32},{32,64},{64,96},{96,0},{1,33},{33,65},{65,97},{97,1},{2,34}... | collective-permute-start | bytes 1474568 | tf_op jit(solution)/shard_map/ppermute | solution.py:558
  22.5 1.3 %collective-permute-start.4 = (f32[128,128]{1,0:T(8,128)S(1)}, f32[128,128]{1,0:T(8,128)S(1)}, u32[]{:S(2)}, u32[]{:S(2)}) collective-permute-start(f32[128,128]{1,0:T(8,128)S(1)} %slot.1), channel_id=1, source_target_pairs={{0,4},{4,0},{8,12},{12,8},{16,20},{20,16},{24,28},{28,24},{1,5},{5... | collective-permute-start | bytes 196616 | tf_op jit(solution)/shard_map/ppermute | solution.py:466
  23.8 27.6 %copy-start.2 = (s32[8,128]{1,0:T(8,128)S(1)}, s32[8,128]{1,0:T(8,128)}, u32[]{:S(2)}) copy-start(s32[8,128]{1,0:T(8,128)} %class_ref.3) | copy-start | bytes 12292
  23.8 5.7 %collective-permute-start.5 = (f32[128,128]{1,0:T(8,128)S(1)}, f32[128,128]{1,0:T(8,128)S(1)}, u32[]{:S(2)}, u32[]{:S(2)}) collective-permute-start(f32[128,128]{1,0:T(8,128)S(1)} %add.24), channel_id=1, source_target_pairs={{0,1},{1,2},{2,3},{3,0},{4,5},{5,6},{6,7},{7,4},{8,9},{9,10},{10,1... | collective-permute-start | bytes 196616 | tf_op jit(solution)/shard_map/ppermute | solution.py:471
  25.3 6.3 %collective-permute-start.6 = (f32[128,128]{1,0:T(8,128)S(1)}, f32[128,128]{1,0:T(8,128)S(1)}, u32[]{:S(2)}, u32[]{:S(2)}) collective-permute-start(f32[128,128]{1,0:T(8,128)S(1)} %add.24), channel_id=1, source_target_pairs={{0,2},{1,3},{2,0},{3,1},{4,6},{5,7},{6,4},{7,5},{8,10},{9,11},{10,... | collective-permute-start | bytes 196616 | tf_op jit(solution)/shard_map/ppermute | solution.py:471
  28.1 4.3 %collective-permute-start.7 = (f32[128,128]{1,0:T(8,128)S(1)}, f32[128,128]{1,0:T(8,128)S(1)}, u32[]{:S(2)}, u32[]{:S(2)}) collective-permute-start(f32[128,128]{1,0:T(8,128)S(1)} %add.24), channel_id=1, source_target_pairs={{0,3},{1,0},{2,1},{3,2},{4,7},{5,4},{6,5},{7,6},{8,11},{9,8},{10,9... | collective-permute-start | bytes 196616 | tf_op jit(solution)/shard_map/ppermute | solution.py:471
  32.3 10.0 %collective-permute-start.10 = (f32[128,128]{1,0:T(8,128)S(1)}, f32[128,128]{1,0:T(8,128)S(1)}, u32[]{:S(2)}, u32[]{:S(2)}) collective-permute-start(f32[128,128]{1,0:T(8,128)S(1)} %add_add_fusion.1), channel_id=1, source_target_pairs={{0,24},{4,28},{8,0},{12,4},{16,8},{20,12},{24,16},{28,20},{1,25},{... | collective-permute-start | bytes 196616 | tf_op jit(solution)/shard_map/ppermute | solution.py:471
  34.7 8.0 %collective-permute-start.8 = (f32[128,128]{1,0:T(8,128)S(1)}, f32[128,128]{1,0:T(8,128)S(1)}, u32[]{:S(2)}, u32[]{:S(2)}) collective-permute-start(f32[128,128]{1,0:T(8,128)S(1)} %add_add_fusion.1), channel_id=1, source_target_pairs={{0,8},{4,12},{8,16},{12,20},{16,24},{20,28},{24,0},{28,4},{1,9},{5... | collective-permute-start | bytes 196616 | tf_op jit(solution)/shard_map/ppermute | solution.py:471
  34.7 8.0 %collective-permute-start.9 = (f32[128,128]{1,0:T(8,128)S(1)}, f32[128,128]{1,0:T(8,128)S(1)}, u32[]{:S(2)}, u32[]{:S(2)}) collective-permute-start(f32[128,128]{1,0:T(8,128)S(1)} %add_add_fusion.1), channel_id=1, source_target_pairs={{0,16},{4,20},{8,24},{12,28},{16,0},{20,4},{24,8},{28,12},{1,17},{... | collective-permute-start | bytes 196616 | tf_op jit(solution)/shard_map/ppermute | solution.py:471
  38.1 12.2 %collective-permute-start.15 = (f32[480,128]{1,0:T(8,128)S(1)}, f32[480,128]{1,0:T(8,128)S(1)}, u32[]{:S(2)}, u32[]{:S(2)}) collective-permute-start(f32[480,128]{1,0:T(8,128)S(1)} %get-tuple-element.40), channel_id=1, source_target_pairs={{0,1},{1,2},{2,3},{3,0},{4,5},{5,6},{6,7},{7,4},{8,9},{9,10},{10,1... | collective-permute-start | bytes 737288 | tf_op jit(solution)/shard_map/ppermute | solution.py:589
  38.8 12.5 %collective-permute-start.16 = (f32[480,128]{1,0:T(8,128)S(1)}, f32[480,128]{1,0:T(8,128)S(1)}, u32[]{:S(2)}, u32[]{:S(2)}) collective-permute-start(f32[480,128]{1,0:T(8,128)S(1)} %get-tuple-element.41), channel_id=1, source_target_pairs={{0,2},{1,3},{2,0},{3,1},{4,6},{5,7},{6,4},{7,5},{8,10},{9,11},{10,... | collective-permute-start | bytes 737288 | tf_op jit(solution)/shard_map/ppermute | solution.py:589
  42.3 9.0 %collective-permute-start.17 = (f32[480,128]{1,0:T(8,128)S(1)}, f32[480,128]{1,0:T(8,128)S(1)}, u32[]{:S(2)}, u32[]{:S(2)}) collective-permute-start(f32[480,128]{1,0:T(8,128)S(1)} %get-tuple-element.42), channel_id=1, source_target_pairs={{0,3},{1,0},{2,1},{3,2},{4,7},{5,4},{6,5},{7,6},{8,11},{9,8},{10,9... | collective-permute-start | bytes 737288 | tf_op jit(solution)/shard_map/ppermute | solution.py:589
  42.7 4.3 %collective-permute-start.13 = (f32[128,128]{1,0:T(8,128)S(1)}, f32[128,128]{1,0:T(8,128)S(1)}, u32[]{:S(2)}, u32[]{:S(2)}) collective-permute-start(f32[128,128]{1,0:T(8,128)S(1)} %add_add_fusion), channel_id=1, source_target_pairs={{0,32},{32,0},{64,96},{96,64},{1,33},{33,1},{65,97},{97,65},{2,34}... | collective-permute-start | bytes 196616 | tf_op jit(solution)/shard_map/ppermute | solution.py:466
  47.1 7.8 %collective-permute-start.14 = (f32[128,128]{1,0:T(8,128)S(1)}, f32[128,128]{1,0:T(8,128)S(1)}, u32[]{:S(2)}, u32[]{:S(2)}) collective-permute-start(f32[128,128]{1,0:T(8,128)S(1)} %add.31.a_ref), channel_id=1, source_target_pairs={{0,96},{32,64},{64,32},{96,0},{1,97},{33,65},{65,33},{97,1},{2,98}... | collective-permute-start | bytes 196616 | tf_op jit(solution)/shard_map/ppermute | solution.py:466
  (1 other events, 1.5 us)

commit v5 on v4

--- a/solution.py
+++ b/solution.py
@@ -190,14 +190,14 @@
     )
 
 
-def table_kernel(class_ref, span_ref, ot_ref, info_ref):
-    info_ref[0:8, :] = class_ref[...]
-    info_ref[8:16, :] = span_ref[...]
-    for block in range(8):
-        ot_ref[LANES * block : LANES * (block + 1), :] = slot_block(info_ref, block)
-
-
-def pack_kernel(x_ref, info_ref, l_ref, r_ref):
+def pack_kernel(x_ref, class_ref, span_ref, l_ref, r_ref, ot_ref, info_ref):
+    @pl.when(pl.program_id(0) == 0)
+    def _():
+        info_ref[0:8, :] = class_ref[...]
+        info_ref[8:16, :] = span_ref[...]
+        for block in range(8):
+            ot_ref[LANES * block : LANES * (block + 1), :] = slot_block(info_ref, block)
+
     lane = lax.broadcasted_iota(jnp.int32, (2 * GROUP, ROWS, LANES), 2) // 8
     left = jnp.zeros((2 * GROUP, ROWS, LANES), F32)
     right = jnp.zeros((2 * GROUP, ROWS, LANES), F32)
@@ -492,24 +492,29 @@
     )(mixing.reshape(1, -1), relaxation.reshape(1, -1), forcing)
 
     steps = FIELDS // GROUP
-    onehot, info = pl.pallas_call(
-        table_kernel,
-        out_shape=(shaped(1024, 1024, dtype=BF16), shaped(16, LANES, dtype=jnp.int32)),
-        compiler_params=LIMIT,
-        name="table",
-    )(stay(cost_class), stay(span_map.reshape(ROWS, LANES)))
-    left, right = pl.pallas_call(
+    left, right, onehot, info = pl.pallas_call(
         pack_kernel,
         grid=(steps,),
         in_specs=[
             pl.BlockSpec((2 * GROUP, 16, ROWS, LANES), lambda f: (f, 0, 0, 0)),
-            pl.BlockSpec(memory_space=pl.ANY),
+            whole_spec((ROWS, LANES)),
+            whole_spec((ROWS, LANES)),
         ],
-        out_specs=[pl.BlockSpec((2 * GROUP, ROWS, LANES), lambda f: (f, 0, 0))] * 2,
-        out_shape=(shaped(30, ROWS, LANES), shaped(30, ROWS, LANES)),
+        out_specs=[pl.BlockSpec((2 * GROUP, ROWS, LANES), lambda f: (f, 0, 0))] * 2
+        + [whole_spec((1024, 1024)), whole_spec((16, LANES))],
+        out_shape=(
+            shaped(30, ROWS, LANES),
+            shaped(30, ROWS, LANES),
+            shaped(1024, 1024, dtype=BF16),
+            shaped(16, LANES, dtype=jnp.int32),
+        ),
         compiler_params=LIMIT,
         name="pack",
-    )(state.reshape(30, 16, ROWS, LANES), info)
+    )(
+        stay(state.reshape(30, 16, ROWS, LANES)),
+        stay(cost_class),
+        stay(span_map.reshape(ROWS, LANES)),
+    )
     from_left = lax.ppermute(right, "ey", shift("ey", 1))
     from_right = lax.ppermute(left, "ey", shift("ey", -1))
     info_top = lax.ppermute(info, "ex", shift("ex", 1))
@@ -585,9 +590,9 @@
         name="meet",
     )(diffusivity, coef, part, top, bottom)
 
-    g1, g2, g3 = [
+    g1, g3, g2 = [
         lax.ppermute(m, "lb", shift("lb", r)).reshape(FIELDS, 4, ROWS, LANES)
-        for m, r in ((m1, 1), (m2, 2), (m3, 3))
+        for m, r in ((m1, 1), (m3, 3), (m2, 2))
     ]
     *others, moved = lax.optimization_barrier((*others, moved))
     slots = sum(others, slots)

time: 57.5 us -> 57.2 us (level)
  local copies, waits for them, and re-layouts: 1.57 us -> 0.02 us
  Pallas kernels: 19.2 us -> 20.6 us
    pallas_call x1, Pallas kernels: 0.71 us -> 3.3 us  [local(): pl.pallas_call(pack_kernel, grid=(steps,), in_specs=[pl.BlockSpec((2 * GR...]
    unnamed x14 -> x12, local copies, waits for them, and re-layouts: 1.57 us -> 0.02 us
    pallas_call x1 -> x0, Pallas kernels: 1.25 us -> none  [local(): pl.pallas_call(table_kernel, out_shape=(shaped(1024, 1024, dtype=BF16), s...]
where the time goes in v5:
time: 57.2 us; the launch traced here: 56.8 us
  starting transfers between devices  27.1 us (47%)
  Pallas kernels  20.6 us (36%)
  waiting for transfers between devices  8.94 us (16%)
    ppermute x6, starting transfers between devices, ring(): lax.ppermute(value, axis, shift(axis, r))  9.94 us
    pallas_call x1, Pallas kernels, local(): pl.pallas_call(move_kernel, grid=(steps,), in_specs=[SMEM, whole_spec((56...  5.8 us
    ppermute x3, waiting for transfers between devices, swap(): return lax.ppermute(value, axis, [(i, i ^ mask) for i in range(count)])  5.15 us
    ppermute x3, starting transfers between devices, local(): lax.ppermute(m, 'lb', shift('lb', r)).reshape(FIELDS, 4, ROWS, LANES)  4.59 us
    ppermute x3, starting transfers between devices, swap(): return lax.ppermute(value, axis, [(i, i ^ mask) for i in range(count)])  3.72 us
    ppermute x1, starting transfers between devices, local(): from_right = lax.ppermute(left, 'ey', shift('ey', -1))  3.59 us
    pallas_call x1, Pallas kernels, local(): pl.pallas_call(solve_kernel, grid=(FIELDS // group,), in_specs=[SMEM, fiv...  3.53 us
    pallas_call x1, Pallas kernels, local(): pl.pallas_call(prep_kernel, out_shape=shaped(56, LANES), scratch_shapes=[...  3.4 us
  transfers between devices with their start and end apart: 18, of which 5 were waited for; matrix products, arithmetic and copies ran while one was open for 0% of the time, Pallas kernels for 15%

profile of v5, /device:TPU:0, one launch (start us, length us, event | category | flops | bytes accessed | tf_op | source)
XLA Modules:
  0.0 56.8 jit_solution(5388823239404172765)
XLA Ops:
  0.0 3.3 %pack.1 = (f32[30,8,128]{2,1,0:T(8,128)S(1)}, f32[30,8,128]{2,1,0:T(8,128)S(1)}, bf16[1024,1024]{1,0:T(8,128)(2,1)S(1)}, s32[16,128]{1,0:T(8,128)S(1)}) custom-call(f32[30,16,8,128]{3,2,1,0:T(8,128)} %bitcast.9, s32[8,128]{1,0:T(8,128)} %class_ref.3, s32[8,128]{1,0:T(8,128)} %bitcast.17), custom_call_target="tpu_custom_call" | custom-call | tf_op jit(solution)/shard_map/pack/pallas_call | solution.py:495
  3.3 3.6 %collective-permute-start.1 = (f32[30,8,128]{2,1,0:T(8,128)S(1)}, f32[30,8,128]{2,1,0:T(8,128)S(1)}, u32[]{:S(2)}, u32[]{:S(2)}) collective-permute-start(f32[30,8,128]{2,1,0:T(8,128)S(1)} %get-tuple-element.26), channel_id=1, source_target_pairs={{0,28},{4,0},{8,4},{12,8},{16,12},{20,16},{24,20},{28,24},{1,29},{... | collective-permute-start | bytes 368648 | tf_op jit(solution)/shard_map/ppermute | solution.py:519
  6.9 1.6 %collective-permute-start.2 = (s32[16,128]{1,0:T(8,128)S(1)}, s32[16,128]{1,0:T(8,128)S(1)}, u32[]{:S(2)}, u32[]{:S(2)}) collective-permute-start(s32[16,128]{1,0:T(8,128)S(1)} %get-tuple-element.27.own_ref), channel_id=1, source_target_pairs={{0,32},{32,64},{64,96},{96,0},{1,33},{33,65},{65,97},{97,1},{2,34}... | collective-permute-start | bytes 24584 | tf_op jit(solution)/shard_map/ppermute | solution.py:520
  8.5 1.7 %collective-permute-start.3 = (s32[16,128]{1,0:T(8,128)S(1)}, s32[16,128]{1,0:T(8,128)S(1)}, u32[]{:S(2)}, u32[]{:S(2)}) collective-permute-start(s32[16,128]{1,0:T(8,128)S(1)} %get-tuple-element.27.own_ref), channel_id=1, source_target_pairs={{0,96},{32,0},{64,32},{96,64},{1,97},{33,1},{65,33},{97,65},{2,98}... | collective-permute-start | bytes 24584 | tf_op jit(solution)/shard_map/ppermute | solution.py:521
  10.2 3.4 %prep.1.c_ref = f32[56,128]{1,0:T(8,128)S(1)} custom-call(f32[1,127]{1,0:T(1,128)S(1)} %bitcast.15, f32[1,128]{1,0:T(1,128)S(1)} %bitcast.16, f32[15,128]{1,0:T(8,128)S(1)} %copy-done.2), custom_call_target="tpu_custom_call" | custom-call | tf_op jit(solution)/shard_map/prep/pallas_call | solution.py:482
  13.6 5.8 %move.1 = (f32[3840,128]{1,0:T(8,128)S(1)}, f32[15,2,32,128]{3,2,1,0:T(8,128)S(1)}, f32[15,2,32,128]{3,2,1,0:T(8,128)S(1)}, f32[288,128]{1,0:T(8,128)S(1)}) custom-call(f32[15]{0:T(128)S(1)} %copy-done.3, f32[56,128]{1,0:T(8,128)S(1)} %prep.1.c_ref, f32[3840,128]{1,0:T(8,128)S(1)} %bitcast.10, f32[30,8,128]{2,1,0:T(8,128)S(1)} %collective-permute-done.hl_ref, ...), custom_call_target="tpu_custom_call" | custom-call | tf_op jit(solution)/shard_map/move/pallas_call | solution.py:528
  19.4 0.8 %slot.1 = f32[128,128]{1,0:T(8,128)S(1)} custom-call(f32[288,128]{1,0:T(8,128)S(1)} %get-tuple-element.29.ch_ref, s32[16,128]{1,0:T(8,128)S(1)} %collective-permute-done.2.top_ref, s32[16,128]{1,0:T(8,128)S(1)} %collective-permute-done.3.bot_ref, bf16[1024,1024]{1,0:T(8,128)(2,1)S(1)} %get-tuple-element.30.ot_ref), custom_call_target="tpu_custom_call" | custom-call | tf_op jit(solution)/shard_map/slot/pallas_call | solution.py:565
  20.2 1.8 %collective-permute-start.12 = (f32[15,2,32,128]{3,2,1,0:T(8,128)S(1)}, f32[15,2,32,128]{3,2,1,0:T(8,128)S(1)}, u32[]{:S(2)}, u32[]{:S(2)}) collective-permute-start(f32[15,2,32,128]{3,2,1,0:T(8,128)S(1)} %get-tuple-element.34), channel_id=1, source_target_pairs={{0,96},{32,0},{64,32},{96,64},{1,97},{33,1},{65,33},{97,65},{2,98}... | collective-permute-start | bytes 1474568 | tf_op jit(solution)/shard_map/ppermute | solution.py:572
  22.3 1.3 %collective-permute-done.4 = f32[128,128]{1,0:T(8,128)S(1)} collective-permute-done((f32[128,128]{1,0:T(8,128)S(1)}, f32[128,128]{1,0:T(8,128)S(1)}, u32[]{:S(2)}, u32[]{:S(2)}) %collective-permute-start.4) | collective-permute-done | bytes 65568 | tf_op jit(solution)/shard_map/ppermute | solution.py:466
  23.6 1.6 %collective-permute-start.5 = (f32[128,128]{1,0:T(8,128)S(1)}, f32[128,128]{1,0:T(8,128)S(1)}, u32[]{:S(2)}, u32[]{:S(2)}) collective-permute-start(f32[128,128]{1,0:T(8,128)S(1)} %add.24), channel_id=1, source_target_pairs={{0,1},{1,2},{2,3},{3,0},{4,5},{5,6},{6,7},{7,4},{8,9},{9,10},{10,1... | collective-permute-start | bytes 196616 | tf_op jit(solution)/shard_map/ppermute | solution.py:471
  25.1 2.7 %collective-permute-start.6 = (f32[128,128]{1,0:T(8,128)S(1)}, f32[128,128]{1,0:T(8,128)S(1)}, u32[]{:S(2)}, u32[]{:S(2)}) collective-permute-start(f32[128,128]{1,0:T(8,128)S(1)} %add.24), channel_id=1, source_target_pairs={{0,2},{1,3},{2,0},{3,1},{4,6},{5,7},{6,4},{7,5},{8,10},{9,11},{10,... | collective-permute-start | bytes 196616 | tf_op jit(solution)/shard_map/ppermute | solution.py:471
  27.9 1.4 %collective-permute-start.7 = (f32[128,128]{1,0:T(8,128)S(1)}, f32[128,128]{1,0:T(8,128)S(1)}, u32[]{:S(2)}, u32[]{:S(2)}) collective-permute-start(f32[128,128]{1,0:T(8,128)S(1)} %add.24), channel_id=1, source_target_pairs={{0,3},{1,0},{2,1},{3,2},{4,7},{5,4},{6,5},{7,6},{8,11},{9,8},{10,9... | collective-permute-start | bytes 196616 | tf_op jit(solution)/shard_map/ppermute | solution.py:471
  29.3 2.1 %collective-permute-done.6 = f32[128,128]{1,0:T(8,128)S(1)} collective-permute-done((f32[128,128]{1,0:T(8,128)S(1)}, f32[128,128]{1,0:T(8,128)S(1)}, u32[]{:S(2)}, u32[]{:S(2)}) %collective-permute-start.6) | collective-permute-done | bytes 65568 | tf_op jit(solution)/shard_map/ppermute | solution.py:471
  31.4 0.7 %collective-permute-done.7 = f32[128,128]{1,0:T(8,128)S(1)} collective-permute-done((f32[128,128]{1,0:T(8,128)S(1)}, f32[128,128]{1,0:T(8,128)S(1)}, u32[]{:S(2)}, u32[]{:S(2)}) %collective-permute-start.7) | collective-permute-done | bytes 65568 | tf_op jit(solution)/shard_map/ppermute | solution.py:471
  32.1 2.3 %collective-permute-start.10 = (f32[128,128]{1,0:T(8,128)S(1)}, f32[128,128]{1,0:T(8,128)S(1)}, u32[]{:S(2)}, u32[]{:S(2)}) collective-permute-start(f32[128,128]{1,0:T(8,128)S(1)} %add_add_fusion.1), channel_id=1, source_target_pairs={{0,24},{4,28},{8,0},{12,4},{16,8},{20,12},{24,16},{28,20},{1,25},{... | collective-permute-start | bytes 196616 | tf_op jit(solution)/shard_map/ppermute | solution.py:471
  34.5 1.9 %collective-permute-start.9 = (f32[128,128]{1,0:T(8,128)S(1)}, f32[128,128]{1,0:T(8,128)S(1)}, u32[]{:S(2)}, u32[]{:S(2)}) collective-permute-start(f32[128,128]{1,0:T(8,128)S(1)} %add_add_fusion.1), channel_id=1, source_target_pairs={{0,16},{4,20},{8,24},{12,28},{16,0},{20,4},{24,8},{28,12},{1,17},{... | collective-permute-start | bytes 196616 | tf_op jit(solution)/shard_map/ppermute | solution.py:471
  36.4 1.6 %meet.1 = (f32[3840,128]{1,0:T(8,128)S(1)}, f32[480,128]{1,0:T(8,128)S(1)}, f32[480,128]{1,0:T(8,128)S(1)}, f32[480,128]{1,0:T(8,128)S(1)}) custom-call(f32[15]{0:T(128)S(1)} %copy-done.3, f32[56,128]{1,0:T(8,128)S(1)} %prep.1.c_ref, f32[3840,128]{1,0:T(8,128)S(1)} %get-tuple-element.32.u_ref, f32[15,2,32,128]{3,2,1,0:T(8,128)S(1)} %collective-permute-done.11.top_ref, ...), custom_call_target="tpu_custom_call" | custom-call | tf_op jit(solution)/shard_map/meet/pallas_call | solution.py:578
  37.9 0.7 %collective-permute-start.15 = (f32[480,128]{1,0:T(8,128)S(1)}, f32[480,128]{1,0:T(8,128)S(1)}, u32[]{:S(2)}, u32[]{:S(2)}) collective-permute-start(f32[480,128]{1,0:T(8,128)S(1)} %get-tuple-element.40), channel_id=1, source_target_pairs={{0,1},{1,2},{2,3},{3,0},{4,5},{5,6},{6,7},{7,4},{8,9},{9,10},{10,1... | collective-permute-start | bytes 737288 | tf_op jit(solution)/shard_map/ppermute | solution.py:594
  38.6 3.5 %collective-permute-start.16 = (f32[480,128]{1,0:T(8,128)S(1)}, f32[480,128]{1,0:T(8,128)S(1)}, u32[]{:S(2)}, u32[]{:S(2)}) collective-permute-start(f32[480,128]{1,0:T(8,128)S(1)} %get-tuple-element.41), channel_id=1, source_target_pairs={{0,2},{1,3},{2,0},{3,1},{4,6},{5,7},{6,4},{7,5},{8,10},{9,11},{10,... | collective-permute-start | bytes 737288 | tf_op jit(solution)/shard_map/ppermute | solution.py:594
  43.0 3.9 %collective-permute-done.13 = f32[128,128]{1,0:T(8,128)S(1)} collective-permute-done((f32[128,128]{1,0:T(8,128)S(1)}, f32[128,128]{1,0:T(8,128)S(1)}, u32[]{:S(2)}, u32[]{:S(2)}) %collective-permute-start.13) | collective-permute-done | bytes 65568 | tf_op jit(solution)/shard_map/ppermute | solution.py:466
  46.9 3.3 %collective-permute-start.14 = (f32[128,128]{1,0:T(8,128)S(1)}, f32[128,128]{1,0:T(8,128)S(1)}, u32[]{:S(2)}, u32[]{:S(2)}) collective-permute-start(f32[128,128]{1,0:T(8,128)S(1)} %add.31.a_ref), channel_id=1, source_target_pairs={{0,96},{32,64},{64,32},{96,0},{1,97},{33,65},{65,33},{97,1},{2,98}... | collective-permute-start | bytes 196616 | tf_op jit(solution)/shard_map/ppermute | solution.py:466
  50.2 0.9 %collective-permute-done.16 = f32[480,128]{1,0:T(8,128)S(1)} collective-permute-done((f32[480,128]{1,0:T(8,128)S(1)}, f32[480,128]{1,0:T(8,128)S(1)}, u32[]{:S(2)}, u32[]{:S(2)}) %collective-permute-start.16) | collective-permute-done | bytes 245792 | tf_op jit(solution)/shard_map/ppermute | solution.py:594
  51.1 3.5 %solve.1.p_ref = f32[15,32,8,128]{3,2,1,0:T(8,128)S(1)} custom-call(f32[56,128]{1,0:T(8,128)S(1)} %prep.1.c_ref, f32[15,32,8,128]{3,2,1,0:T(8,128)S(1)} %bitcast.11, f32[15,4,8,128]{3,2,1,0:T(8,128)S(1)} %bitcast.12, f32[15,4,8,128]{3,2,1,0:T(8,128)S(1)} %bitcast.13, f32[15,4,8,128]{3,2,1,0:T(8,128)S(1)} %bitcast.14, s32[8,128]{1,0:T(8,128)S(1)} %copy-done.1), custom_call_target="tpu_custom_call" | custom-call | tf_op jit(solution)/shard_map/solve/pallas_call | solution.py:604
  54.7 2.2 %share.1 = f32[15,32,8,128]{3,2,1,0:T(8,128)} custom-call(f32[15,32,8,128]{3,2,1,0:T(8,128)S(1)} %solve.1.p_ref, bf16[1024,1024]{1,0:T(8,128)(2,1)S(1)} %get-tuple-element.30.ot_ref, f32[128,128]{1,0:T(8,128)S(1)} %add.31.a_ref, f32[128,128]{1,0:T(8,128)S(1)} %collective-permute-done.14.b_ref), custom_call_target="tpu_custom_call" | custom-call | tf_op jit(solution)/shard_map/share/pallas_call | solution.py:616
  (35 shorter events, 1.2 us)
Async XLA Ops:
  0.0 13.6 %copy-start = (f32[15,32,8,128]{3,2,1,0:T(8,128)S(1)}, f32[15,32,8,128]{3,2,1,0:T(8,128)}, u32[]{:S(2)}) copy-start(f32[15,32,8,128]{3,2,1,0:T(8,128)} %param.8) | copy-start | bytes 5898244
  0.0 10.2 %copy-start.4 = (f32[127]{0:T(128)S(1)}, f32[127]{0:T(128)}, u32[]{:S(2)}) copy-start(f32[127]{0:T(128)} %param.10) | copy-start | bytes 1528
  0.0 10.2 %copy-start.5 = (f32[128]{0:T(128)S(1)}, f32[128]{0:T(128)}, u32[]{:S(2)}) copy-start(f32[128]{0:T(128)} %param.11) | copy-start | bytes 1540
  0.0 10.2 %copy-start.2 = (f32[15,128]{1,0:T(8,128)S(1)}, f32[15,128]{1,0:T(8,128)}, u32[]{:S(2)}) copy-start(f32[15,128]{1,0:T(8,128)} %g_ref.1) | copy-start | bytes 23044
  0.0 13.6 %copy-start.3 = (f32[15]{0:T(128)S(1)}, f32[15]{0:T(128)}, u32[]{:S(2)}) copy-start(f32[15]{0:T(128)} %d_ref.3) | copy-start | bytes 184
  3.3 10.3 %collective-permute-start = (f32[30,8,128]{2,1,0:T(8,128)S(1)}, f32[30,8,128]{2,1,0:T(8,128)S(1)}, u32[]{:S(2)}, u32[]{:S(2)}) collective-permute-start(f32[30,8,128]{2,1,0:T(8,128)S(1)} %get-tuple-element.25), channel_id=1, source_target_pairs={{0,4},{4,8},{8,12},{12,16},{16,20},{20,24},{24,28},{28,0},{1,5},{5... | collective-permute-start | bytes 368648 | tf_op jit(solution)/shard_map/ppermute | solution.py:518
  3.3 10.3 %collective-permute-start.1 = (f32[30,8,128]{2,1,0:T(8,128)S(1)}, f32[30,8,128]{2,1,0:T(8,128)S(1)}, u32[]{:S(2)}, u32[]{:S(2)}) collective-permute-start(f32[30,8,128]{2,1,0:T(8,128)S(1)} %get-tuple-element.26), channel_id=1, source_target_pairs={{0,28},{4,0},{8,4},{12,8},{16,12},{20,16},{24,20},{28,24},{1,29},{... | collective-permute-start | bytes 368648 | tf_op jit(solution)/shard_map/ppermute | solution.py:519
  6.9 6.6 %collective-permute-start.2 = (s32[16,128]{1,0:T(8,128)S(1)}, s32[16,128]{1,0:T(8,128)S(1)}, u32[]{:S(2)}, u32[]{:S(2)}) collective-permute-start(s32[16,128]{1,0:T(8,128)S(1)} %get-tuple-element.27.own_ref), channel_id=1, source_target_pairs={{0,32},{32,64},{64,96},{96,0},{1,33},{33,65},{65,97},{97,1},{2,34}... | collective-permute-start | bytes 24584 | tf_op jit(solution)/shard_map/ppermute | solution.py:520
  8.5 5.1 %collective-permute-start.3 = (s32[16,128]{1,0:T(8,128)S(1)}, s32[16,128]{1,0:T(8,128)S(1)}, u32[]{:S(2)}, u32[]{:S(2)}) collective-permute-start(s32[16,128]{1,0:T(8,128)S(1)} %get-tuple-element.27.own_ref), channel_id=1, source_target_pairs={{0,96},{32,0},{64,32},{96,64},{1,97},{33,1},{65,33},{97,65},{2,98}... | collective-permute-start | bytes 24584 | tf_op jit(solution)/shard_map/ppermute | solution.py:521
  20.2 16.1 %collective-permute-start.12 = (f32[15,2,32,128]{3,2,1,0:T(8,128)S(1)}, f32[15,2,32,128]{3,2,1,0:T(8,128)S(1)}, u32[]{:S(2)}, u32[]{:S(2)}) collective-permute-start(f32[15,2,32,128]{3,2,1,0:T(8,128)S(1)} %get-tuple-element.34), channel_id=1, source_target_pairs={{0,96},{32,0},{64,32},{96,64},{1,97},{33,1},{65,33},{97,65},{2,98}... | collective-permute-start | bytes 1474568 | tf_op jit(solution)/shard_map/ppermute | solution.py:572
  22.1 14.3 %collective-permute-start.11 = (f32[15,2,32,128]{3,2,1,0:T(8,128)S(1)}, f32[15,2,32,128]{3,2,1,0:T(8,128)S(1)}, u32[]{:S(2)}, u32[]{:S(2)}) collective-permute-start(f32[15,2,32,128]{3,2,1,0:T(8,128)S(1)} %get-tuple-element.33), channel_id=1, source_target_pairs={{0,32},{32,64},{64,96},{96,0},{1,33},{33,65},{65,97},{97,1},{2,34}... | collective-permute-start | bytes 1474568 | tf_op jit(solution)/shard_map/ppermute | solution.py:563
  22.3 1.3 %collective-permute-start.4 = (f32[128,128]{1,0:T(8,128)S(1)}, f32[128,128]{1,0:T(8,128)S(1)}, u32[]{:S(2)}, u32[]{:S(2)}) collective-permute-start(f32[128,128]{1,0:T(8,128)S(1)} %slot.1), channel_id=1, source_target_pairs={{0,4},{4,0},{8,12},{12,8},{16,20},{20,16},{24,28},{28,24},{1,5},{5... | collective-permute-start | bytes 196616 | tf_op jit(solution)/shard_map/ppermute | solution.py:466
  23.6 27.6 %copy-start.1 = (s32[8,128]{1,0:T(8,128)S(1)}, s32[8,128]{1,0:T(8,128)}, u32[]{:S(2)}) copy-start(s32[8,128]{1,0:T(8,128)} %class_ref.3) | copy-start | bytes 12292
  23.6 5.7 %collective-permute-start.5 = (f32[128,128]{1,0:T(8,128)S(1)}, f32[128,128]{1,0:T(8,128)S(1)}, u32[]{:S(2)}, u32[]{:S(2)}) collective-permute-start(f32[128,128]{1,0:T(8,128)S(1)} %add.24), channel_id=1, source_target_pairs={{0,1},{1,2},{2,3},{3,0},{4,5},{5,6},{6,7},{7,4},{8,9},{9,10},{10,1... | collective-permute-start | bytes 196616 | tf_op jit(solution)/shard_map/ppermute | solution.py:471
  25.1 6.3 %collective-permute-start.6 = (f32[128,128]{1,0:T(8,128)S(1)}, f32[128,128]{1,0:T(8,128)S(1)}, u32[]{:S(2)}, u32[]{:S(2)}) collective-permute-start(f32[128,128]{1,0:T(8,128)S(1)} %add.24), channel_id=1, source_target_pairs={{0,2},{1,3},{2,0},{3,1},{4,6},{5,7},{6,4},{7,5},{8,10},{9,11},{10,... | collective-permute-start | bytes 196616 | tf_op jit(solution)/shard_map/ppermute | solution.py:471
  27.9 4.3 %collective-permute-start.7 = (f32[128,128]{1,0:T(8,128)S(1)}, f32[128,128]{1,0:T(8,128)S(1)}, u32[]{:S(2)}, u32[]{:S(2)}) collective-permute-start(f32[128,128]{1,0:T(8,128)S(1)} %add.24), channel_id=1, source_target_pairs={{0,3},{1,0},{2,1},{3,2},{4,7},{5,4},{6,5},{7,6},{8,11},{9,8},{10,9... | collective-permute-start | bytes 196616 | tf_op jit(solution)/shard_map/ppermute | solution.py:471
  32.1 10.0 %collective-permute-start.10 = (f32[128,128]{1,0:T(8,128)S(1)}, f32[128,128]{1,0:T(8,128)S(1)}, u32[]{:S(2)}, u32[]{:S(2)}) collective-permute-start(f32[128,128]{1,0:T(8,128)S(1)} %add_add_fusion.1), channel_id=1, source_target_pairs={{0,24},{4,28},{8,0},{12,4},{16,8},{20,12},{24,16},{28,20},{1,25},{... | collective-permute-start | bytes 196616 | tf_op jit(solution)/shard_map/ppermute | solution.py:471
  34.5 8.0 %collective-permute-start.8 = (f32[128,128]{1,0:T(8,128)S(1)}, f32[128,128]{1,0:T(8,128)S(1)}, u32[]{:S(2)}, u32[]{:S(2)}) collective-permute-start(f32[128,128]{1,0:T(8,128)S(1)} %add_add_fusion.1), channel_id=1, source_target_pairs={{0,8},{4,12},{8,16},{12,20},{16,24},{20,28},{24,0},{28,4},{1,9},{5... | collective-permute-start | bytes 196616 | tf_op jit(solution)/shard_map/ppermute | solution.py:471
  34.5 8.0 %collective-permute-start.9 = (f32[128,128]{1,0:T(8,128)S(1)}, f32[128,128]{1,0:T(8,128)S(1)}, u32[]{:S(2)}, u32[]{:S(2)}) collective-permute-start(f32[128,128]{1,0:T(8,128)S(1)} %add_add_fusion.1), channel_id=1, source_target_pairs={{0,16},{4,20},{8,24},{12,28},{16,0},{20,4},{24,8},{28,12},{1,17},{... | collective-permute-start | bytes 196616 | tf_op jit(solution)/shard_map/ppermute | solution.py:471
  37.9 12.3 %collective-permute-start.15 = (f32[480,128]{1,0:T(8,128)S(1)}, f32[480,128]{1,0:T(8,128)S(1)}, u32[]{:S(2)}, u32[]{:S(2)}) collective-permute-start(f32[480,128]{1,0:T(8,128)S(1)} %get-tuple-element.40), channel_id=1, source_target_pairs={{0,1},{1,2},{2,3},{3,0},{4,5},{5,6},{6,7},{7,4},{8,9},{9,10},{10,1... | collective-permute-start | bytes 737288 | tf_op jit(solution)/shard_map/ppermute | solution.py:594
  38.6 12.5 %collective-permute-start.16 = (f32[480,128]{1,0:T(8,128)S(1)}, f32[480,128]{1,0:T(8,128)S(1)}, u32[]{:S(2)}, u32[]{:S(2)}) collective-permute-start(f32[480,128]{1,0:T(8,128)S(1)} %get-tuple-element.41), channel_id=1, source_target_pairs={{0,2},{1,3},{2,0},{3,1},{4,6},{5,7},{6,4},{7,5},{8,10},{9,11},{10,... | collective-permute-start | bytes 737288 | tf_op jit(solution)/shard_map/ppermute | solution.py:594
  42.1 9.0 %collective-permute-start.17 = (f32[480,128]{1,0:T(8,128)S(1)}, f32[480,128]{1,0:T(8,128)S(1)}, u32[]{:S(2)}, u32[]{:S(2)}) collective-permute-start(f32[480,128]{1,0:T(8,128)S(1)} %get-tuple-element.42), channel_id=1, source_target_pairs={{0,3},{1,0},{2,1},{3,2},{4,7},{5,4},{6,5},{7,6},{8,11},{9,8},{10,9... | collective-permute-start | bytes 737288 | tf_op jit(solution)/shard_map/ppermute | solution.py:594
  42.6 4.3 %collective-permute-start.13 = (f32[128,128]{1,0:T(8,128)S(1)}, f32[128,128]{1,0:T(8,128)S(1)}, u32[]{:S(2)}, u32[]{:S(2)}) collective-permute-start(f32[128,128]{1,0:T(8,128)S(1)} %add_add_fusion), channel_id=1, source_target_pairs={{0,32},{32,0},{64,96},{96,64},{1,33},{33,1},{65,97},{97,65},{2,34}... | collective-permute-start | bytes 196616 | tf_op jit(solution)/shard_map/ppermute | solution.py:466
  46.9 7.7 %collective-permute-start.14 = (f32[128,128]{1,0:T(8,128)S(1)}, f32[128,128]{1,0:T(8,128)S(1)}, u32[]{:S(2)}, u32[]{:S(2)}) collective-permute-start(f32[128,128]{1,0:T(8,128)S(1)} %add.31.a_ref), channel_id=1, source_target_pairs={{0,96},{32,64},{64,32},{96,0},{1,97},{33,65},{65,33},{97,1},{2,98}... | collective-permute-start | bytes 196616 | tf_op jit(solution)/shard_map/ppermute | solution.py:466

commit v6 on v5

--- a/solution.py
+++ b/solution.py
@@ -590,9 +590,9 @@
         name="meet",
     )(diffusivity, coef, part, top, bottom)
 
-    g1, g3, g2 = [
+    g2, g1, g3 = [
         lax.ppermute(m, "lb", shift("lb", r)).reshape(FIELDS, 4, ROWS, LANES)
-        for m, r in ((m1, 1), (m3, 3), (m2, 2))
+        for m, r in ((m2, 2), (m1, 1), (m3, 3))
     ]
     *others, moved = lax.optimization_barrier((*others, moved))
     slots = sum(others, slots)

time: 57.2 us -> 57.2 us (level)
  no operation moved by 1% of the time
where the time goes in v6:
time: 57.2 us; the launch traced here: 56.8 us
  starting transfers between devices  27.1 us (47%)
  Pallas kernels  20.6 us (36%)
  waiting for transfers between devices  8.94 us (16%)
    ppermute x6, starting transfers between devices, ring(): lax.ppermute(value, axis, shift(axis, r))  9.94 us
    pallas_call x1, Pallas kernels, local(): pl.pallas_call(move_kernel, grid=(steps,), in_specs=[SMEM, whole_spec((56...  5.8 us
    ppermute x3, waiting for transfers between devices, swap(): return lax.ppermute(value, axis, [(i, i ^ mask) for i in range(count)])  5.15 us
    ppermute x3, starting transfers between devices, local(): lax.ppermute(m, 'lb', shift('lb', r)).reshape(FIELDS, 4, ROWS, LANES)  4.59 us
    ppermute x3, starting transfers between devices, swap(): return lax.ppermute(value, axis, [(i, i ^ mask) for i in range(count)])  3.72 us
    ppermute x1, starting transfers between devices, local(): from_right = lax.ppermute(left, 'ey', shift('ey', -1))  3.59 us
    pallas_call x1, Pallas kernels, local(): pl.pallas_call(solve_kernel, grid=(FIELDS // group,), in_specs=[SMEM, fiv...  3.53 us
    pallas_call x1, Pallas kernels, local(): pl.pallas_call(prep_kernel, out_shape=shaped(56, LANES), scratch_shapes=[...  3.4 us
  transfers between devices with their start and end apart: 18, of which 5 were waited for; matrix products, arithmetic and copies ran while one was open for 0% of the time, Pallas kernels for 15%

profile of v6, /device:TPU:0, one launch (start us, length us, event | category | flops | bytes accessed | tf_op | source)
XLA Modules:
  0.0 56.8 jit_solution(5388823239404172765)
XLA Ops:
  0.0 3.3 %pack.1 = (f32[30,8,128]{2,1,0:T(8,128)S(1)}, f32[30,8,128]{2,1,0:T(8,128)S(1)}, bf16[1024,1024]{1,0:T(8,128)(2,1)S(1)}, s32[16,128]{1,0:T(8,128)S(1)}) custom-call(f32[30,16,8,128]{3,2,1,0:T(8,128)} %bitcast.9, s32[8,128]{1,0:T(8,128)} %class_ref.3, s32[8,128]{1,0:T(8,128)} %bitcast.17), custom_call_target="tpu_custom_call" | custom-call | tf_op jit(solution)/shard_map/pack/pallas_call | solution.py:495
  3.3 3.6 %collective-permute-start.1 = (f32[30,8,128]{2,1,0:T(8,128)S(1)}, f32[30,8,128]{2,1,0:T(8,128)S(1)}, u32[]{:S(2)}, u32[]{:S(2)}) collective-permute-start(f32[30,8,128]{2,1,0:T(8,128)S(1)} %get-tuple-element.26), channel_id=1, source_target_pairs={{0,28},{4,0},{8,4},{12,8},{16,12},{20,16},{24,20},{28,24},{1,29},{... | collective-permute-start | bytes 368648 | tf_op jit(solution)/shard_map/ppermute | solution.py:519
  6.9 1.6 %collective-permute-start.2 = (s32[16,128]{1,0:T(8,128)S(1)}, s32[16,128]{1,0:T(8,128)S(1)}, u32[]{:S(2)}, u32[]{:S(2)}) collective-permute-start(s32[16,128]{1,0:T(8,128)S(1)} %get-tuple-element.27.own_ref), channel_id=1, source_target_pairs={{0,32},{32,64},{64,96},{96,0},{1,33},{33,65},{65,97},{97,1},{2,34}... | collective-permute-start | bytes 24584 | tf_op jit(solution)/shard_map/ppermute | solution.py:520
  8.5 1.7 %collective-permute-start.3 = (s32[16,128]{1,0:T(8,128)S(1)}, s32[16,128]{1,0:T(8,128)S(1)}, u32[]{:S(2)}, u32[]{:S(2)}) collective-permute-start(s32[16,128]{1,0:T(8,128)S(1)} %get-tuple-element.27.own_ref), channel_id=1, source_target_pairs={{0,96},{32,0},{64,32},{96,64},{1,97},{33,1},{65,33},{97,65},{2,98}... | collective-permute-start | bytes 24584 | tf_op jit(solution)/shard_map/ppermute | solution.py:521
  10.2 3.4 %prep.1.c_ref = f32[56,128]{1,0:T(8,128)S(1)} custom-call(f32[1,127]{1,0:T(1,128)S(1)} %bitcast.15, f32[1,128]{1,0:T(1,128)S(1)} %bitcast.16, f32[15,128]{1,0:T(8,128)S(1)} %copy-done.2), custom_call_target="tpu_custom_call" | custom-call | tf_op jit(solution)/shard_map/prep/pallas_call | solution.py:482
  13.6 5.8 %move.1 = (f32[3840,128]{1,0:T(8,128)S(1)}, f32[15,2,32,128]{3,2,1,0:T(8,128)S(1)}, f32[15,2,32,128]{3,2,1,0:T(8,128)S(1)}, f32[288,128]{1,0:T(8,128)S(1)}) custom-call(f32[15]{0:T(128)S(1)} %copy-done.3, f32[56,128]{1,0:T(8,128)S(1)} %prep.1.c_ref, f32[3840,128]{1,0:T(8,128)S(1)} %bitcast.10, f32[30,8,128]{2,1,0:T(8,128)S(1)} %collective-permute-done.hl_ref, ...), custom_call_target="tpu_custom_call" | custom-call | tf_op jit(solution)/shard_map/move/pallas_call | solution.py:528
  19.4 0.8 %slot.1 = f32[128,128]{1,0:T(8,128)S(1)} custom-call(f32[288,128]{1,0:T(8,128)S(1)} %get-tuple-element.29.ch_ref, s32[16,128]{1,0:T(8,128)S(1)} %collective-permute-done.2.top_ref, s32[16,128]{1,0:T(8,128)S(1)} %collective-permute-done.3.bot_ref, bf16[1024,1024]{1,0:T(8,128)(2,1)S(1)} %get-tuple-element.30.ot_ref), custom_call_target="tpu_custom_call" | custom-call | tf_op jit(solution)/shard_map/slot/pallas_call | solution.py:565
  20.2 1.8 %collective-permute-start.12 = (f32[15,2,32,128]{3,2,1,0:T(8,128)S(1)}, f32[15,2,32,128]{3,2,1,0:T(8,128)S(1)}, u32[]{:S(2)}, u32[]{:S(2)}) collective-permute-start(f32[15,2,32,128]{3,2,1,0:T(8,128)S(1)} %get-tuple-element.34), channel_id=1, source_target_pairs={{0,96},{32,0},{64,32},{96,64},{1,97},{33,1},{65,33},{97,65},{2,98}... | collective-permute-start | bytes 1474568 | tf_op jit(solution)/shard_map/ppermute | solution.py:572
  22.3 1.3 %collective-permute-done.4 = f32[128,128]{1,0:T(8,128)S(1)} collective-permute-done((f32[128,128]{1,0:T(8,128)S(1)}, f32[128,128]{1,0:T(8,128)S(1)}, u32[]{:S(2)}, u32[]{:S(2)}) %collective-permute-start.4) | collective-permute-done | bytes 65568 | tf_op jit(solution)/shard_map/ppermute | solution.py:466
  23.6 1.6 %collective-permute-start.5 = (f32[128,128]{1,0:T(8,128)S(1)}, f32[128,128]{1,0:T(8,128)S(1)}, u32[]{:S(2)}, u32[]{:S(2)}) collective-permute-start(f32[128,128]{1,0:T(8,128)S(1)} %add.24), channel_id=1, source_target_pairs={{0,1},{1,2},{2,3},{3,0},{4,5},{5,6},{6,7},{7,4},{8,9},{9,10},{10,1... | collective-permute-start | bytes 196616 | tf_op jit(solution)/shard_map/ppermute | solution.py:471
  25.1 2.7 %collective-permute-start.6 = (f32[128,128]{1,0:T(8,128)S(1)}, f32[128,128]{1,0:T(8,128)S(1)}, u32[]{:S(2)}, u32[]{:S(2)}) collective-permute-start(f32[128,128]{1,0:T(8,128)S(1)} %add.24), channel_id=1, source_target_pairs={{0,2},{1,3},{2,0},{3,1},{4,6},{5,7},{6,4},{7,5},{8,10},{9,11},{10,... | collective-permute-start | bytes 196616 | tf_op jit(solution)/shard_map/ppermute | solution.py:471
  27.9 1.4 %collective-permute-start.7 = (f32[128,128]{1,0:T(8,128)S(1)}, f32[128,128]{1,0:T(8,128)S(1)}, u32[]{:S(2)}, u32[]{:S(2)}) collective-permute-start(f32[128,128]{1,0:T(8,128)S(1)} %add.24), channel_id=1, source_target_pairs={{0,3},{1,0},{2,1},{3,2},{4,7},{5,4},{6,5},{7,6},{8,11},{9,8},{10,9... | collective-permute-start | bytes 196616 | tf_op jit(solution)/shard_map/ppermute | solution.py:471
  29.3 2.1 %collective-permute-done.6 = f32[128,128]{1,0:T(8,128)S(1)} collective-permute-done((f32[128,128]{1,0:T(8,128)S(1)}, f32[128,128]{1,0:T(8,128)S(1)}, u32[]{:S(2)}, u32[]{:S(2)}) %collective-permute-start.6) | collective-permute-done | bytes 65568 | tf_op jit(solution)/shard_map/ppermute | solution.py:471
  31.4 0.7 %collective-permute-done.7 = f32[128,128]{1,0:T(8,128)S(1)} collective-permute-done((f32[128,128]{1,0:T(8,128)S(1)}, f32[128,128]{1,0:T(8,128)S(1)}, u32[]{:S(2)}, u32[]{:S(2)}) %collective-permute-start.7) | collective-permute-done | bytes 65568 | tf_op jit(solution)/shard_map/ppermute | solution.py:471
  32.1 2.3 %collective-permute-start.10 = (f32[128,128]{1,0:T(8,128)S(1)}, f32[128,128]{1,0:T(8,128)S(1)}, u32[]{:S(2)}, u32[]{:S(2)}) collective-permute-start(f32[128,128]{1,0:T(8,128)S(1)} %add_add_fusion.1), channel_id=1, source_target_pairs={{0,24},{4,28},{8,0},{12,4},{16,8},{20,12},{24,16},{28,20},{1,25},{... | collective-permute-start | bytes 196616 | tf_op jit(solution)/shard_map/ppermute | solution.py:471
  34.5 1.9 %collective-permute-start.9 = (f32[128,128]{1,0:T(8,128)S(1)}, f32[128,128]{1,0:T(8,128)S(1)}, u32[]{:S(2)}, u32[]{:S(2)}) collective-permute-start(f32[128,128]{1,0:T(8,128)S(1)} %add_add_fusion.1), channel_id=1, source_target_pairs={{0,16},{4,20},{8,24},{12,28},{16,0},{20,4},{24,8},{28,12},{1,17},{... | collective-permute-start | bytes 196616 | tf_op jit(solution)/shard_map/ppermute | solution.py:471
  36.4 1.6 %meet.1 = (f32[3840,128]{1,0:T(8,128)S(1)}, f32[480,128]{1,0:T(8,128)S(1)}, f32[480,128]{1,0:T(8,128)S(1)}, f32[480,128]{1,0:T(8,128)S(1)}) custom-call(f32[15]{0:T(128)S(1)} %copy-done.3, f32[56,128]{1,0:T(8,128)S(1)} %prep.1.c_ref, f32[3840,128]{1,0:T(8,128)S(1)} %get-tuple-element.32.u_ref, f32[15,2,32,128]{3,2,1,0:T(8,128)S(1)} %collective-permute-done.11.top_ref, ...), custom_call_target="tpu_custom_call" | custom-call | tf_op jit(solution)/shard_map/meet/pallas_call | solution.py:578
  37.9 0.7 %collective-permute-start.15 = (f32[480,128]{1,0:T(8,128)S(1)}, f32[480,128]{1,0:T(8,128)S(1)}, u32[]{:S(2)}, u32[]{:S(2)}) collective-permute-start(f32[480,128]{1,0:T(8,128)S(1)} %get-tuple-element.40), channel_id=1, source_target_pairs={{0,1},{1,2},{2,3},{3,0},{4,5},{5,6},{6,7},{7,4},{8,9},{9,10},{10,1... | collective-permute-start | bytes 737288 | tf_op jit(solution)/shard_map/ppermute | solution.py:594
  38.6 3.5 %collective-permute-start.16 = (f32[480,128]{1,0:T(8,128)S(1)}, f32[480,128]{1,0:T(8,128)S(1)}, u32[]{:S(2)}, u32[]{:S(2)}) collective-permute-start(f32[480,128]{1,0:T(8,128)S(1)} %get-tuple-element.41), channel_id=1, source_target_pairs={{0,2},{1,3},{2,0},{3,1},{4,6},{5,7},{6,4},{7,5},{8,10},{9,11},{10,... | collective-permute-start | bytes 737288 | tf_op jit(solution)/shard_map/ppermute | solution.py:594
  43.0 3.9 %collective-permute-done.13 = f32[128,128]{1,0:T(8,128)S(1)} collective-permute-done((f32[128,128]{1,0:T(8,128)S(1)}, f32[128,128]{1,0:T(8,128)S(1)}, u32[]{:S(2)}, u32[]{:S(2)}) %collective-permute-start.13) | collective-permute-done | bytes 65568 | tf_op jit(solution)/shard_map/ppermute | solution.py:466
  46.9 3.3 %collective-permute-start.14 = (f32[128,128]{1,0:T(8,128)S(1)}, f32[128,128]{1,0:T(8,128)S(1)}, u32[]{:S(2)}, u32[]{:S(2)}) collective-permute-start(f32[128,128]{1,0:T(8,128)S(1)} %add.31.a_ref), channel_id=1, source_target_pairs={{0,96},{32,64},{64,32},{96,0},{1,97},{33,65},{65,33},{97,1},{2,98}... | collective-permute-start | bytes 196616 | tf_op jit(solution)/shard_map/ppermute | solution.py:466
  50.2 0.9 %collective-permute-done.16 = f32[480,128]{1,0:T(8,128)S(1)} collective-permute-done((f32[480,128]{1,0:T(8,128)S(1)}, f32[480,128]{1,0:T(8,128)S(1)}, u32[]{:S(2)}, u32[]{:S(2)}) %collective-permute-start.16) | collective-permute-done | bytes 245792 | tf_op jit(solution)/shard_map/ppermute | solution.py:594
  51.1 3.5 %solve.1.p_ref = f32[15,32,8,128]{3,2,1,0:T(8,128)S(1)} custom-call(f32[56,128]{1,0:T(8,128)S(1)} %prep.1.c_ref, f32[15,32,8,128]{3,2,1,0:T(8,128)S(1)} %bitcast.11, f32[15,4,8,128]{3,2,1,0:T(8,128)S(1)} %bitcast.12, f32[15,4,8,128]{3,2,1,0:T(8,128)S(1)} %bitcast.13, f32[15,4,8,128]{3,2,1,0:T(8,128)S(1)} %bitcast.14, s32[8,128]{1,0:T(8,128)S(1)} %copy-done.1), custom_call_target="tpu_custom_call" | custom-call | tf_op jit(solution)/shard_map/solve/pallas_call | solution.py:604
  54.7 2.2 %share.1 = f32[15,32,8,128]{3,2,1,0:T(8,128)} custom-call(f32[15,32,8,128]{3,2,1,0:T(8,128)S(1)} %solve.1.p_ref, bf16[1024,1024]{1,0:T(8,128)(2,1)S(1)} %get-tuple-element.30.ot_ref, f32[128,128]{1,0:T(8,128)S(1)} %add.31.a_ref, f32[128,128]{1,0:T(8,128)S(1)} %collective-permute-done.14.b_ref), custom_call_target="tpu_custom_call" | custom-call | tf_op jit(solution)/shard_map/share/pallas_call | solution.py:616
  (35 shorter events, 1.2 us)
Async XLA Ops:
  0.0 13.6 %copy-start = (f32[15,32,8,128]{3,2,1,0:T(8,128)S(1)}, f32[15,32,8,128]{3,2,1,0:T(8,128)}, u32[]{:S(2)}) copy-start(f32[15,32,8,128]{3,2,1,0:T(8,128)} %param.8) | copy-start | bytes 5898244
  0.0 10.2 %copy-start.4 = (f32[127]{0:T(128)S(1)}, f32[127]{0:T(128)}, u32[]{:S(2)}) copy-start(f32[127]{0:T(128)} %param.10) | copy-start | bytes 1528
  0.0 10.2 %copy-start.5 = (f32[128]{0:T(128)S(1)}, f32[128]{0:T(128)}, u32[]{:S(2)}) copy-start(f32[128]{0:T(128)} %param.11) | copy-start | bytes 1540
  0.0 10.2 %copy-start.2 = (f32[15,128]{1,0:T(8,128)S(1)}, f32[15,128]{1,0:T(8,128)}, u32[]{:S(2)}) copy-start(f32[15,128]{1,0:T(8,128)} %g_ref.1) | copy-start | bytes 23044
  0.0 13.6 %copy-start.3 = (f32[15]{0:T(128)S(1)}, f32[15]{0:T(128)}, u32[]{:S(2)}) copy-start(f32[15]{0:T(128)} %d_ref.3) | copy-start | bytes 184
  3.3 10.3 %collective-permute-start = (f32[30,8,128]{2,1,0:T(8,128)S(1)}, f32[30,8,128]{2,1,0:T(8,128)S(1)}, u32[]{:S(2)}, u32[]{:S(2)}) collective-permute-start(f32[30,8,128]{2,1,0:T(8,128)S(1)} %get-tuple-element.25), channel_id=1, source_target_pairs={{0,4},{4,8},{8,12},{12,16},{16,20},{20,24},{24,28},{28,0},{1,5},{5... | collective-permute-start | bytes 368648 | tf_op jit(solution)/shard_map/ppermute | solution.py:518
  3.3 10.3 %collective-permute-start.1 = (f32[30,8,128]{2,1,0:T(8,128)S(1)}, f32[30,8,128]{2,1,0:T(8,128)S(1)}, u32[]{:S(2)}, u32[]{:S(2)}) collective-permute-start(f32[30,8,128]{2,1,0:T(8,128)S(1)} %get-tuple-element.26), channel_id=1, source_target_pairs={{0,28},{4,0},{8,4},{12,8},{16,12},{20,16},{24,20},{28,24},{1,29},{... | collective-permute-start | bytes 368648 | tf_op jit(solution)/shard_map/ppermute | solution.py:519
  6.9 6.6 %collective-permute-start.2 = (s32[16,128]{1,0:T(8,128)S(1)}, s32[16,128]{1,0:T(8,128)S(1)}, u32[]{:S(2)}, u32[]{:S(2)}) collective-permute-start(s32[16,128]{1,0:T(8,128)S(1)} %get-tuple-element.27.own_ref), channel_id=1, source_target_pairs={{0,32},{32,64},{64,96},{96,0},{1,33},{33,65},{65,97},{97,1},{2,34}... | collective-permute-start | bytes 24584 | tf_op jit(solution)/shard_map/ppermute | solution.py:520
  8.5 5.1 %collective-permute-start.3 = (s32[16,128]{1,0:T(8,128)S(1)}, s32[16,128]{1,0:T(8,128)S(1)}, u32[]{:S(2)}, u32[]{:S(2)}) collective-permute-start(s32[16,128]{1,0:T(8,128)S(1)} %get-tuple-element.27.own_ref), channel_id=1, source_target_pairs={{0,96},{32,0},{64,32},{96,64},{1,97},{33,1},{65,33},{97,65},{2,98}... | collective-permute-start | bytes 24584 | tf_op jit(solution)/shard_map/ppermute | solution.py:521
  20.2 16.1 %collective-permute-start.12 = (f32[15,2,32,128]{3,2,1,0:T(8,128)S(1)}, f32[15,2,32,128]{3,2,1,0:T(8,128)S(1)}, u32[]{:S(2)}, u32[]{:S(2)}) collective-permute-start(f32[15,2,32,128]{3,2,1,0:T(8,128)S(1)} %get-tuple-element.34), channel_id=1, source_target_pairs={{0,96},{32,0},{64,32},{96,64},{1,97},{33,1},{65,33},{97,65},{2,98}... | collective-permute-start | bytes 1474568 | tf_op jit(solution)/shard_map/ppermute | solution.py:572
  22.1 14.3 %collective-permute-start.11 = (f32[15,2,32,128]{3,2,1,0:T(8,128)S(1)}, f32[15,2,32,128]{3,2,1,0:T(8,128)S(1)}, u32[]{:S(2)}, u32[]{:S(2)}) collective-permute-start(f32[15,2,32,128]{3,2,1,0:T(8,128)S(1)} %get-tuple-element.33), channel_id=1, source_target_pairs={{0,32},{32,64},{64,96},{96,0},{1,33},{33,65},{65,97},{97,1},{2,34}... | collective-permute-start | bytes 1474568 | tf_op jit(solution)/shard_map/ppermute | solution.py:563
  22.3 1.3 %collective-permute-start.4 = (f32[128,128]{1,0:T(8,128)S(1)}, f32[128,128]{1,0:T(8,128)S(1)}, u32[]{:S(2)}, u32[]{:S(2)}) collective-permute-start(f32[128,128]{1,0:T(8,128)S(1)} %slot.1), channel_id=1, source_target_pairs={{0,4},{4,0},{8,12},{12,8},{16,20},{20,16},{24,28},{28,24},{1,5},{5... | collective-permute-start | bytes 196616 | tf_op jit(solution)/shard_map/ppermute | solution.py:466
  23.6 27.6 %copy-start.1 = (s32[8,128]{1,0:T(8,128)S(1)}, s32[8,128]{1,0:T(8,128)}, u32[]{:S(2)}) copy-start(s32[8,128]{1,0:T(8,128)} %class_ref.3) | copy-start | bytes 12292
  23.6 5.7 %collective-permute-start.5 = (f32[128,128]{1,0:T(8,128)S(1)}, f32[128,128]{1,0:T(8,128)S(1)}, u32[]{:S(2)}, u32[]{:S(2)}) collective-permute-start(f32[128,128]{1,0:T(8,128)S(1)} %add.24), channel_id=1, source_target_pairs={{0,1},{1,2},{2,3},{3,0},{4,5},{5,6},{6,7},{7,4},{8,9},{9,10},{10,1... | collective-permute-start | bytes 196616 | tf_op jit(solution)/shard_map/ppermute | solution.py:471
  25.1 6.3 %collective-permute-start.6 = (f32[128,128]{1,0:T(8,128)S(1)}, f32[128,128]{1,0:T(8,128)S(1)}, u32[]{:S(2)}, u32[]{:S(2)}) collective-permute-start(f32[128,128]{1,0:T(8,128)S(1)} %add.24), channel_id=1, source_target_pairs={{0,2},{1,3},{2,0},{3,1},{4,6},{5,7},{6,4},{7,5},{8,10},{9,11},{10,... | collective-permute-start | bytes 196616 | tf_op jit(solution)/shard_map/ppermute | solution.py:471
  27.9 4.3 %collective-permute-start.7 = (f32[128,128]{1,0:T(8,128)S(1)}, f32[128,128]{1,0:T(8,128)S(1)}, u32[]{:S(2)}, u32[]{:S(2)}) collective-permute-start(f32[128,128]{1,0:T(8,128)S(1)} %add.24), channel_id=1, source_target_pairs={{0,3},{1,0},{2,1},{3,2},{4,7},{5,4},{6,5},{7,6},{8,11},{9,8},{10,9... | collective-permute-start | bytes 196616 | tf_op jit(solution)/shard_map/ppermute | solution.py:471
  32.1 10.0 %collective-permute-start.10 = (f32[128,128]{1,0:T(8,128)S(1)}, f32[128,128]{1,0:T(8,128)S(1)}, u32[]{:S(2)}, u32[]{:S(2)}) collective-permute-start(f32[128,128]{1,0:T(8,128)S(1)} %add_add_fusion.1), channel_id=1, source_target_pairs={{0,24},{4,28},{8,0},{12,4},{16,8},{20,12},{24,16},{28,20},{1,25},{... | collective-permute-start | bytes 196616 | tf_op jit(solution)/shard_map/ppermute | solution.py:471
  34.5 8.0 %collective-permute-start.8 = (f32[128,128]{1,0:T(8,128)S(1)}, f32[128,128]{1,0:T(8,128)S(1)}, u32[]{:S(2)}, u32[]{:S(2)}) collective-permute-start(f32[128,128]{1,0:T(8,128)S(1)} %add_add_fusion.1), channel_id=1, source_target_pairs={{0,8},{4,12},{8,16},{12,20},{16,24},{20,28},{24,0},{28,4},{1,9},{5... | collective-permute-start | bytes 196616 | tf_op jit(solution)/shard_map/ppermute | solution.py:471
  34.5 8.0 %collective-permute-start.9 = (f32[128,128]{1,0:T(8,128)S(1)}, f32[128,128]{1,0:T(8,128)S(1)}, u32[]{:S(2)}, u32[]{:S(2)}) collective-permute-start(f32[128,128]{1,0:T(8,128)S(1)} %add_add_fusion.1), channel_id=1, source_target_pairs={{0,16},{4,20},{8,24},{12,28},{16,0},{20,4},{24,8},{28,12},{1,17},{... | collective-permute-start | bytes 196616 | tf_op jit(solution)/shard_map/ppermute | solution.py:471
  37.9 12.3 %collective-permute-start.15 = (f32[480,128]{1,0:T(8,128)S(1)}, f32[480,128]{1,0:T(8,128)S(1)}, u32[]{:S(2)}, u32[]{:S(2)}) collective-permute-start(f32[480,128]{1,0:T(8,128)S(1)} %get-tuple-element.40), channel_id=1, source_target_pairs={{0,1},{1,2},{2,3},{3,0},{4,5},{5,6},{6,7},{7,4},{8,9},{9,10},{10,1... | collective-permute-start | bytes 737288 | tf_op jit(solution)/shard_map/ppermute | solution.py:594
  38.6 12.5 %collective-permute-start.16 = (f32[480,128]{1,0:T(8,128)S(1)}, f32[480,128]{1,0:T(8,128)S(1)}, u32[]{:S(2)}, u32[]{:S(2)}) collective-permute-start(f32[480,128]{1,0:T(8,128)S(1)} %get-tuple-element.41), channel_id=1, source_target_pairs={{0,2},{1,3},{2,0},{3,1},{4,6},{5,7},{6,4},{7,5},{8,10},{9,11},{10,... | collective-permute-start | bytes 737288 | tf_op jit(solution)/shard_map/ppermute | solution.py:594
  42.1 9.0 %collective-permute-start.17 = (f32[480,128]{1,0:T(8,128)S(1)}, f32[480,128]{1,0:T(8,128)S(1)}, u32[]{:S(2)}, u32[]{:S(2)}) collective-permute-start(f32[480,128]{1,0:T(8,128)S(1)} %get-tuple-element.42), channel_id=1, source_target_pairs={{0,3},{1,0},{2,1},{3,2},{4,7},{5,4},{6,5},{7,6},{8,11},{9,8},{10,9... | collective-permute-start | bytes 737288 | tf_op jit(solution)/shard_map/ppermute | solution.py:594
  42.6 4.3 %collective-permute-start.13 = (f32[128,128]{1,0:T(8,128)S(1)}, f32[128,128]{1,0:T(8,128)S(1)}, u32[]{:S(2)}, u32[]{:S(2)}) collective-permute-start(f32[128,128]{1,0:T(8,128)S(1)} %add_add_fusion), channel_id=1, source_target_pairs={{0,32},{32,0},{64,96},{96,64},{1,33},{33,1},{65,97},{97,65},{2,34}... | collective-permute-start | bytes 196616 | tf_op jit(solution)/shard_map/ppermute | solution.py:466
  46.9 7.7 %collective-permute-start.14 = (f32[128,128]{1,0:T(8,128)S(1)}, f32[128,128]{1,0:T(8,128)S(1)}, u32[]{:S(2)}, u32[]{:S(2)}) collective-permute-start(f32[128,128]{1,0:T(8,128)S(1)} %add.31.a_ref), channel_id=1, source_target_pairs={{0,96},{32,64},{64,32},{96,0},{1,97},{33,65},{65,33},{97,1},{2,98}... | collective-permute-start | bytes 196616 | tf_op jit(solution)/shard_map/ppermute | solution.py:466
